TPU v7x, 32 devices: a whole 2x2x4 slice. The times are simulated.
32 devices in a mesh: fsdp: 4 (over z), ctx: 2 (over x), tp: 4 (over y, core).
Axes of the slice: x: 2, y: 2, z: 4, core: 2. Of those that a mesh axis runs over, the one named last changes fastest.
Arguments:
- tokens: bfloat16 [12288, 2048], P(('fsdp', 'ctx'), 'tp'), may hold values from -6 to 6
- cotangent: bfloat16 [12288, 2048], P(('fsdp', 'ctx'), 'tp'), may hold values from -6 to 6
- lengths: int32 [4, 6], replicated, may hold values from 1 to 1024, 3072 in all within a row
- order: int32 [24], replicated, may hold values from 0 to 23, each once
- w_query: bfloat16 [2048, 2048], P('fsdp', 'tp'), may hold values from -0.1875 to 0.1875
- w_key: bfloat16 [2048, 2048], P('fsdp', 'tp'), may hold values from -0.1875 to 0.1875
- w_value: bfloat16 [2048, 2048], P('fsdp', 'tp'), may hold values from -0.125 to 0.125
- w_output: bfloat16 [2048, 2048], P('fsdp', 'tp'), may hold values from -0.375 to 0.375
- w_gate: bfloat16 [2048, 8192], P('fsdp', 'tp'), may hold values from -0.125 to 0.125
- w_up: bfloat16 [2048, 8192], P('fsdp', 'tp'), may hold values from -0.125 to 0.125
- w_down: bfloat16 [2048, 8192], P('fsdp', 'tp'), may hold values from -0.0625 to 0.0625
Outputs:
- layer_out: bfloat16 [12288, 2048], P(('fsdp', 'ctx'), 'tp')
- input_grad: bfloat16 [12288, 2048], P(('fsdp', 'ctx'), 'tp')
- grad_query: float32 [2048, 2048], P('fsdp', 'tp')
- grad_key: float32 [2048, 2048], P('fsdp', 'tp')
- grad_value: float32 [2048, 2048], P('fsdp', 'tp')
- grad_output: float32 [2048, 2048], P('fsdp', 'tp')
- grad_gate: float32 [2048, 8192], P('fsdp', 'tp')
- grad_up: float32 [2048, 8192], P('fsdp', 'tp')
- grad_down: float32 [2048, 8192], P('fsdp', 'tp')
Inputs may be any that keep to these rules, and one draw needn't show every extreme that they name: Each row gives the lengths of the 6 sequences dealt to one index of fsdp; a row sums to the tokens of that index (1536 times the size of ctx), and its longest sequence has exactly 1024 tokens. `order`: A permutation of the sequence numbers.
All inputs are finite; a program needn't handle non-finite values.
Results may differ from a plain program's by a relative error of at most 0.019.
Values may be sent and summed in bfloat16 or wider, within the bound.
No kernel may reach another device: no remote copies, remote signals or barrier semaphores. Data moves between devices by JAX's collectives and lax.ppermute only.
A program may use at most 320 MiB of HBM per device.

v0:
```python
import math

import jax
import jax.numpy as jnp
from jax import lax
from jax.sharding import PartitionSpec as P

HD = 128


EPSILON = 1e-05
NEG_FILL = -1e30


def normalize(values):
    average = jnp.mean(values, axis=-1, keepdims=True)
    centred = values - average
    spread = jnp.mean(centred * centred, axis=-1, keepdims=True)
    inv_dev = lax.rsqrt(spread + EPSILON)
    return (centred * inv_dev, inv_dev)


def norm_back(grad, normed, inv_dev):
    grad_mean = jnp.mean(grad, axis=-1, keepdims=True)
    cross_mean = jnp.mean(grad * normed, axis=-1, keepdims=True)
    return inv_dev * (grad - grad_mean - normed * cross_mean)


def rope_tables(within):
    half_size = HD // 2
    steps_idx = jnp.arange(half_size, dtype=jnp.float32)
    freq = jnp.exp(steps_idx * (-2.0 * math.log(10000.0) / HD))
    angle = within.astype(jnp.float32)[:, None] * freq[None, :]
    angle = jnp.concatenate([angle, angle], axis=1)
    return (jnp.cos(angle)[:, None, :], jnp.sin(angle)[:, None, :])


def rotate(vector, cos_tab, sin_tab):
    half_size = vector.shape[-1] // 2
    turned = jnp.concatenate([-vector[..., half_size:], vector[..., :half_size]], axis=-1)
    return vector * cos_tab + turned * sin_tab


def rotate_back(grad, cos_tab, sin_tab):
    half_size = grad.shape[-1] // 2
    scaled = grad * sin_tab
    turned = jnp.concatenate([scaled[..., half_size:], -scaled[..., :half_size]], axis=-1)
    return grad * cos_tab + turned


def seq_tables(lengths, order):
    seq_len = lengths.reshape(-1)
    seq_ids = jnp.arange(seq_len.shape[0], dtype=jnp.int32)
    dealt_start = jnp.cumsum(seq_len) - seq_len
    picks = order[:, None] == seq_ids[None, :]
    order_len = jnp.sum(jnp.where(picks, seq_len[None, :], 0), axis=1)
    slot_start = jnp.cumsum(order_len) - order_len
    orig_start = jnp.sum(jnp.where(picks, slot_start[:, None], 0), axis=0)
    return (seq_ids, dealt_start, slot_start, orig_start)


def locate(index, starts):
    inside = index[:, None] >= starts[None, :]
    which = jnp.sum(inside.astype(jnp.int32), axis=1) - 1
    first = jnp.max(jnp.where(inside, starts[None, :], 0), axis=1)
    return (which, index - first)


def lookup(which, table, seq_ids):
    return jnp.sum(jnp.where(which[:, None] == seq_ids[None, :], table[None, :], 0), axis=1)


def tp_total(partial_value):
    return lax.psum(partial_value, "tp")


def dot_plain(left, right):
    return jnp.dot(left, right, preferred_element_type=jnp.float32)


def dot_last(left, right):
    return lax.dot_general(
        left, right, (((1,), (1,)), ((), ())), preferred_element_type=jnp.float32
    )


def dot_rows(left, right):
    return lax.dot_general(
        left, right, (((0,), (0,)), ((), ())), preferred_element_type=jnp.float32
    )


def body(
    tokens, cotangent, lengths, order, w_query, w_key, w_value, w_output, w_gate, w_up, w_down
):
    tok_rows = tokens.shape[0]
    ctx_count = lax.axis_size("ctx")
    ctx_place = lax.axis_index("ctx")
    fsdp_place = lax.axis_index("fsdp")
    tp_place = lax.axis_index("tp")
    group_rows = tok_rows * ctx_count
    block_place = fsdp_place * ctx_count + ctx_place
    scale = HD ** (-0.5)
    seq_ids, dealt_start, slot_start, orig_start = seq_tables(lengths, order)
    key_index = fsdp_place * group_rows + jnp.arange(group_rows, dtype=jnp.int32)
    key_seq, key_pos = locate(key_index, dealt_start)
    query_seq = lax.dynamic_slice_in_dim(key_seq, ctx_place * tok_rows, tok_rows)
    query_pos = lax.dynamic_slice_in_dim(key_pos, ctx_place * tok_rows, tok_rows)
    source = lookup(query_seq, orig_start, seq_ids) + query_pos
    spread_x, spread_g = (
        lax.all_gather(tokens, ("fsdp", "ctx"), axis=0, tiled=True),
        lax.all_gather(cotangent, ("fsdp", "ctx"), axis=0, tiled=True),
    )
    dealt_x = jnp.take(spread_x, source, axis=0)
    dealt_g = jnp.take(spread_g, source, axis=0)
    full_x, full_g = (
        lax.all_gather(dealt_x, "tp", axis=1, tiled=True),
        lax.all_gather(dealt_g, "tp", axis=1, tiled=True),
    )
    weights = (w_query, w_key, w_value, w_output, w_gate, w_up, w_down)
    wq_full, wk_full, wv_full, wo_full, wg_full, wu_full, wd_full = (
        lax.all_gather(weights[0], "fsdp", axis=0, tiled=True),
        lax.all_gather(weights[1], "fsdp", axis=0, tiled=True),
        lax.all_gather(weights[2], "fsdp", axis=0, tiled=True),
        lax.all_gather(weights[3], "fsdp", axis=0, tiled=True),
        lax.all_gather(weights[4], "fsdp", axis=0, tiled=True),
        lax.all_gather(weights[5], "fsdp", axis=0, tiled=True),
        lax.all_gather(weights[6], "fsdp", axis=0, tiled=True),
    )
    head_count = wq_full.shape[1] // HD
    own_cos, own_sin = rope_tables(query_pos)
    resid = full_x.astype(jnp.float32)
    normed1, inv_dev1 = normalize(resid)
    hidden1 = normed1.astype(jnp.bfloat16)
    query_rot = rotate(
        dot_plain(hidden1, wq_full).reshape(tok_rows, head_count, HD), own_cos, own_sin
    ).astype(jnp.bfloat16)
    key_rot = rotate(
        dot_plain(hidden1, wk_full).reshape(tok_rows, head_count, HD), own_cos, own_sin
    ).astype(jnp.bfloat16)
    value_low = dot_plain(hidden1, wv_full).astype(jnp.bfloat16).reshape(tok_rows, head_count, HD)
    keys_all, values_all = (
        lax.all_gather(key_rot, "ctx", axis=0, tiled=True),
        lax.all_gather(value_low, "ctx", axis=0, tiled=True),
    )
    block_rows = min(512, tok_rows)
    block_count = tok_rows // block_rows
    query_blocks = query_rot.reshape(block_count, block_rows, head_count, HD)
    seq_blocks = query_seq.reshape(block_count, block_rows)
    pos_blocks = query_pos.reshape(block_count, block_rows)

    def scores_of(query_blk, seq_blk, pos_blk):
        raw = (
            jnp.einsum("qhd,khd->hqk", query_blk, keys_all, preferred_element_type=jnp.float32)
            * scale
        )
        allowed = (seq_blk[:, None] == key_seq[None, :]) & (key_pos[None, :] <= pos_blk[:, None])
        return (raw, allowed)

    def attend(inputs):
        query_blk, seq_blk, pos_blk = inputs
        raw, allowed = scores_of(query_blk, seq_blk, pos_blk)
        masked = jnp.where(allowed[None], raw, NEG_FILL)
        top_score = jnp.max(masked, axis=-1, keepdims=True)
        expo = jnp.where(allowed[None], jnp.exp(masked - top_score), 0.0)
        denom = jnp.sum(expo, axis=-1, keepdims=True)
        probs = (expo / denom).astype(jnp.bfloat16)
        attended = jnp.einsum("hqk,khd->qhd", probs, values_all, preferred_element_type=jnp.float32)
        return (attended, top_score[..., 0] + jnp.log(denom[..., 0]))

    attended, log_norm = lax.map(attend, (query_blocks, seq_blocks, pos_blocks))
    mixed_low = attended.reshape(tok_rows, head_count * HD).astype(jnp.bfloat16)
    attn_part = dot_last(mixed_low, wo_full)
    resid1 = resid + tp_total(attn_part)
    normed2, inv_dev2 = normalize(resid1)
    hidden2 = normed2.astype(jnp.bfloat16)
    gate_proj = dot_plain(hidden2, wg_full)
    up_proj = dot_plain(hidden2, wu_full)
    sig_gate = jax.nn.sigmoid(gate_proj)
    silu_gate = gate_proj * sig_gate
    act_low = (silu_gate * up_proj).astype(jnp.bfloat16)
    mlp_full = dot_last(act_low, wd_full)
    mlp_part = lax.psum_scatter(
        mlp_full.astype(jnp.bfloat16), "tp", scatter_dimension=1, tiled=True
    ).astype(jnp.float32)
    col_count = mlp_part.shape[1]
    resid1_mine = lax.dynamic_slice_in_dim(resid1, tp_place * col_count, col_count, 1)
    y_mine = (resid1_mine + mlp_part).astype(jnp.bfloat16)
    grad_f = full_g.astype(jnp.float32)
    dact = dot_plain(full_g, wd_full).astype(jnp.bfloat16).astype(jnp.float32)
    dgate_low = (dact * up_proj * sig_gate * (1.0 + gate_proj * (1.0 - sig_gate))).astype(
        jnp.bfloat16
    )
    dup_low = (dact * silu_gate).astype(jnp.bfloat16)
    dh2_part = dot_last(dgate_low, wg_full) + dot_last(dup_low, wu_full)
    dx1 = grad_f + norm_back(tp_total(dh2_part), normed2, inv_dev2)
    da_low = dx1.astype(jnp.bfloat16)
    dout_low = dot_plain(da_low, wo_full).astype(jnp.bfloat16)
    dout_blocks = dout_low.reshape(block_count, block_rows, head_count, HD)

    def attend_back(carry, inputs):
        dk_acc, dv_acc = carry
        query_blk, seq_blk, pos_blk, lse_blk, dout_blk = inputs
        raw, allowed = scores_of(query_blk, seq_blk, pos_blk)
        probs = jnp.where(allowed[None], jnp.exp(raw - lse_blk[..., None]), 0.0)
        dprob = jnp.einsum("qhd,khd->hqk", dout_blk, values_all, preferred_element_type=jnp.float32)
        delta = jnp.sum(probs * dprob, axis=-1, keepdims=True)
        dscore = (probs * (dprob - delta)).astype(jnp.bfloat16)
        dquery = (
            jnp.einsum("hqk,khd->qhd", dscore, keys_all, preferred_element_type=jnp.float32) * scale
        )
        dk_acc = (
            dk_acc
            + jnp.einsum("hqk,qhd->khd", dscore, query_blk, preferred_element_type=jnp.float32)
            * scale
        )
        dv_acc = dv_acc + jnp.einsum(
            "hqk,qhd->khd", probs.astype(jnp.bfloat16), dout_blk, preferred_element_type=jnp.float32
        )
        return ((dk_acc, dv_acc), dquery)

    zero_keys = jnp.zeros((group_rows, head_count, HD), jnp.float32)
    (dk_all, dv_all), dq_blocks = lax.scan(
        attend_back,
        (zero_keys, zero_keys),
        (query_blocks, seq_blocks, pos_blocks, log_norm, dout_blocks),
    )
    dk_sum, dv_sum = (
        lax.psum_scatter(
            dk_all.astype(jnp.bfloat16), "ctx", scatter_dimension=0, tiled=True
        ).astype(jnp.float32),
        lax.psum_scatter(
            dv_all.astype(jnp.bfloat16), "ctx", scatter_dimension=0, tiled=True
        ).astype(jnp.float32),
    )
    width_heads = head_count * HD
    dq_low = (
        rotate_back(dq_blocks.reshape(tok_rows, head_count, HD), own_cos, own_sin)
        .astype(jnp.bfloat16)
        .reshape(tok_rows, width_heads)
    )
    dk_low = (
        rotate_back(dk_sum, own_cos, own_sin).astype(jnp.bfloat16).reshape(tok_rows, width_heads)
    )
    dv_low = dv_sum.astype(jnp.bfloat16).reshape(tok_rows, width_heads)
    dh1_part = dot_last(dq_low, wq_full) + dot_last(dk_low, wk_full) + dot_last(dv_low, wv_full)
    dx_full = dx1 + norm_back(tp_total(dh1_part), normed1, inv_dev1)
    dx_mine = lax.dynamic_slice_in_dim(dx_full, tp_place * col_count, col_count, 1).astype(
        jnp.bfloat16
    )
    orig_index = block_place * tok_rows + jnp.arange(tok_rows, dtype=jnp.int32)
    slot_which, slot_within = locate(orig_index, slot_start)
    seq_which = lookup(slot_which, order, seq_ids)
    dealt_index = lookup(seq_which, dealt_start, seq_ids) + slot_within
    back_y, back_dx = (
        lax.all_gather(y_mine, ("fsdp", "ctx"), axis=0, tiled=True),
        lax.all_gather(dx_mine, ("fsdp", "ctx"), axis=0, tiled=True),
    )
    layer_out = jnp.take(back_y, dealt_index, axis=0)
    input_grad = jnp.take(back_dx, dealt_index, axis=0)
    grads = (
        dot_rows(hidden1, dq_low),
        dot_rows(hidden1, dk_low),
        dot_rows(hidden1, dv_low),
        dot_rows(da_low, mixed_low),
        dot_rows(hidden2, dgate_low),
        dot_rows(hidden2, dup_low),
        dot_rows(full_g, act_low),
    )
    shares = (
        lax.psum_scatter(
            grads[0].astype(jnp.bfloat16), "fsdp", scatter_dimension=0, tiled=True
        ).astype(jnp.float32),
        lax.psum_scatter(
            grads[1].astype(jnp.bfloat16), "fsdp", scatter_dimension=0, tiled=True
        ).astype(jnp.float32),
        lax.psum_scatter(
            grads[2].astype(jnp.bfloat16), "fsdp", scatter_dimension=0, tiled=True
        ).astype(jnp.float32),
        lax.psum_scatter(
            grads[3].astype(jnp.bfloat16), "fsdp", scatter_dimension=0, tiled=True
        ).astype(jnp.float32),
        lax.psum_scatter(
            grads[4].astype(jnp.bfloat16), "fsdp", scatter_dimension=0, tiled=True
        ).astype(jnp.float32),
        lax.psum_scatter(
            grads[5].astype(jnp.bfloat16), "fsdp", scatter_dimension=0, tiled=True
        ).astype(jnp.float32),
        lax.psum_scatter(
            grads[6].astype(jnp.bfloat16), "fsdp", scatter_dimension=0, tiled=True
        ).astype(jnp.float32),
    )
    shares = (
        lax.psum(shares[0].astype(jnp.bfloat16), "ctx").astype(jnp.float32),
        lax.psum(shares[1].astype(jnp.bfloat16), "ctx").astype(jnp.float32),
        lax.psum(shares[2].astype(jnp.bfloat16), "ctx").astype(jnp.float32),
        lax.psum(shares[3].astype(jnp.bfloat16), "ctx").astype(jnp.float32),
        lax.psum(shares[4].astype(jnp.bfloat16), "ctx").astype(jnp.float32),
        lax.psum(shares[5].astype(jnp.bfloat16), "ctx").astype(jnp.float32),
        lax.psum(shares[6].astype(jnp.bfloat16), "ctx").astype(jnp.float32),
    )
    return (
        layer_out,
        input_grad,
        shares[0],
        shares[1],
        shares[2],
        shares[3],
        shares[4],
        shares[5],
        shares[6],
    )


def solution(mesh):
    placed = (
        P(("fsdp", "ctx"), "tp"),
        P(("fsdp", "ctx"), "tp"),
        P(),
        P(),
        P("fsdp", "tp"),
        P("fsdp", "tp"),
        P("fsdp", "tp"),
        P("fsdp", "tp"),
        P("fsdp", "tp"),
        P("fsdp", "tp"),
        P("fsdp", "tp"),
    )
    return jax.shard_map(
        body,
        mesh=mesh,
        in_specs=placed,
        out_specs=(
            P(("fsdp", "ctx"), "tp"),
            P(("fsdp", "ctx"), "tp"),
            P("fsdp", "tp"),
            P("fsdp", "tp"),
            P("fsdp", "tp"),
            P("fsdp", "tp"),
            P("fsdp", "tp"),
            P("fsdp", "tp"),
            P("fsdp", "tp"),
        ),
        check_vma=False,
    )
```

profile of v0, /device:TPU:0, one launch (start us, length us, event | category | flops | bytes accessed | tf_op | source)
XLA Modules:
  0.0 3588.8 jit_solution(7519338392230270365)
XLA Ops:
  12.8 176.6 %all-gather.40.cloned.1.call-done = bf16[12288,512]{1,0:T(8,128)(2,1)} async-done(((bf16[1536,512]{1,0:T(8,128)(2,1)}), bf16[12288,512]{1,0:T(8,128)(2,1)}) %all-gather.40.cloned.1.call-update) | async-done | bytes 12582928 | tf_op jit(solution)/shard_map/all_gather | solution.py:112
  200.4 165.8 %all-gather.16.cloned.1.call-done = bf16[12288,512]{1,0:T(8,128)(2,1)} async-done(((bf16[1536,512]{1,0:T(8,128)(2,1)}), bf16[12288,512]{1,0:T(8,128)(2,1)}) %all-gather.16.cloned.1.call-update) | async-done | bytes 12582928 | tf_op jit(solution)/shard_map/all_gather | solution.py:111
  381.5 42.6 %all-gather.18.cloned.1.call-done = bf16[1536,2048]{1,0:T(8,128)(2,1)} async-done(((bf16[1536,512]{1,0:T(8,128)(2,1)}), bf16[1536,2048]{1,0:T(8,128)(2,1)}) %all-gather.18.cloned.1.call-update) | async-done | bytes 6291472 | tf_op jit(solution)/shard_map/all_gather | solution.py:117
  435.0 36.5 %all-gather.26.cloned.1.call-done = bf16[2048,512]{1,0:T(8,128)(2,1)} async-done(((bf16[512,512]{1,0:T(8,128)(2,1)}), bf16[2048,512]{1,0:T(8,128)(2,1)}) %all-gather.26.cloned.1.call-update) | async-done | bytes 2097168 | tf_op jit(solution)/shard_map/all_gather | solution.py:124
  484.8 32.8 all-gather.22.cloned.1.call-done
  539.1 24.6 all-gather.20.cloned.1.call-done
  592.6 16.4 all-gather.28.cloned.1.call-done
  609.0 46.5 %all-gather.24.cloned.1.call-done = bf16[3072,4,128]{2,0,1:T(8,128)(2,1)} async-done(((bf16[1536,4,128]{2,0,1:T(8,128)(2,1)}), bf16[3072,4,128]{2,0,1:T(8,128)(2,1)}) %all-gather.24.cloned.1.call-update) | async-done | bytes 3145744 | tf_op jit(solution)/shard_map/all_gather | solution.py:143
  655.5 129.0 %while.29 = (s32[]{:T(128)}, bf16[3,512,4,128]{3,1,2,0:T(8,128)(2,1)}, f32[3,4,512]{2,1,0:T(4,128)}, s32[3,512]{1,0:T(4,128)S(1)}, s32[3072]{0:T(1024)S(1)}, /*i...) while((s32[]{:T(128)}, ...), condition=%wide.region_12.14_spmd.clone, body=%wide.region_9.13_spmd.sunk.clone | while | flops 3314022400 | bytes 114921672 | solution.py:171
  683.3 13.7 fusion.166
  699.7 13.9 fusion.164
  727.2 13.7 fusion.166
  797.6 55.2 %all-gather.36.cloned.1.call-done = bf16[2048,2048]{1,0:T(8,128)(2,1)} async-done(((bf16[512,2048]{1,0:T(8,128)(2,1)}), bf16[2048,2048]{1,0:T(8,128)(2,1)}) %all-gather.36.cloned.1.call-update) | async-done | bytes 8388624 | tf_op jit(solution)/shard_map/all_gather | solution.py:128
  852.8 46.8 %all-gather.42.cloned.1.call-done = bf16[1536,2048]{1,0:T(8,128)(2,1)} async-done(((bf16[1536,512]{1,0:T(8,128)(2,1)}), bf16[1536,2048]{1,0:T(8,128)(2,1)}) %all-gather.42.cloned.1.call-update) | async-done | bytes 6291472 | tf_op jit(solution)/shard_map/all_gather | solution.py:118
  899.6 18.8 convolution_convert_fusion.3
  918.5 204.2 %all-reduce.6.cloned.1.call-done = f32[1536,2048]{1,0:T(8,128)} async-done(((f32[1536,2048]{1,0:T(8,128)}), f32[1536,2048]{1,0:T(8,128)}) %all-reduce.6.cloned.1.call-update) | async-done | bytes 12582928 | tf_op jit(solution)/shard_map/psum | solution.py:74
  1139.3 134.8 %all-gather.32.cloned.1.call-done = bf16[2048,2048]{1,0:T(8,128)(2,1)} async-done(((bf16[512,2048]{1,0:T(8,128)(2,1)}), bf16[2048,2048]{1,0:T(8,128)(2,1)}) %all-gather.32.cloned.1.call-update) | async-done | bytes 8388624 | tf_op jit(solution)/shard_map/all_gather | solution.py:126
  1274.1 18.9 fusion.83
  1293.0 130.4 %all-gather.34.cloned.1.call-done = bf16[2048,2048]{1,0:T(8,128)(2,1)} async-done(((bf16[512,2048]{1,0:T(8,128)(2,1)}), bf16[2048,2048]{1,0:T(8,128)(2,1)}) %all-gather.34.cloned.1.call-update) | async-done | bytes 8388624 | tf_op jit(solution)/shard_map/all_gather | solution.py:127
  1423.4 31.1 fusion.35
  1454.5 19.1 fusion.84
  1473.6 22.1 convolution_add_fusion
  1495.9 218.9 %all-reduce.8.cloned.1.call-done = f32[1536,2048]{1,0:T(8,128)} async-done(((f32[1536,2048]{1,0:T(8,128)}), f32[1536,2048]{1,0:T(8,128)}) %all-reduce.8.cloned.1.call-update) | async-done | bytes 12582928 | tf_op jit(solution)/shard_map/psum | solution.py:74
  1752.8 248.9 %while.30 = (s32[]{:T(128)}, f32[3072,4,128]{0,2,1:T(8,128)}, f32[3072,4,128]{0,2,1:T(8,128)}, f32[3,512,4,128]{3,1,2,0:T(8,128)}, bf16[3,512,4,128]{3,1,2,0:T(8...) while((s32[]{:T(128)}, f32[3072,4,128]{0,2,1:T(8,128)}, ...), condition=%wide.region_26.28_spmd.clone.clone, body=%wide.region_24.27_spmd.clone.sunk.clone | while | flops 8160278528 | bytes 277967072 | solution.py:223
  1782.6 22.1 multiply_reduce_fusion.6
  1804.7 17.1 multiply_convert_fusion.4
  1850.5 15.7 bitcast_add_fusion.7
  1866.2 22.1 multiply_reduce_fusion.6
  1888.4 17.1 multiply_convert_fusion.4
  1934.2 15.7 bitcast_add_fusion.7
  1949.9 22.1 multiply_reduce_fusion.6
  1972.0 17.1 multiply_convert_fusion.4
  2022.7 19.6 convolution_convert_fusion
  2042.4 19.4 convolution_convert_fusion.2
  2061.9 19.6 convolution_convert_fusion.1
  2126.9 19.0 convolution_convert_fusion.4
  2161.0 14.4 add_add_fusion
  2175.5 113.4 %reduce-scatter.29.cloned.1.call-done = bf16[512,2048]{1,0:T(8,128)(2,1)} async-done(((bf16[2048,2048]{1,0:T(8,128)(2,1)}), bf16[512,2048]{1,0:T(8,128)(2,1)}) %reduce-scatter.29.cloned.1.call-update) | async-done | bytes 2097168 | tf_op jit(solution)/shard_map/reduce_scatter | solution.py:289
  2288.9 147.5 %reduce-scatter.25.cloned.1.call-done = bf16[512,2048]{1,0:T(8,128)(2,1)} async-done(((bf16[2048,2048]{1,0:T(8,128)(2,1)}), bf16[512,2048]{1,0:T(8,128)(2,1)}) %reduce-scatter.25.cloned.1.call-update) | async-done | bytes 2097168 | tf_op jit(solution)/shard_map/reduce_scatter | solution.py:283
  2436.5 147.7 %reduce-scatter.27.cloned.1.call-done = bf16[512,2048]{1,0:T(8,128)(2,1)} async-done(((bf16[2048,2048]{1,0:T(8,128)(2,1)}), bf16[512,2048]{1,0:T(8,128)(2,1)}) %reduce-scatter.27.cloned.1.call-update) | async-done | bytes 2097168 | tf_op jit(solution)/shard_map/reduce_scatter | solution.py:286
  2584.2 47.0 %reduce-scatter.21.cloned.1.call-done = bf16[512,512]{1,0:T(8,128)(2,1)} async-done(((bf16[2048,512]{1,0:T(8,128)(2,1)}), bf16[512,512]{1,0:T(8,128)(2,1)}) %reduce-scatter.21.cloned.1.call-update) | async-done | bytes 524304 | tf_op jit(solution)/shard_map/reduce_scatter | solution.py:277
  2631.2 46.1 %reduce-scatter.19.cloned.1.call-done = bf16[512,512]{1,0:T(8,128)(2,1)} async-done(((bf16[2048,512]{1,0:T(8,128)(2,1)}), bf16[512,512]{1,0:T(8,128)(2,1)}) %reduce-scatter.19.cloned.1.call-update) | async-done | bytes 524304 | tf_op jit(solution)/shard_map/reduce_scatter | solution.py:274
  2677.3 46.0 %reduce-scatter.17.cloned.1.call-done = bf16[512,512]{1,0:T(8,128)(2,1)} async-done(((bf16[2048,512]{1,0:T(8,128)(2,1)}), bf16[512,512]{1,0:T(8,128)(2,1)}) %reduce-scatter.17.cloned.1.call-update) | async-done | bytes 524304 | tf_op jit(solution)/shard_map/reduce_scatter | solution.py:271
  2723.4 60.2 %reduce-scatter.11.cloned.1.call-done = bf16[1536,512]{1,0:T(8,128)(2,1)} async-done(((bf16[1536,2048]{1,0:T(8,128)(2,1)}), bf16[1536,512]{1,0:T(8,128)(2,1)}) %reduce-scatter.11.cloned.1.call-update) | async-done | bytes 1572880 | tf_op jit(solution)/shard_map/reduce_scatter | solution.py:183
  2788.0 218.8 %all-reduce.10.cloned.1.call-done = f32[1536,2048]{1,0:T(8,128)} async-done(((f32[1536,2048]{1,0:T(8,128)}), f32[1536,2048]{1,0:T(8,128)}) %all-reduce.10.cloned.1.call-update) | async-done | bytes 12582928 | tf_op jit(solution)/shard_map/psum | solution.py:74
  3020.6 190.8 %all-reduce.12.cloned.1.call-done = (bf16[512,512]{1,0:T(8,128)(2,1)}, bf16[512,512]{1,0:T(8,128)(2,1)}, bf16[512,512]{1,0:T(8,128)(2,1)}, bf16[512,512]{1,0:T(8...) async-done(((bf16[512,512]{1,0:T(8,128)(2,1)}, bf16[512,512]{1,0:T(8,128)(2,1)}, bf16[512,512]{1,0:T(8,128)(2,1)}, ...) | async-done | bytes 8388624 | tf_op jit(solution)/shard_map/psum | solution.py:294
  3227.9 163.3 %all-gather.38.cloned.1.call-done = bf16[12288,512]{1,0:T(8,128)(2,1)} async-done(((bf16[1536,512]{1,0:T(8,128)(2,1)}), bf16[12288,512]{1,0:T(8,128)(2,1)}) %all-gather.38.cloned.1.call-update) | async-done | bytes 12582928 | tf_op jit(solution)/shard_map/all_gather | solution.py:256
  3402.2 166.6 %all-gather.44.cloned.1.call-done = bf16[12288,512]{1,0:T(8,128)(2,1)} async-done(((bf16[1536,512]{1,0:T(8,128)(2,1)}), bf16[12288,512]{1,0:T(8,128)(2,1)}) %all-gather.44.cloned.1.call-update) | async-done | bytes 12582928 | tf_op jit(solution)/shard_map/all_gather | solution.py:257
  (323 shorter events, 500.3 us)
Async XLA Ops:
  7.2 182.2 %all-gather.40.cloned.1.call-start = ((), (), s32[]{:S(2)}) async-start(), calls=%async_computation.24 | async-start | bytes 14155776 | tf_op jit(solution)/shard_map/all_gather | solution.py:112
  7.9 358.3 %all-gather.16.cloned.1.call-start = ((), (), s32[]{:S(2)}) async-start(), calls=%async_computation.10 | async-start | bytes 14155776 | tf_op jit(solution)/shard_map/all_gather | solution.py:111
  8.7 415.5 %all-gather.18.cloned.1.call-start = ((), (), s32[]{:S(2)}) async-start(), calls=%async_computation.11 | async-start | bytes 7864320 | tf_op jit(solution)/shard_map/all_gather | solution.py:117
  379.4 92.1 %all-gather.26.cloned.1.call-start = ((), (), s32[]{:S(2)}) async-start(), calls=%async_computation.15 | async-start | bytes 2621440 | tf_op jit(solution)/shard_map/all_gather | solution.py:124
  380.0 137.6 %all-gather.22.cloned.1.call-start = ((), (), s32[]{:S(2)}) async-start(), calls=%async_computation.13 | async-start | bytes 2621440 | tf_op jit(solution)/shard_map/all_gather | solution.py:123
  380.6 183.2 %all-gather.20.cloned.1.call-start = ((), (), s32[]{:S(2)}) async-start(), calls=%async_computation.12 | async-start | bytes 2621440 | tf_op jit(solution)/shard_map/all_gather | solution.py:122
  381.1 227.8 %all-gather.28.cloned.1.call-start = ((), (), s32[]{:S(2)}) async-start(), calls=%async_computation.16 | async-start | bytes 4718592 | tf_op jit(solution)/shard_map/all_gather | solution.py:144
  480.1 175.4 %all-gather.24.cloned.1.call-start = ((), (), s32[]{:S(2)}) async-start(), calls=%async_computation.14 | async-start | bytes 4718592 | tf_op jit(solution)/shard_map/all_gather | solution.py:143
  532.1 255.6 %all-gather.30.cloned.1.call-start = ((), (), s32[]{:S(2)}) async-start(), calls=%async_computation.17 | async-start | bytes 2621440 | tf_op jit(solution)/shard_map/all_gather | solution.py:125
  532.8 320.0 %all-gather.36.cloned.1.call-start = ((), (), s32[]{:S(2)}) async-start(), calls=%async_computation.21 | async-start | bytes 10485760 | tf_op jit(solution)/shard_map/all_gather | solution.py:128
  533.4 366.2 %all-gather.42.cloned.1.call-start = ((), (), s32[]{:S(2)}) async-start(), calls=%async_computation.25 | async-start | bytes 7864320 | tf_op jit(solution)/shard_map/all_gather | solution.py:118
  539.1 583.6 %all-reduce.6.cloned.1.call-start = ((), (), s32[]{:S(2)}) async-start(), calls=%async_computation.18 | async-start | bytes 25165824 | tf_op jit(solution)/shard_map/psum | solution.py:74
  670.2 13.1 copy-start.4
  670.2 13.1 copy-start.13
  713.6 13.6 copy-start.4
  713.6 13.6 copy-start.13
  756.5 13.1 copy-start.4
  756.5 13.1 copy-start.13
  796.3 477.8 %all-gather.32.cloned.1.call-start = ((), (), s32[]{:S(2)}) async-start(), calls=%async_computation.19 | async-start | bytes 10485760 | tf_op jit(solution)/shard_map/all_gather | solution.py:126
  797.0 626.4 %all-gather.34.cloned.1.call-start = ((), (), s32[]{:S(2)}) async-start(), calls=%async_computation.20 | async-start | bytes 10485760 | tf_op jit(solution)/shard_map/all_gather | solution.py:127
  797.6 917.2 %all-reduce.8.cloned.1.call-start = ((), (), s32[]{:S(2)}) async-start(), calls=%async_computation.26 | async-start | bytes 25165824 | tf_op jit(solution)/shard_map/psum | solution.py:74
  1495.8 585.8 %reduce-scatter.15.cloned.1.call-start = ((), (), s32[]{:S(2)}) async-start(), calls=%async_computation.28 | async-start | bytes 4718592 | tf_op jit(solution)/shard_map/reduce_scatter | solution.py:232
  1714.8 11.8 copy-start.6
  1726.6 13.4 copy-start.40
  1740.0 12.8 copy-start.1
  1740.0 12.8 copy-start.21
  1740.0 12.8 copy-start.23
  1782.6 43.7 %slice-start = ((s8[6291456]{0:T(1024)(128)(4,1)}), s8[2097152]{0:T(1024)(128)(4,1)S(1)}, s32[]{:S(2)}) async-start(s8[6291456]{0:T(1024)(128)(4,1)} %bitcast.184), calls=%async_computation.39 | async-start | bytes 4194304 | tf_op jit(solution)/shard_map/while
  1804.7 21.6 slice-start.1
  1866.2 43.7 %slice-start = ((s8[6291456]{0:T(1024)(128)(4,1)}), s8[2097152]{0:T(1024)(128)(4,1)S(1)}, s32[]{:S(2)}) async-start(s8[6291456]{0:T(1024)(128)(4,1)} %bitcast.184), calls=%async_computation.39 | async-start | bytes 4194304 | tf_op jit(solution)/shard_map/while
  1888.4 21.6 slice-start.1
  1949.9 43.7 %slice-start = ((s8[6291456]{0:T(1024)(128)(4,1)}), s8[2097152]{0:T(1024)(128)(4,1)S(1)}, s32[]{:S(2)}) async-start(s8[6291456]{0:T(1024)(128)(4,1)} %bitcast.184), calls=%async_computation.39 | async-start | bytes 4194304 | tf_op jit(solution)/shard_map/while
  1972.0 21.6 slice-start.1
  2006.7 89.8 %reduce-scatter.13.cloned.1.call-start = ((), (), s32[]{:S(2)}) async-start(), calls=%async_computation.27 | async-start | bytes 4718592 | tf_op jit(solution)/shard_map/reduce_scatter | solution.py:229
  2012.2 163.2 %reduce-scatter.23.cloned.1.call-start = ((), (), s32[]{:S(2)}) async-start(), calls=%async_computation.34 | async-start | bytes 2621440 | tf_op jit(solution)/shard_map/reduce_scatter | solution.py:280
  2022.7 266.2 %reduce-scatter.29.cloned.1.call-start = ((), (), s32[]{:S(2)}) async-start(), calls=%async_computation.37 | async-start | bytes 10485760 | tf_op jit(solution)/shard_map/reduce_scatter | solution.py:289
  2042.3 394.1 %reduce-scatter.25.cloned.1.call-start = ((), (), s32[]{:S(2)}) async-start(), calls=%async_computation.35 | async-start | bytes 10485760 | tf_op jit(solution)/shard_map/reduce_scatter | solution.py:283
  2061.8 522.4 %reduce-scatter.27.cloned.1.call-start = ((), (), s32[]{:S(2)}) async-start(), calls=%async_computation.36 | async-start | bytes 10485760 | tf_op jit(solution)/shard_map/reduce_scatter | solution.py:286
  2081.5 549.7 %reduce-scatter.21.cloned.1.call-start = ((), (), s32[]{:S(2)}) async-start(), calls=%async_computation.33 | async-start | bytes 2621440 | tf_op jit(solution)/shard_map/reduce_scatter | solution.py:277
  2089.9 587.4 %reduce-scatter.19.cloned.1.call-start = ((), (), s32[]{:S(2)}) async-start(), calls=%async_computation.32 | async-start | bytes 2621440 | tf_op jit(solution)/shard_map/reduce_scatter | solution.py:274
  2113.9 609.4 %reduce-scatter.17.cloned.1.call-start = ((), (), s32[]{:S(2)}) async-start(), calls=%async_computation.31 | async-start | bytes 2621440 | tf_op jit(solution)/shard_map/reduce_scatter | solution.py:271
  2126.9 656.7 %reduce-scatter.11.cloned.1.call-start = ((), (), s32[]{:S(2)}) async-start(), calls=%async_computation.22 | async-start | bytes 7864320 | tf_op jit(solution)/shard_map/reduce_scatter | solution.py:183
  2146.0 860.8 %all-reduce.10.cloned.1.call-start = ((), (), s32[]{:S(2)}) async-start(), calls=%async_computation.29 | async-start | bytes 25165824 | tf_op jit(solution)/shard_map/psum | solution.py:74
  2175.4 1036.0 %all-reduce.12.cloned.1.call-start = ((), (), s32[]{:S(2)}) async-start(), calls=%async_computation.38 | async-start | bytes 16777216 | tf_op jit(solution)/shard_map/psum | solution.py:294
  2723.3 283.5 %copy-start.29 = (f32[1536]{0:T(1024)S(1)}, f32[1536]{0:T(1024)}, u32[]{:S(2)}) copy-start(f32[1536]{0:T(1024)} %copy-done.28) | copy-start | bytes 18436
  2723.3 283.5 %copy-start.31 = (f32[1536]{0:T(1024)S(1)}, f32[1536]{0:T(1024)}, u32[]{:S(2)}) copy-start(f32[1536]{0:T(1024)} %copy-done.30) | copy-start | bytes 18436
  2723.3 667.8 %all-gather.38.cloned.1.call-start = ((), (), s32[]{:S(2)}) async-start(), calls=%async_computation.23 | async-start | bytes 14155776 | tf_op jit(solution)/shard_map/all_gather | solution.py:256
  2787.7 781.2 %all-gather.44.cloned.1.call-start = ((), (), s32[]{:S(2)}) async-start(), calls=%async_computation.30 | async-start | bytes 14155776 | tf_op jit(solution)/shard_map/all_gather | solution.py:257
  (38 other events, 198.5 us)
Sparse Core Ops, SparseCore 0:
  10.2 179.1 all-gather.39
  191.5 174.6 all-gather.15
  379.5 44.5 all-gather.17
  425.6 45.9 all-gather.25
  472.9 44.6 all-gather.21
  519.1 44.6 all-gather.19
  565.3 43.6 all-gather.27
  610.5 44.9 all-gather.23
  657.0 45.9 all-gather.29
  704.4 148.3 all-gather.35
  855.0 44.5 all-gather.41
  901.9 220.6 all-reduce.5
  1124.2 149.8 all-gather.31
  1275.5 147.8 all-gather.33
  1495.9 218.8 all-reduce.7
  2006.8 43.5 reduce-scatter.14
  2053.1 43.3 reduce-scatter.12
  2098.7 43.8 reduce-scatter.22
  2145.1 143.8 reduce-scatter.28
  2291.2 145.1 reduce-scatter.24
  2438.9 145.1 reduce-scatter.26
  2586.6 44.5 reduce-scatter.20
  2634.0 43.1 reduce-scatter.18
  2680.1 43.1 reduce-scatter.16
  2725.8 57.6 reduce-scatter.10
  2786.1 220.6 all-reduce.9
  3010.0 201.3 all-reduce.11
  3214.4 176.7 all-gather.37
  3394.2 174.6 all-gather.43
where the time goes:
time: 3600 us; the launch traced here: 3590 us
  waiting for transfers between devices  2690 us (75%)
  matrix products  542 us (15%)
  other arithmetic  221 us (6%)
  local copies, waits for them, and re-layouts  117 us (3%)
    psum x3, waiting for transfers between devices, tp_total(): return lax.psum(partial_value, 'tp')  642 us
    psum x1, waiting for transfers between devices, body(): lax.psum(shares[0].astype(jnp.bfloat16), 'ctx').astype(jnp.float32)  191 us
    all_gather x1, waiting for transfers between devices, body(): lax.all_gather(cotangent, ('fsdp', 'ctx'), axis=0, tiled=True)  177 us
    all_gather x1, waiting for transfers between devices, body(): lax.all_gather(dx_mine, ('fsdp', 'ctx'), axis=0, tiled=True)  167 us
    all_gather x1, waiting for transfers between devices, body(): lax.all_gather(tokens, ('fsdp', 'ctx'), axis=0, tiled=True)  166 us
    all_gather x1, waiting for transfers between devices, body(): lax.all_gather(y_mine, ('fsdp', 'ctx'), axis=0, tiled=True)  163 us
    reduce_scatter x1, waiting for transfers between devices, body(): lax.psum_scatter(grads[5].astype(jnp.bfloat16), 'fsdp', scatter_dimension...  148 us
    reduce_scatter x1, waiting for transfers between devices, body(): lax.psum_scatter(grads[4].astype(jnp.bfloat16), 'fsdp', scatter_dimension...  148 us
  transfers between devices with their start and end apart: 29, of which 26 were waited for; matrix products, arithmetic and copies ran while one was open for 13% of the time, Pallas kernels for 0%

commit v1 on v0

v1 whole, which is shorter than its diff:
```python
import functools
import math

import jax
import jax.numpy as jnp
from jax import lax
from jax.experimental import pallas as pl
from jax.experimental.pallas import tpu as pltpu
from jax.sharding import PartitionSpec as P

HD = 128
HALO = 1024
EPSILON = 1e-05
NEG_FILL = -1e30
PLANE = ("ctx", "tp")
BF = jnp.bfloat16
F32 = jnp.float32


def dot_plain(left, right):
    return jnp.dot(left, right, preferred_element_type=F32)


def dot_last(left, right):
    return lax.dot_general(left, right, (((1,), (1,)), ((), ())), preferred_element_type=F32)


def dot_rows(left, right):
    return lax.dot_general(left, right, (((0,), (0,)), ((), ())), preferred_element_type=F32)


def normalize(values):
    average = jnp.mean(values, axis=-1, keepdims=True)
    centred = values - average
    spread = jnp.mean(centred * centred, axis=-1, keepdims=True)
    inv_dev = lax.rsqrt(spread + EPSILON)
    return (centred * inv_dev, inv_dev)


def norm_back(grad, normed, inv_dev):
    grad_mean = jnp.mean(grad, axis=-1, keepdims=True)
    cross_mean = jnp.mean(grad * normed, axis=-1, keepdims=True)
    return inv_dev * (grad - grad_mean - normed * cross_mean)


def slots(lengths, order):
    seq_len = lengths.reshape(-1)
    seq_ids = jnp.arange(seq_len.shape[0], dtype=jnp.int32)
    picks = order[:, None] == seq_ids[None, :]
    order_len = jnp.sum(jnp.where(picks, seq_len[None, :], 0), axis=1)
    return jnp.cumsum(order_len) - order_len


def first_of(index, starts):
    inside = index[:, None] >= starts[None, :]
    return jnp.max(jnp.where(inside, starts[None, :], 0), axis=1)


def qkv_kernel(heads, x_ref, own_ref, oth_ref, cos_ref, sin_ref, h_ref, q_ref, k_ref, v_ref, e_ref):
    values = x_ref[...].astype(F32)
    normed, _ = normalize(values)
    hidden = normed.astype(BF)
    h_ref[...] = hidden
    cos, sin = cos_ref[...], sin_ref[...]
    width = heads * HD
    for piece, w_ref in enumerate((own_ref, oth_ref)):
        out = dot_plain(hidden, w_ref[...])
        for head in range(heads):
            to = (piece * heads + head) * HD
            swapped = ((1 - piece) * heads + head) * HD
            query = out[:, head * HD : (head + 1) * HD]
            key = out[:, width + head * HD : width + (head + 1) * HD]
            value = out[:, 2 * width + head * HD : 2 * width + (head + 1) * HD].astype(BF)
            query = (query * cos + pltpu.roll(query, HD // 2, 1) * sin).astype(BF)
            key = (key * cos + pltpu.roll(key, HD // 2, 1) * sin).astype(BF)
            q_ref[:, to : to + HD] = query
            k_ref[:, to : to + HD] = key
            v_ref[:, to : to + HD] = value
            e_ref[:, swapped : swapped + HD] = key
            e_ref[:, 2 * width + swapped : 2 * width + swapped + HD] = value


def project(x, w_own, w_oth, cos_tab, sin_tab, heads):
    rows, width = x.shape
    block = rows // 3
    skip = rows // block - HALO // block
    local = 2 * heads * HD
    row = lambda i: (i, 0)
    return pl.pallas_call(
        functools.partial(qkv_kernel, heads),
        grid=(rows // block,),
        in_specs=[
            pl.BlockSpec((block, width), row),
            pl.BlockSpec((width, 3 * heads * HD), lambda i: (0, 0)),
            pl.BlockSpec((width, 3 * heads * HD), lambda i: (0, 0)),
            pl.BlockSpec((block, HD), lambda i: (i + HALO // block, 0)),
            pl.BlockSpec((block, HD), lambda i: (i + HALO // block, 0)),
        ],
        out_specs=[
            pl.BlockSpec((block, width), row),
            pl.BlockSpec((block, local), row),
            pl.BlockSpec((block, local), row),
            pl.BlockSpec((block, local), row),
            pl.BlockSpec((block, 2 * local), lambda i: (jnp.maximum(i - skip, 0), 0)),
        ],
        out_shape=[
            jax.ShapeDtypeStruct((rows, width), BF),
            jax.ShapeDtypeStruct((rows, local), BF),
            jax.ShapeDtypeStruct((rows, local), BF),
            jax.ShapeDtypeStruct((rows, local), BF),
            jax.ShapeDtypeStruct((HALO, 2 * local), BF),
        ],
        cost_estimate=pl.CostEstimate(
            flops=2 * rows * width * 3 * local, bytes_accessed=20_000_000, transcendentals=0
        ),
        name="norm_project",
    )(x, w_own, w_oth, cos_tab, sin_tab)


def allowed_keys(first_ref, step, block):
    span = block + HALO
    keys = lax.broadcasted_iota(jnp.int32, (block, span), 1)
    rows = lax.broadcasted_iota(jnp.int32, (block, span), 0)
    first = first_ref[...] - step * block
    return (keys >= first) & (keys <= rows + HALO)


def attend_kernel(q_ref, k_ref, v_ref, ke_ref, ve_ref, first_ref, o_ref, lse_ref, keys, values):
    step = pl.program_id(1)
    block = q_ref.shape[0]

    @pl.when(step == 0)
    def _():
        keys[:HALO] = ke_ref[...]
        keys[HALO:] = k_ref[...]
        values[:HALO] = ve_ref[...]
        values[HALO:] = v_ref[...]

    window = pl.ds(pl.multiple_of(step * block, block), block + HALO)
    raw = dot_last(q_ref[...], keys[window, :]) * (HD**-0.5)
    raw = jnp.where(allowed_keys(first_ref, step, block), raw, NEG_FILL)
    top = jnp.max(raw, axis=-1, keepdims=True)
    expo = jnp.exp(raw - top)
    denom = jnp.sum(expo, axis=-1, keepdims=True)
    probs = (expo * (1.0 / denom)).astype(BF)
    o_ref[...] = dot_plain(probs, values[window, :]).astype(BF)
    lse_ref[...] = top + jnp.log(denom)


def attend(q, k, v, halo, first, block=256):
    rows, local = q.shape
    heads = local // HD
    span = block + HALO
    return pl.pallas_call(
        attend_kernel,
        grid=(heads, rows // block),
        in_specs=[
            pl.BlockSpec((block, HD), lambda h, i: (i, h)),
            pl.BlockSpec((rows, HD), lambda h, i: (0, h)),
            pl.BlockSpec((rows, HD), lambda h, i: (0, h)),
            pl.BlockSpec((HALO, HD), lambda h, i: (0, h)),
            pl.BlockSpec((HALO, HD), lambda h, i: (0, h + heads)),
            pl.BlockSpec((block, 1), lambda h, i: (i, 0)),
        ],
        out_specs=[
            pl.BlockSpec((block, HD), lambda h, i: (i, h)),
            pl.BlockSpec((None, block, 1), lambda h, i: (h, i, 0)),
        ],
        out_shape=[
            jax.ShapeDtypeStruct((rows, local), BF),
            jax.ShapeDtypeStruct((heads, rows, 1), F32),
        ],
        scratch_shapes=[pltpu.VMEM((HALO + rows, HD), BF)] * 2,
        cost_estimate=pl.CostEstimate(
            flops=8 * rows * span * HD * heads,
            bytes_accessed=10_000_000,
            transcendentals=rows * span * heads,
        ),
        name="attend",
    )(q, k, v, halo, halo, first)


def rotate_back(grad, cos, sin):
    return grad * cos - pltpu.roll(grad, HD // 2, 1) * sin


def attend_back_kernel(
    q_ref, k_ref, v_ref, ke_ref, ve_ref, first_ref, lse_ref, do_ref, cos_ref, sin_ref,
    dq_ref, dk_ref, dv_ref, dke_ref, dve_ref, keys, values, dkeys, dvalues,
):
    step = pl.program_id(1)
    block = q_ref.shape[0]
    scale = HD**-0.5

    @pl.when(step == 0)
    def _():
        keys[:HALO] = ke_ref[...]
        keys[HALO:] = k_ref[...]
        values[:HALO] = ve_ref[...]
        values[HALO:] = v_ref[...]
        dkeys[...] = jnp.zeros_like(dkeys)
        dvalues[...] = jnp.zeros_like(dvalues)

    window = pl.ds(pl.multiple_of(step * block, block), block + HALO)
    query, dout = q_ref[...], do_ref[...]
    raw = dot_last(query, keys[window, :]) * scale
    probs = jnp.where(allowed_keys(first_ref, step, block), jnp.exp(raw - lse_ref[...]), 0.0)
    dprob = dot_last(dout, values[window, :])
    delta = jnp.sum(probs * dprob, axis=-1, keepdims=True)
    dscore = (probs * (dprob - delta)).astype(BF)
    mine = pl.ds(pl.multiple_of(HALO + step * block, block), block)
    dquery = dot_plain(dscore, keys[window, :]) * scale
    dq_ref[...] = rotate_back(dquery, cos_ref[mine, :], sin_ref[mine, :]).astype(BF)
    dkeys[window, :] += dot_rows(dscore, query)
    dvalues[window, :] += dot_rows(probs.astype(BF), dout)

    @pl.when(step == pl.num_programs(1) - 1)
    def _():
        dkey = rotate_back(dkeys[...] * scale, cos_ref[...], sin_ref[...])
        dke_ref[...] = dkey[:HALO].astype(BF)
        dk_ref[...] = dkey[HALO:]
        dve_ref[...] = dvalues[:HALO].astype(BF)
        dv_ref[...] = dvalues[HALO:]


def attend_back(q, k, v, halo, first, lse, dout, cos_tab, sin_tab, block=256):
    rows, local = q.shape
    heads = local // HD
    span = block + HALO
    column = pl.BlockSpec((rows, HD), lambda h, i: (0, h))
    piece = pl.BlockSpec((block, HD), lambda h, i: (i, h))
    table = pl.BlockSpec((HALO + rows, HD), lambda h, i: (0, 0))
    edge = pl.BlockSpec((HALO, HD), lambda h, i: (0, h))
    return pl.pallas_call(
        attend_back_kernel,
        grid=(heads, rows // block),
        in_specs=[
            piece,
            column,
            column,
            edge,
            pl.BlockSpec((HALO, HD), lambda h, i: (0, h + heads)),
            pl.BlockSpec((block, 1), lambda h, i: (i, 0)),
            pl.BlockSpec((None, block, 1), lambda h, i: (h, i, 0)),
            piece,
            table,
            table,
        ],
        out_specs=[piece, column, column, edge, edge],
        out_shape=[
            jax.ShapeDtypeStruct((rows, local), BF),
            jax.ShapeDtypeStruct((rows, local), F32),
            jax.ShapeDtypeStruct((rows, local), F32),
            jax.ShapeDtypeStruct((HALO, local), BF),
            jax.ShapeDtypeStruct((HALO, local), BF),
        ],
        scratch_shapes=[pltpu.VMEM((HALO + rows, HD), BF)] * 2
        + [pltpu.VMEM((HALO + rows, HD), F32)] * 2,
        cost_estimate=pl.CostEstimate(
            flops=20 * rows * span * HD * heads,
            bytes_accessed=20_000_000,
            transcendentals=rows * span * heads,
        ),
        name="attend_back",
    )(q, k, v, halo, halo, first, lse, dout, cos_tab, sin_tab)


class Plane:
    def __init__(self):
        self.nc, self.nt = lax.axis_size("ctx"), lax.axis_size("tp")
        assert self.nc == 2 and self.nt % 2 == 0
        self.hi = self.nt // self.nc
        self.ranks = self.nc * self.hi
        tp_place = lax.axis_index("tp")
        self.c = lax.axis_index("ctx")
        self.h, self.k = tp_place // self.nc, tp_place % self.nc
        self.r = self.c * self.hi + self.h

    def perm(self, move):
        pairs = []
        for c in range(self.nc):
            for h in range(self.hi):
                for k in range(self.nc):
                    c2, h2, k2 = move(c, h, k)
                    pairs.append((c * self.nt + h * self.nc + k, c2 * self.nt + h2 * self.nc + k2))
        return pairs

    def spread_rows(self, block):
        full = jnp.zeros((block.shape[0], block.shape[1] * self.nt), block.dtype)
        for jh in range(self.hi):
            for jk in range(self.nc):
                move = lambda c, h, k: (k ^ jk, h ^ jh, c)
                got = lax.ppermute(block, PLANE, self.perm(move))
                place = (self.h ^ jh) * self.nc + (self.c ^ jk)
                full = lax.dynamic_update_slice(full, got, (0, place * block.shape[1]))
        return full

    def to_blocks(self, mine):
        chunk, width = mine.shape
        cols = width // self.nt
        full = jnp.zeros((chunk * self.ranks, cols), mine.dtype)
        for jh in range(self.hi):
            for jk in range(self.nc):
                move = lambda c, h, k: (k, h ^ jh, c ^ jk)
                place = (self.h ^ jh) * self.nc + (self.c ^ jk)
                piece = lax.dynamic_slice_in_dim(mine, place * cols, cols, 1)
                got = lax.ppermute(piece, PLANE, self.perm(move))
                rank = (self.k ^ jk) * self.hi + (self.h ^ jh)
                full = lax.dynamic_update_slice(full, got, (rank * chunk, 0))
        return full

    def swap(self, value, j):
        def move(c, h, k):
            rank = (c * self.hi + h) ^ j
            return rank // self.hi, rank % self.hi, k

        return lax.ppermute(value, PLANE, self.perm(move))

    def chunk_of(self, value, j):
        size = value.shape[0] // self.ranks
        return lax.dynamic_slice_in_dim(value, (self.r ^ j) * size, size, 0)

    def turn(self, value):
        return jnp.concatenate([self.chunk_of(value, j) for j in range(self.ranks)], axis=0)

    def gather(self, mine):
        return jnp.concatenate([mine] + [self.swap(mine, j) for j in range(1, self.ranks)], axis=0)

    def pair(self, value):
        perm = [(t, t ^ 1) for t in range(self.nt)]
        return lax.ppermute(value, "tp", perm)


def body(
    tokens, cotangent, lengths, order, w_query, w_key, w_value, w_output, w_gate, w_up, w_down
):
    plane = Plane()
    rows = tokens.shape[0]
    nf, nc, nt, ranks = lax.axis_size("fsdp"), plane.nc, plane.nt, plane.ranks
    z = lax.axis_index("fsdp")
    chunk = rows // ranks
    head_cols = w_query.shape[1] // nc
    heads = head_cols // HD

    def part(weight):
        size = weight.shape[1] // nc
        return lax.dynamic_slice_in_dim(weight, plane.c * size, size, 1)

    def collect(shard):
        own = lax.all_gather(shard, "fsdp", axis=0, tiled=True)
        return own, plane.pair(own)

    attn_own, attn_oth = collect(
        jnp.concatenate([part(w) for w in (w_query, w_key, w_value, w_output)], axis=1)
    )
    wg = collect(part(w_gate))
    wu = collect(part(w_up))
    wd = collect(part(w_down))

    full_x = plane.spread_rows(tokens)
    full_g = plane.spread_rows(cotangent)
    base = (z * nc + plane.k) * rows - HALO
    index = base + jnp.arange(HALO + rows, dtype=jnp.int32)
    starts = first_of(index, slots(lengths, order))
    within = index - starts
    first = (starts[HALO:] - base)[:, None]
    lane = jnp.arange(HD, dtype=jnp.int32)
    freq = jnp.exp((lane % (HD // 2)).astype(F32) * (-2.0 * math.log(10000.0) / HD))
    angle = within.astype(F32)[:, None] * freq[None, :]
    cos_tab = jnp.cos(angle)
    sin_tab = jnp.sin(angle) * jnp.where(lane < HD // 2, -1.0, 1.0)[None, :]

    hidden1, query, key, value, edge = project(full_x, attn_own, attn_oth, cos_tab, sin_tab, heads)
    onward = []
    for f in range(nf):
        for h in range(plane.hi):
            for k in range(nc):
                to = f * nc + k + 1
                if to < nf * nc:
                    onward.append((f * nt + h * nc + k, to // nc * nt + h * nc + to % nc))
    backward = [(b, a) for a, b in onward]
    halo = lax.ppermute(edge, ("fsdp", "tp"), onward)
    mixed, lse = attend(query, key, value, halo, first)

    wo = jnp.concatenate([attn_own[:, 3 * head_cols :], attn_oth[:, 3 * head_cols :]], axis=1)
    resid = plane.chunk_of(full_x, 0).astype(F32)
    resid1 = resid + dot_last(plane.chunk_of(mixed, 0), wo)
    for j in range(1, ranks):
        resid1 = resid1 + plane.swap(
            dot_last(plane.chunk_of(mixed, j), wo).astype(BF), j
        ).astype(F32)
    normed2, inv_dev2 = normalize(resid1)
    hidden2 = plane.gather(normed2.astype(BF))

    grad_rows = plane.turn(full_g)
    acts, dgates, dups = [], [], []
    for piece in range(2):
        dact = dot_plain(grad_rows, wd[piece]).astype(BF).astype(F32)
        gate = dot_plain(hidden2, wg[piece])
        up = dot_plain(hidden2, wu[piece])
        sig = jax.nn.sigmoid(gate)
        silu = gate * sig
        acts.append((silu * up).astype(BF))
        dgates.append((dact * up * sig * (1.0 + gate * (1.0 - sig))).astype(BF))
        dups.append((dact * silu).astype(BF))

    def scatter(parts):
        total = parts[:chunk]
        low = parts.astype(BF)
        for j in range(1, ranks):
            total = total + plane.swap(low[j * chunk : (j + 1) * chunk], j).astype(F32)
        return total

    dh2 = (
        dot_last(dgates[0], wg[0])
        + dot_last(dups[0], wu[0])
        + dot_last(dgates[1], wg[1])
        + dot_last(dups[1], wu[1])
    )
    dx1 = grad_rows[:chunk].astype(F32) + norm_back(scatter(dh2), normed2, inv_dev2)
    da = plane.gather(dx1.astype(BF))
    mlp = dot_last(acts[0], wd[0]) + dot_last(acts[1], wd[1])
    layer_out = plane.to_blocks((resid1 + scatter(mlp)).astype(BF))

    def share(left, right_own, right_oth, cut=None):
        other = plane.pair(dot_rows(left, right_oth).astype(BF))
        total = (dot_rows(left, right_own) + other.astype(F32)).astype(BF)
        return lax.psum_scatter(total, "fsdp", scatter_dimension=0, tiled=True)

    def finish(mine):
        perm = [(0, 1), (1, 0)]
        other = lax.ppermute(mine, "ctx", perm)
        here = plane.c == 0
        return jnp.concatenate(
            [jnp.where(here, mine, other), jnp.where(here, other, mine)], axis=1
        ).astype(F32)

    grad_down = finish(share(grad_rows, acts[0], acts[1]))
    grad_gate = finish(share(hidden2, dgates[0], dgates[1]))
    grad_up = finish(share(hidden2, dups[0], dups[1]))

    mixed_rows = plane.turn(mixed)
    grad_output = finish(share(da, mixed_rows[:, :head_cols], mixed_rows[:, head_cols:]))
    dout = plane.turn(dot_plain(da, wo).astype(BF))
    dquery, dkey, dvalue, dkey_edge, dvalue_edge = attend_back(
        query, key, value, halo, first, lse, dout, cos_tab, sin_tab
    )
    edges = jnp.concatenate(
        [
            dkey_edge[:, head_cols:],
            dkey_edge[:, :head_cols],
            dvalue_edge[:, head_cols:],
            dvalue_edge[:, :head_cols],
        ],
        axis=1,
    )
    edges = lax.ppermute(edges, ("fsdp", "tp"), backward)
    edges = jnp.pad(edges, ((rows - HALO, 0), (0, 0))).astype(F32)
    local = 2 * head_cols
    dkey = (dkey + edges[:, :local]).astype(BF)
    dvalue = (dvalue + edges[:, local:]).astype(BF)
    own, oth = slice(0, head_cols), slice(head_cols, local)
    d_own = jnp.concatenate([dquery[:, own], dkey[:, own], dvalue[:, own]], axis=1)
    d_oth = jnp.concatenate([dquery[:, oth], dkey[:, oth], dvalue[:, oth]], axis=1)
    qkv_own, qkv_oth = attn_own[:, : 3 * head_cols], attn_oth[:, : 3 * head_cols]
    dh1 = plane.turn(
        jnp.concatenate([d_own, d_oth], axis=1)
    )
    dh1 = dot_last(dh1[:, : 3 * head_cols], qkv_own) + dot_last(dh1[:, 3 * head_cols :], qkv_oth)
    normed1, inv_dev1 = normalize(resid)
    dx = dx1 + norm_back(scatter(dh1), normed1, inv_dev1)
    input_grad = plane.to_blocks(dx.astype(BF))

    grads_qkv = share(hidden1, d_own, d_oth)
    grad_query, grad_key, grad_value = (
        finish(grads_qkv[:, i * head_cols : (i + 1) * head_cols]) for i in range(3)
    )
    return (
        layer_out, input_grad, grad_query, grad_key, grad_value, grad_output,
        grad_gate, grad_up, grad_down,
    )


def solution(mesh):
    rows = P(("fsdp", "ctx"), "tp")
    weight = P("fsdp", "tp")
    return jax.shard_map(
        body,
        mesh=mesh,
        in_specs=(rows, rows, P(), P()) + (weight,) * 7,
        out_specs=(rows, rows) + (weight,) * 7,
        check_vma=False,
    )
```

time: 3600 us -> 1290 us (0.36)
  waiting for transfers between devices: 2690 us -> 562 us
  matrix products: 542 us -> 304 us
  starting transfers between devices: 3.03 us -> 182 us
  other arithmetic: 221 us -> 53.8 us
  Pallas kernels: 0 us -> 92.6 us
  local copies, waits for them, and re-layouts: 117 us -> 69.7 us
    all_gather x15 -> x4, waiting for transfers between devices: 1240 us -> 127 us  [collect(): own = lax.all_gather(shard, 'fsdp', axis=0, tiled=True)]
    psum x4 -> x0, waiting for transfers between devices: 833 us -> none  [the longest x3 642 us: tp_total(): return lax.psum(partial_value, 'tp')]
    reduce_scatter x10 -> x5, waiting for transfers between devices: 612 us -> 0.05 us  [share(): return lax.psum_scatter(total, 'fsdp', scatter_dimension=0, tiled=True)]
    ppermute x0 -> x52, waiting for transfers between devices: none -> 435 us  [the longest x18 237 us: swap(): return lax.ppermute(value, PLANE, self.perm(move))]
    dot_general x28 -> x7, matrix products: 355 us -> 90.2 us  [dot_plain(): return jnp.dot(left, right, preferred_element_type=F32)]
    ppermute x0 -> x52, starting transfers between devices: none -> 182 us  [the longest x9 81.3 us: pair(): return lax.ppermute(value, 'tp', perm)]
    pallas_call x0 -> x3, Pallas kernels: none -> 92.6 us  [the longest x1 42.8 us: attend_back(): pl.pallas_call(attend_back_kernel, grid=(heads, rows // block), in_specs=...]
    convert_element_type x20 -> x13, other arithmetic: 99.6 us -> 24.2 us  [the longest x7 12 us: finish(): return jnp.concatenate([jnp.where(here, mine, other), jnp.where(here, oth...]
  transfers between devices with their start and end apart: 29 -> 61, of which waited for: 26 -> 30; matrix products, arithmetic and copies ran while one was open for 13% -> 27% of each run, Pallas kernels for 0% -> 7%
where the time goes in v1:
time: 1290 us; the launch traced here: 1280 us
  waiting for transfers between devices  562 us (44%)
  matrix products  304 us (24%)
  starting transfers between devices  182 us (14%)
  Pallas kernels  92.6 us (7%)
  local copies, waits for them, and re-layouts  69.7 us (5%)
  other arithmetic  53.8 us (4%)
  between operations  15.3 us (1%)
    ppermute x18, waiting for transfers between devices, swap(): return lax.ppermute(value, PLANE, self.perm(move))  237 us
    all_gather x4, waiting for transfers between devices, collect(): own = lax.all_gather(shard, 'fsdp', axis=0, tiled=True)  127 us
    dot_general x12, matrix products, dot_last(): lax.dot_general(left, right, (((1,), (1,)), ((), ())), preferred_element_...  119 us
    dot_general x10, matrix products, dot_rows(): lax.dot_general(left, right, (((0,), (0,)), ((), ())), preferred_element_...  94.6 us
    dot_general x7, matrix products, dot_plain(): return jnp.dot(left, right, preferred_element_type=F32)  90.2 us
    ppermute x8, waiting for transfers between devices, to_blocks(): got = lax.ppermute(piece, PLANE, self.perm(move))  85 us
    ppermute x9, starting transfers between devices, pair(): return lax.ppermute(value, 'tp', perm)  81.3 us
    ppermute x8, waiting for transfers between devices, spread_rows(): got = lax.ppermute(block, PLANE, self.perm(move))  67.5 us
  transfers between devices with their start and end apart: 61, of which 30 were waited for; matrix products, arithmetic and copies ran while one was open for 27% of the time, Pallas kernels for 7%

profile of v1, /device:TPU:0, one launch (start us, length us, event | category | flops | bytes accessed | tf_op | source)
XLA Modules:
  0.0 1279.2 jit_solution(4177785746236934361)
XLA Ops:
  14.2 80.0 %all-gather.5.cloned.1.call-done.own_ref = bf16[2048,1024]{1,0:T(8,128)(2,1)} async-done(((bf16[512,1024]{1,0:T(8,128)(2,1)}), bf16[2048,1024]{1,0:T(8,128)(2,1)}) %all-gather.5.cloned.1.call-update) | async-done | bytes 4194320 | tf_op jit(solution)/shard_map/all_gather | solution.py:350
  94.3 13.3 %collective-permute-start = (bf16[1536,512]{1,0:T(8,128)(2,1)}, bf16[1536,512]{1,0:T(8,128)(2,1)}, u32[]{:S(2)}, u32[]{:S(2)}) collective-permute-start(bf16[1536,512]{1,0:T(8,128)(2,1)} %param.11), channel_id=1, source_target_pairs={{0,0},{1,4},{2,2},{3,6},{4,1},{5,5},{6,3},{7,7},{8,8},{9,12},{10,1... | collective-permute-start | bytes 4718600 | tf_op jit(solution)/shard_map/ppermute | solution.py:293
  113.8 6.3 fusion.50
  120.1 13.3 %collective-permute-start.22 = (bf16[1536,512]{1,0:T(8,128)(2,1)}, bf16[1536,512]{1,0:T(8,128)(2,1)}, u32[]{:S(2)}, u32[]{:S(2)}) collective-permute-start(bf16[1536,512]{1,0:T(8,128)(2,1)} %param.12), channel_id=1, source_target_pairs={{0,0},{1,4},{2,2},{3,6},{4,1},{5,5},{6,3},{7,7},{8,8},{9,12},{10,1... | collective-permute-start | bytes 4718600 | tf_op jit(solution)/shard_map/ppermute | solution.py:293
  148.0 28.7 %collective-permute-done.2 = bf16[1536,512]{1,0:T(8,128)(2,1)} collective-permute-done((bf16[1536,512]{1,0:T(8,128)(2,1)}, bf16[1536,512]{1,0:T(8,128)(2,1)}, u32[]{:S(2)}, u32[]{:S(2)}) %collective-permute-start.2) | collective-permute-done | bytes 1572896 | tf_op jit(solution)/shard_map/ppermute | solution.py:293
  183.5 19.3 %norm_project.1 = (bf16[1536,2048]{1,0:T(8,128)(2,1)}, bf16[1536,512]{1,0:T(8,128)(2,1)}, bf16[1536,512]{1,0:T(8,128)(2,1)}, bf16[1536,512]{1,0:T(8,128)(2,1)}, bf16[1024,1024]{1,0:T(8,128)(2,1)}) custom-call(bf16[1536,2048]{1,0:T(8,128)(2,1)} %constant_dynamic-update-slice_fusion.18.x_ref, bf16[2048,1024]{1,0:T(8,128)(2,1)} %all-gather.5.cloned.1.call-done.own_ref, ...), custom_call_target="tpu_custom_call" | custom-call | flops 9663676416 | bytes 20000000 | tf_op jit(solution)/shard_map/norm_project/pallas_call | solution.py:89
  211.9 34.0 %collective-permute-done.24 = bf16[1536,512]{1,0:T(8,128)(2,1)} collective-permute-done((bf16[1536,512]{1,0:T(8,128)(2,1)}, bf16[1536,512]{1,0:T(8,128)(2,1)}, u32[]{:S(2)}, u32[]{:S(2)}) %collective-permute-start.24) | collective-permute-done | bytes 1572896 | tf_op jit(solution)/shard_map/ppermute | solution.py:293
  254.5 20.9 %all-gather.11.cloned.1.call-done = bf16[2048,1024]{1,0:T(8,128)(2,1)} async-done(((bf16[512,1024]{1,0:T(8,128)(2,1)}), bf16[2048,1024]{1,0:T(8,128)(2,1)}) %all-gather.11.cloned.1.call-update) | async-done | bytes 4194320 | tf_op jit(solution)/shard_map/all_gather | solution.py:350
  277.7 30.5 %attend.1 = (bf16[1536,512]{1,0:T(8,128)(2,1)}, f32[4,1536,1]{2,1,0:T(8,128)}) custom-call(bf16[1536,512]{1,0:T(8,128)(2,1)} %get-tuple-element.21.q_ref, bf16[1536,512]{1,0:T(8,128)(2,1)} %get-tuple-element.22.k_ref, bf16[1536,512]{1,0:T(8,128)(2,1)} %get-tuple-element.23.v_ref, bf16[1024,1024]{1,0:T(8,128)(2,1)} %collective-permute-done.5.ke_ref.ve_ref, ...), custom_call_target="tpu_custom_call" | custom-call | flops 8053063680 | bytes 10000000 | tf_op jit(solution)/shard_map/attend/pallas_call | solution.py:154
  320.7 12.5 convolution_convert_fusion.4
  333.1 25.6 %all-gather.9.cloned.1.call-done = bf16[2048,1024]{1,0:T(8,128)(2,1)} async-done(((bf16[512,1024]{1,0:T(8,128)(2,1)}), bf16[2048,1024]{1,0:T(8,128)(2,1)}) %all-gather.9.cloned.1.call-update) | async-done | bytes 4194320 | tf_op jit(solution)/shard_map/all_gather | solution.py:350
  358.8 28.2 %collective-permute-done.8 = bf16[384,2048]{1,0:T(8,128)(2,1)} collective-permute-done((bf16[384,2048]{1,0:T(8,128)(2,1)}, bf16[384,2048]{1,0:T(8,128)(2,1)}, u32[]{:S(2)}, u32[]{:S(2)}) %collective-permute-start.8) | collective-permute-done | bytes 1572896 | tf_op jit(solution)/shard_map/ppermute | solution.py:317
  396.9 15.0 %convolution_convert_fusion.3 = bf16[1536,1024]{1,0:T(8,128)(2,1)} fusion(bf16[2048,1024]{1,0:T(8,128)(2,1)} %collective-permute-done.14, bf16[384,2048]{1,0:T(8,128)(2,1)S(1)} %copy-done.30, bf16[384,2048]{1,0:T(8,128)(2,1)S(1)} %copy-done.33, bf16[384,2048]{1,0:T(8,128)(2,1)S(1)} %copy-done.36, bf16[384,2048]{1,0:T(8,128)(2,1)S(1)} %get-tuple-element.53), kind=kOutput, calls=%fused_computation.35 | convolution fusion | flops 6469189632 | bytes 13631488 | tf_op jit(solution)/shard_map/dot_general | solution.py:21
  411.9 18.8 %collective-permute-done.10 = bf16[384,2048]{1,0:T(8,128)(2,1)S(1)} collective-permute-done((bf16[384,2048]{1,0:T(8,128)(2,1)S(1)}, bf16[384,2048]{1,0:T(8,128)(2,1)S(1)}, u32[]{:S(2)}, u32[]{:S(2)}) %collective-permute-start.10) | collective-permute-done | bytes 1572896 | tf_op jit(solution)/shard_map/ppermute | solution.py:317
  430.7 33.3 %collective-permute-done.11 = bf16[384,2048]{1,0:T(8,128)(2,1)S(1)} collective-permute-done((bf16[384,2048]{1,0:T(8,128)(2,1)S(1)}, bf16[384,2048]{1,0:T(8,128)(2,1)S(1)}, u32[]{:S(2)}, u32[]{:S(2)}) %collective-permute-start.11) | collective-permute-done | bytes 1572896 | tf_op jit(solution)/shard_map/ppermute | solution.py:317
  465.4 13.0 %fusion.69 = f32[1536,1024]{1,0:T(8,128)} fusion(bf16[2048,1024]{1,0:T(8,128)(2,1)S(1)} %copy-done.55, bf16[384,2048]{1,0:T(8,128)(2,1)S(1)} %collective-permute-done.11, bf16[384,2048]{1,0:T(8,128)(2,1)S(1)} %collective-permute-done.10, bf16[384,2048]{1,0:T(8,128)(2,1)S(1)} %collective-permute-done.9, bf16[384,2048]{1,0:T(8,128)(2,1)S(1)} %fusion.37), kind=kOutput, calls=%fused_computation.204 | convolution fusion | flops 6467616768 | bytes 16777216 | tf_op jit(solution)/shard_map/dot_general | solution.py:21
  478.4 11.6 fusion.67
  490.1 19.0 %fusion.2 = (bf16[1536,1024]{1,0:T(8,128)(2,1)}, bf16[1536,1024]{1,0:T(8,128)(2,1)}) fusion(bf16[1536,1024]{1,0:T(8,128)(2,1)} %convolution_convert_fusion.4, f32[1536,1024]{1,0:T(8,128)} %fusion.69, bf16[2048,1024]{1,0:T(8,128)(2,1)} %all-gather.9.cloned.1.call-done, bf16[384,2048]{1,0:T(8,128)(2,1)} %copy-done.61, bf16[384,2048]{1,0:T(8,128)(2,1)S(1)} %copy-done.58, ...), kind=kOutput, calls=%fused_computation.12 | convolution fusion | flops 6489636864 | bytes 26214400 | tf_op jit(solution)/shard_map/dot_general | solution.py:21
  509.0 12.4 fusion.88
  521.5 12.6 fusion.64
  534.1 15.6 %fusion.6 = (bf16[1536,1024]{1,0:T(8,128)(2,1)}, bf16[1536,1024]{1,0:T(8,128)(2,1)}) fusion(bf16[1536,1024]{1,0:T(8,128)(2,1)} %convolution_convert_fusion.3, f32[1536,1024]{1,0:T(8,128)S(1)} %fusion.67, bf16[2048,1024]{1,0:T(8,128)(2,1)} %collective-permute-done.13, bf16[384,2048]{1,0:T(8,128)(2,1)} %copy-done.61, bf16[384,2048]{1,0:T(8,128)(2,1)} %copy-done.57, ...), kind=kOutput, calls=%fused_computation.16 | convolution fusion | flops 6489636864 | bytes 26214400 | tf_op jit(solution)/shard_map/dot_general | solution.py:21
  549.7 12.2 fusion.89
  561.9 26.6 %fusion.84 = (bf16[1536,2048]{1,0:T(8,128)(2,1)}, f32[1536,2048]{1,0:T(8,128)}) fusion(bf16[2048,1024]{1,0:T(8,128)(2,1)} %collective-permute-done.13, bf16[1536,1024]{1,0:T(8,128)(2,1)} %convolution_convert_fusion.3, f32[1536,1024]{1,0:T(8,128)} %copy-done.4, f32[1536,2048]{1,0:T(8,128)} %fusion.89, f32[1536,2048]{1,0:T(8,128)} %fusion.88, ...), kind=kOutput, calls=%fused_computation.217 | convolution fusion | flops 6466043904 | bytes 70254592 | tf_op jit(solution)/shard_map/dot_general | solution.py:25
  597.1 9.2 fusion.87
  606.3 14.1 %fusion.85 = (bf16[1536,2048]{1,0:T(8,128)(2,1)S(1)}, f32[1536,2048]{1,0:T(8,128)}) fusion(f32[1536,2048]{1,0:T(8,128)} %fusion.87, bf16[1536,1024]{1,0:T(8,128)(2,1)} %get-tuple-element.44, bf16[2048,1024]{1,0:T(8,128)(2,1)} %collective-permute-done.14), kind=kOutput, calls=%fused_computation.218 | convolution fusion | flops 6448742400 | bytes 38797312 | tf_op jit(solution)/shard_map/dot_general | solution.py:25
  623.1 40.2 %collective-permute-done.26 = bf16[384,2048]{1,0:T(8,128)(2,1)S(1)} collective-permute-done((bf16[384,2048]{1,0:T(8,128)(2,1)}, bf16[384,2048]{1,0:T(8,128)(2,1)S(1)}, u32[]{:S(2)}, u32[]{:S(2)}) %collective-permute-start.26) | collective-permute-done | bytes 1572896 | tf_op jit(solution)/shard_map/ppermute | solution.py:317
  671.1 26.5 %collective-permute-done.15 = bf16[384,2048]{1,0:T(8,128)(2,1)S(1)} collective-permute-done((bf16[384,2048]{1,0:T(8,128)(2,1)S(1)}, bf16[384,2048]{1,0:T(8,128)(2,1)S(1)}, u32[]{:S(2)}, u32[]{:S(2)}) %collective-permute-start.15) | collective-permute-done | bytes 1572896 | tf_op jit(solution)/shard_map/ppermute | solution.py:317
  698.9 30.6 %collective-permute-done.17 = bf16[384,2048]{1,0:T(8,128)(2,1)S(1)} collective-permute-done((bf16[384,2048]{1,0:T(8,128)(2,1)S(1)}, bf16[384,2048]{1,0:T(8,128)(2,1)S(1)}, u32[]{:S(2)}, u32[]{:S(2)}) %collective-permute-start.17) | collective-permute-done | bytes 1572896 | tf_op jit(solution)/shard_map/ppermute | solution.py:317
  738.2 8.6 convolution_convert_fusion
  746.9 24.2 %collective-permute-done.29 = bf16[384,2048]{1,0:T(8,128)(2,1)S(1)} collective-permute-done((bf16[384,2048]{1,0:T(8,128)(2,1)S(1)}, bf16[384,2048]{1,0:T(8,128)(2,1)S(1)}, u32[]{:S(2)}, u32[]{:S(2)}) %collective-permute-start.29) | collective-permute-done | bytes 1572896 | tf_op jit(solution)/shard_map/ppermute | solution.py:317
  772.3 29.5 %collective-permute-done.31 = bf16[384,2048]{1,0:T(8,128)(2,1)S(1)} collective-permute-done((bf16[384,2048]{1,0:T(8,128)(2,1)S(1)}, bf16[384,2048]{1,0:T(8,128)(2,1)S(1)}, u32[]{:S(2)}, u32[]{:S(2)}) %collective-permute-start.31) | collective-permute-done | bytes 1572896 | tf_op jit(solution)/shard_map/ppermute | solution.py:317
  809.6 11.6 add_convert_fusion
  822.6 12.1 convolution_convert_fusion.1
  834.9 7.0 collective-permute-done.48
  842.0 13.7 %add_convert_fusion.1 = bf16[2048,1024]{1,0:T(8,128)(2,1)} fusion(bf16[2048,1024]{1,0:T(8,128)(2,1)S(1)} %collective-permute-done.48, bf16[1536,1024]{1,0:T(8,128)(2,1)} %convolution_convert_fusion.4, f32[1536,1024]{1,0:T(8,128)} %fusion.69, bf16[384,2048]{1,0:T(8,128)(2,1)} %copy-done.61, bf16[384,2048]{1,0:T(8,128)(2,1)S(1)} %copy-done.59, ...), kind=kOutput, calls=%fused_computation.4 | convolution fusion | flops 6484918272 | bytes 24117248 | tf_op jit(solution)/shard_map/dot_general | solution.py:29
  855.8 11.6 convolution_convert_fusion.2
  872.6 42.8 %attend_back.1 = (bf16[1536,512]{1,0:T(8,128)(2,1)}, f32[1536,512]{1,0:T(8,128)}, f32[1536,512]{1,0:T(8,128)}, bf16[1024,512]{1,0:T(8,128)(2,1)}, bf16[1024,512]{1,0:T(8,128)(2,1)}) custom-call(bf16[1536,512]{1,0:T(8,128)(2,1)} %get-tuple-element.21.q_ref, bf16[1536,512]{1,0:T(8,128)(2,1)} %get-tuple-element.22.k_ref, ...), custom_call_target="tpu_custom_call" | custom-call | flops 20132659200 | bytes 20000000 | tf_op jit(solution)/shard_map/attend_back/pallas_call | solution.py:234
  922.8 11.1 add_convert_fusion.2
  940.5 10.4 convolution_convert_fusion.5
  950.9 80.8 %collective-permute-start.40 = (bf16[2048,768]{1,0:T(8,128)(2,1)}, bf16[2048,768]{1,0:T(8,128)(2,1)}, u32[]{:S(2)}, u32[]{:S(2)}) collective-permute-start(bf16[2048,768]{1,0:T(8,128)(2,1)} %convolution_convert_fusion.5), channel_id=1, source_target_pairs={{0,1},{1,0},{2,3},{3,2},{4,5},{5,4},{6,7},{7,6},{8,9},{9,8},{10,11... | collective-permute-start | bytes 9437192 | tf_op jit(solution)/shard_map/ppermute | solution.py:331
  1034.5 7.9 fusion.26
  1042.4 12.9 %fusion.86 = (bf16[1536,2048]{1,0:T(8,128)(2,1)}, f32[1536,2048]{1,0:T(8,128)}) fusion(f32[1536,2048]{1,0:T(8,128)} %fusion.26, bf16[2048,1024]{1,0:T(8,128)(2,1)} %collective-permute-done.4.oth_ref, bf16[1536,1536]{1,0:T(8,128)(2,1)S(1)} %pad_maximum_fusion.3), kind=kOutput, calls=%fused_computation.219 | convolution fusion | flops 4838129664 | bytes 36962304 | tf_op jit(solution)/shard_map/dot_general | solution.py:25
  1055.3 10.5 add_convert_fusion.3
  1084.6 65.3 %collective-permute-done.19 = bf16[384,512]{1,0:T(8,128)(2,1)S(1)} collective-permute-done((bf16[384,512]{1,0:T(8,128)(2,1)S(1)}, bf16[384,512]{1,0:T(8,128)(2,1)S(1)}, u32[]{:S(2)}, u32[]{:S(2)}) %collective-permute-start.19) | collective-permute-done | bytes 393248 | tf_op jit(solution)/shard_map/ppermute | solution.py:307
  1173.1 21.8 %collective-permute-start.49 = (bf16[512,1024]{1,0:T(8,128)(2,1)}, bf16[512,1024]{1,0:T(8,128)(2,1)}, u32[]{:S(2)}, u32[]{:S(2)}) collective-permute-start(bf16[512,1024]{1,0:T(8,128)(2,1)} %reduce-scatter.12.cloned.1.call-done), channel_id=1, source_target_pairs={{0,4},{4,0},{1,5},{5,1},{2,6},{6,2},{3,7},{7,3},{8,12},{12,8},{9,1... | collective-permute-start | bytes 3145736 | tf_op jit(solution)/shard_map/ppermute | solution.py:432
  1200.1 15.7 %collective-permute-done.39 = bf16[384,512]{1,0:T(8,128)(2,1)} collective-permute-done((bf16[384,512]{1,0:T(8,128)(2,1)}, bf16[384,512]{1,0:T(8,128)(2,1)}, u32[]{:S(2)}, u32[]{:S(2)}) %collective-permute-start.39) | collective-permute-done | bytes 393248 | tf_op jit(solution)/shard_map/ppermute | solution.py:307
  1221.9 16.2 %collective-permute-done.49 = bf16[512,1024]{1,0:T(8,128)(2,1)} collective-permute-done((bf16[512,1024]{1,0:T(8,128)(2,1)}, bf16[512,1024]{1,0:T(8,128)(2,1)}, u32[]{:S(2)}, u32[]{:S(2)}) %collective-permute-start.49) | collective-permute-done | bytes 1048608 | tf_op jit(solution)/shard_map/ppermute | solution.py:432
  1243.2 10.5 collective-permute-done.47
  (366 shorter events, 216.2 us)
Async XLA Ops:
  7.2 87.1 %all-gather.5.cloned.1.call-start = ((), (), s32[]{:S(2)}) async-start(), calls=%async_computation.5 | async-start | bytes 5242880 | tf_op jit(solution)/shard_map/all_gather | solution.py:350
  10.7 243.8 %all-gather.7.cloned.1.call-start = ((), (), s32[]{:S(2)}) async-start(), calls=%async_computation.6 | async-start | bytes 5242880 | tf_op jit(solution)/shard_map/all_gather | solution.py:350
  11.9 263.6 %all-gather.11.cloned.1.call-start = ((), (), s32[]{:S(2)}) async-start(), calls=%async_computation.8 | async-start | bytes 5242880 | tf_op jit(solution)/shard_map/all_gather | solution.py:350
  14.2 344.6 %all-gather.9.cloned.1.call-start = ((), (), s32[]{:S(2)}) async-start(), calls=%async_computation.7 | async-start | bytes 5242880 | tf_op jit(solution)/shard_map/all_gather | solution.py:350
  94.3 89.2 %collective-permute-start.4 = (bf16[2048,1024]{1,0:T(8,128)(2,1)}, bf16[2048,1024]{1,0:T(8,128)(2,1)}, u32[]{:S(2)}, u32[]{:S(2)}) collective-permute-start(bf16[2048,1024]{1,0:T(8,128)(2,1)} %all-gather.5.cloned.1.call-done.own_ref), channel_id=1, source_target_pairs={{0,1},{1,0},{2,3},{3,2},{4,5},{5,4},{6,7},{7,6},{8,9},{9,8},{10,11... | collective-permute-start | bytes 12582920 | tf_op jit(solution)/shard_map/ppermute | solution.py:331
  107.6 35.2 %collective-permute-start.1 = (bf16[1536,512]{1,0:T(8,128)(2,1)}, bf16[1536,512]{1,0:T(8,128)(2,1)}, u32[]{:S(2)}, u32[]{:S(2)}) collective-permute-start(bf16[1536,512]{1,0:T(8,128)(2,1)} %param.11), channel_id=1, source_target_pairs={{0,4},{1,0},{2,6},{3,2},{4,5},{5,1},{6,7},{7,3},{8,12},{9,8},{10,1... | collective-permute-start | bytes 4718600 | tf_op jit(solution)/shard_map/ppermute | solution.py:293
  107.6 69.1 %collective-permute-start.2 = (bf16[1536,512]{1,0:T(8,128)(2,1)}, bf16[1536,512]{1,0:T(8,128)(2,1)}, u32[]{:S(2)}, u32[]{:S(2)}) collective-permute-start(bf16[1536,512]{1,0:T(8,128)(2,1)} %param.11), channel_id=1, source_target_pairs={{0,2},{1,6},{2,0},{3,4},{4,3},{5,7},{6,1},{7,5},{8,10},{9,14},{10,... | collective-permute-start | bytes 4718600 | tf_op jit(solution)/shard_map/ppermute | solution.py:293
  109.1 73.0 %collective-permute-start.3 = (bf16[1536,512]{1,0:T(8,128)(2,1)}, bf16[1536,512]{1,0:T(8,128)(2,1)S(1)}, u32[]{:S(2)}, u32[]{:S(2)}) collective-permute-start(bf16[1536,512]{1,0:T(8,128)(2,1)} %param.11), channel_id=1, source_target_pairs={{0,6},{1,2},{2,4},{3,0},{4,7},{5,3},{6,5},{7,1},{8,14},{9,10},{10,... | collective-permute-start | bytes 4718600 | tf_op jit(solution)/shard_map/ppermute | solution.py:293
  113.0 1039.3 %reduce-scatter.8.cloned.1.call-start = ((), (), s32[]{:S(2)}) async-start(), calls=%async_computation.10 | async-start | bytes 1310720 | tf_op jit(solution)/shard_map/reduce_scatter | solution.py:428
  120.1 87.3 %collective-permute-start.22 = (bf16[1536,512]{1,0:T(8,128)(2,1)}, bf16[1536,512]{1,0:T(8,128)(2,1)}, u32[]{:S(2)}, u32[]{:S(2)}) collective-permute-start(bf16[1536,512]{1,0:T(8,128)(2,1)} %param.12), channel_id=1, source_target_pairs={{0,0},{1,4},{2,2},{3,6},{4,1},{5,5},{6,3},{7,7},{8,8},{9,12},{10,1... | collective-permute-start | bytes 4718600 | tf_op jit(solution)/shard_map/ppermute | solution.py:293
  142.8 67.5 %collective-permute-start.23 = (bf16[1536,512]{1,0:T(8,128)(2,1)}, bf16[1536,512]{1,0:T(8,128)(2,1)}, u32[]{:S(2)}, u32[]{:S(2)}) collective-permute-start(bf16[1536,512]{1,0:T(8,128)(2,1)} %param.12), channel_id=1, source_target_pairs={{0,4},{1,0},{2,6},{3,2},{4,5},{5,1},{6,7},{7,3},{8,12},{9,8},{10,1... | collective-permute-start | bytes 4718600 | tf_op jit(solution)/shard_map/ppermute | solution.py:293
  176.7 69.2 %collective-permute-start.24 = (bf16[1536,512]{1,0:T(8,128)(2,1)}, bf16[1536,512]{1,0:T(8,128)(2,1)}, u32[]{:S(2)}, u32[]{:S(2)}) collective-permute-start(bf16[1536,512]{1,0:T(8,128)(2,1)} %param.12), channel_id=1, source_target_pairs={{0,2},{1,6},{2,0},{3,4},{4,3},{5,7},{6,1},{7,5},{8,10},{9,14},{10,... | collective-permute-start | bytes 4718600 | tf_op jit(solution)/shard_map/ppermute | solution.py:293
  182.1 66.5 %collective-permute-start.25 = (bf16[1536,512]{1,0:T(8,128)(2,1)}, bf16[1536,512]{1,0:T(8,128)(2,1)}, u32[]{:S(2)}, u32[]{:S(2)}) collective-permute-start(bf16[1536,512]{1,0:T(8,128)(2,1)} %param.12), channel_id=1, source_target_pairs={{0,6},{1,2},{2,4},{3,0},{4,7},{5,3},{6,5},{7,1},{8,14},{9,10},{10,... | collective-permute-start | bytes 4718600 | tf_op jit(solution)/shard_map/ppermute | solution.py:293
  202.8 74.9 %collective-permute-start.5 = (bf16[1024,1024]{1,0:T(8,128)(2,1)}, bf16[1024,1024]{1,0:T(8,128)(2,1)}, u32[]{:S(2)}, u32[]{:S(2)}) collective-permute-start(bf16[1024,1024]{1,0:T(8,128)(2,1)} %get-tuple-element.24), channel_id=1, source_target_pairs={{0,1},{1,8},{2,3},{3,10},{8,9},{9,16},{10,11},{11,18},{16,17},{17,... | collective-permute-start | bytes 6291464 | tf_op jit(solution)/shard_map/ppermute | solution.py:382
  254.4 223.9 %collective-permute-start.12 = (bf16[2048,1024]{1,0:T(8,128)(2,1)}, bf16[2048,1024]{1,0:T(8,128)(2,1)}, u32[]{:S(2)}, u32[]{:S(2)}) collective-permute-start(bf16[2048,1024]{1,0:T(8,128)(2,1)} %all-gather.7.cloned.1.call-done), channel_id=1, source_target_pairs={{0,1},{1,0},{2,3},{3,2},{4,5},{5,4},{6,7},{7,6},{8,9},{9,8},{10,11... | collective-permute-start | bytes 12582920 | tf_op jit(solution)/shard_map/ppermute | solution.py:331
  275.5 121.1 %collective-permute-start.14 = (bf16[2048,1024]{1,0:T(8,128)(2,1)}, bf16[2048,1024]{1,0:T(8,128)(2,1)}, u32[]{:S(2)}, u32[]{:S(2)}) collective-permute-start(bf16[2048,1024]{1,0:T(8,128)(2,1)} %all-gather.11.cloned.1.call-done), channel_id=1, source_target_pairs={{0,1},{1,0},{2,3},{3,2},{4,5},{5,4},{6,7},{7,6},{8,9},{9,8},{10,11... | collective-permute-start | bytes 12582920 | tf_op jit(solution)/shard_map/ppermute | solution.py:331
  312.8 46.0 %collective-permute-start.6 = (bf16[384,2048]{1,0:T(8,128)(2,1)}, bf16[384,2048]{1,0:T(8,128)(2,1)}, u32[]{:S(2)}, u32[]{:S(2)}) collective-permute-start(bf16[384,2048]{1,0:T(8,128)(2,1)} %convolution_convert_fusion.9), channel_id=1, source_target_pairs={{0,2},{1,3},{2,0},{3,1},{4,6},{5,7},{6,4},{7,5},{8,10},{9,11},{10,... | collective-permute-start | bytes 4718600 | tf_op jit(solution)/shard_map/ppermute | solution.py:317
  316.6 42.1 %collective-permute-start.7 = (bf16[384,2048]{1,0:T(8,128)(2,1)}, bf16[384,2048]{1,0:T(8,128)(2,1)}, u32[]{:S(2)}, u32[]{:S(2)}) collective-permute-start(bf16[384,2048]{1,0:T(8,128)(2,1)} %convolution_convert_fusion.8), channel_id=1, source_target_pairs={{0,4},{1,5},{2,6},{3,7},{4,0},{5,1},{6,2},{7,3},{8,12},{9,13},{10,... | collective-permute-start | bytes 4718600 | tf_op jit(solution)/shard_map/ppermute | solution.py:317
  320.3 66.7 %collective-permute-start.8 = (bf16[384,2048]{1,0:T(8,128)(2,1)}, bf16[384,2048]{1,0:T(8,128)(2,1)}, u32[]{:S(2)}, u32[]{:S(2)}) collective-permute-start(bf16[384,2048]{1,0:T(8,128)(2,1)} %convolution_convert_fusion.7), channel_id=1, source_target_pairs={{0,6},{1,7},{2,4},{3,5},{4,2},{5,3},{6,0},{7,1},{8,14},{9,15},{10,... | collective-permute-start | bytes 4718600 | tf_op jit(solution)/shard_map/ppermute | solution.py:317
  358.8 175.3 %collective-permute-start.13 = (bf16[2048,1024]{1,0:T(8,128)(2,1)}, bf16[2048,1024]{1,0:T(8,128)(2,1)}, u32[]{:S(2)}, u32[]{:S(2)}) collective-permute-start(bf16[2048,1024]{1,0:T(8,128)(2,1)} %all-gather.9.cloned.1.call-done), channel_id=1, source_target_pairs={{0,1},{1,0},{2,3},{3,2},{4,5},{5,4},{6,7},{7,6},{8,9},{9,8},{10,11... | collective-permute-start | bytes 12582920 | tf_op jit(solution)/shard_map/ppermute | solution.py:331
  393.4 37.3 %collective-permute-start.10 = (bf16[384,2048]{1,0:T(8,128)(2,1)S(1)}, bf16[384,2048]{1,0:T(8,128)(2,1)S(1)}, u32[]{:S(2)}, u32[]{:S(2)}) collective-permute-start(bf16[384,2048]{1,0:T(8,128)(2,1)S(1)} %fusion.37), channel_id=1, source_target_pairs={{0,4},{1,5},{2,6},{3,7},{4,0},{5,1},{6,2},{7,3},{8,12},{9,13},{10,... | collective-permute-start | bytes 4718600 | tf_op jit(solution)/shard_map/ppermute | solution.py:317
  395.1 68.9 %collective-permute-start.11 = (bf16[384,2048]{1,0:T(8,128)(2,1)S(1)}, bf16[384,2048]{1,0:T(8,128)(2,1)S(1)}, u32[]{:S(2)}, u32[]{:S(2)}) collective-permute-start(bf16[384,2048]{1,0:T(8,128)(2,1)S(1)} %fusion.37), channel_id=1, source_target_pairs={{0,6},{1,7},{2,4},{3,5},{4,2},{5,3},{6,0},{7,1},{8,14},{9,15},{10,... | collective-permute-start | bytes 4718600 | tf_op jit(solution)/shard_map/ppermute | solution.py:317
  396.5 68.8 %collective-permute-start.9 = (bf16[384,2048]{1,0:T(8,128)(2,1)S(1)}, bf16[384,2048]{1,0:T(8,128)(2,1)S(1)}, u32[]{:S(2)}, u32[]{:S(2)}) collective-permute-start(bf16[384,2048]{1,0:T(8,128)(2,1)S(1)} %fusion.37), channel_id=1, source_target_pairs={{0,2},{1,3},{2,0},{3,1},{4,6},{5,7},{6,4},{7,5},{8,10},{9,11},{10,... | collective-permute-start | bytes 4718600 | tf_op jit(solution)/shard_map/ppermute | solution.py:317
  593.6 69.7 %collective-permute-start.26 = (bf16[384,2048]{1,0:T(8,128)(2,1)}, bf16[384,2048]{1,0:T(8,128)(2,1)S(1)}, u32[]{:S(2)}, u32[]{:S(2)}) collective-permute-start(bf16[384,2048]{1,0:T(8,128)(2,1)} %get-tuple-element.50), channel_id=1, source_target_pairs={{0,2},{1,3},{2,0},{3,1},{4,6},{5,7},{6,4},{7,5},{8,10},{9,11},{10,... | collective-permute-start | bytes 4718600 | tf_op jit(solution)/shard_map/ppermute | solution.py:317
  593.9 70.8 %collective-permute-start.27 = (bf16[384,2048]{1,0:T(8,128)(2,1)}, bf16[384,2048]{1,0:T(8,128)(2,1)}, u32[]{:S(2)}, u32[]{:S(2)}) collective-permute-start(bf16[384,2048]{1,0:T(8,128)(2,1)} %get-tuple-element.52), channel_id=1, source_target_pairs={{0,4},{1,5},{2,6},{3,7},{4,0},{5,1},{6,2},{7,3},{8,12},{9,13},{10,... | collective-permute-start | bytes 4718600 | tf_op jit(solution)/shard_map/ppermute | solution.py:317
  595.6 70.8 %collective-permute-start.28 = (bf16[384,2048]{1,0:T(8,128)(2,1)}, bf16[384,2048]{1,0:T(8,128)(2,1)}, u32[]{:S(2)}, u32[]{:S(2)}) collective-permute-start(bf16[384,2048]{1,0:T(8,128)(2,1)} %get-tuple-element.51), channel_id=1, source_target_pairs={{0,6},{1,7},{2,4},{3,5},{4,2},{5,3},{6,0},{7,1},{8,14},{9,15},{10,... | collective-permute-start | bytes 4718600 | tf_op jit(solution)/shard_map/ppermute | solution.py:317
  621.0 76.6 %collective-permute-start.15 = (bf16[384,2048]{1,0:T(8,128)(2,1)S(1)}, bf16[384,2048]{1,0:T(8,128)(2,1)S(1)}, u32[]{:S(2)}, u32[]{:S(2)}) collective-permute-start(bf16[384,2048]{1,0:T(8,128)(2,1)S(1)} %get-tuple-element.57), channel_id=1, source_target_pairs={{0,2},{1,3},{2,0},{3,1},{4,6},{5,7},{6,4},{7,5},{8,10},{9,11},{10,... | collective-permute-start | bytes 4718600 | tf_op jit(solution)/shard_map/ppermute | solution.py:317
  621.4 77.5 %collective-permute-start.16 = (bf16[384,2048]{1,0:T(8,128)(2,1)S(1)}, bf16[384,2048]{1,0:T(8,128)(2,1)S(1)}, u32[]{:S(2)}, u32[]{:S(2)}) collective-permute-start(bf16[384,2048]{1,0:T(8,128)(2,1)S(1)} %get-tuple-element.59), channel_id=1, source_target_pairs={{0,4},{1,5},{2,6},{3,7},{4,0},{5,1},{6,2},{7,3},{8,12},{9,13},{10,... | collective-permute-start | bytes 4718600 | tf_op jit(solution)/shard_map/ppermute | solution.py:317
  663.3 66.2 %collective-permute-start.17 = (bf16[384,2048]{1,0:T(8,128)(2,1)S(1)}, bf16[384,2048]{1,0:T(8,128)(2,1)S(1)}, u32[]{:S(2)}, u32[]{:S(2)}) collective-permute-start(bf16[384,2048]{1,0:T(8,128)(2,1)S(1)} %get-tuple-element.58), channel_id=1, source_target_pairs={{0,6},{1,7},{2,4},{3,5},{4,2},{5,3},{6,0},{7,1},{8,14},{9,15},{10,... | collective-permute-start | bytes 4718600 | tf_op jit(solution)/shard_map/ppermute | solution.py:317
  734.6 36.5 %collective-permute-start.29 = (bf16[384,2048]{1,0:T(8,128)(2,1)S(1)}, bf16[384,2048]{1,0:T(8,128)(2,1)S(1)}, u32[]{:S(2)}, u32[]{:S(2)}) collective-permute-start(bf16[384,2048]{1,0:T(8,128)(2,1)S(1)} %get-tuple-element.38), channel_id=1, source_target_pairs={{0,2},{1,3},{2,0},{3,1},{4,6},{5,7},{6,4},{7,5},{8,10},{9,11},{10,... | collective-permute-start | bytes 4718600 | tf_op jit(solution)/shard_map/ppermute | solution.py:317
  735.0 37.3 %collective-permute-start.30 = (bf16[384,2048]{1,0:T(8,128)(2,1)S(1)}, bf16[384,2048]{1,0:T(8,128)(2,1)S(1)}, u32[]{:S(2)}, u32[]{:S(2)}) collective-permute-start(bf16[384,2048]{1,0:T(8,128)(2,1)S(1)} %get-tuple-element.38), channel_id=1, source_target_pairs={{0,4},{1,5},{2,6},{3,7},{4,0},{5,1},{6,2},{7,3},{8,12},{9,13},{10,... | collective-permute-start | bytes 4718600 | tf_op jit(solution)/shard_map/ppermute | solution.py:317
  736.8 65.0 %collective-permute-start.31 = (bf16[384,2048]{1,0:T(8,128)(2,1)S(1)}, bf16[384,2048]{1,0:T(8,128)(2,1)S(1)}, u32[]{:S(2)}, u32[]{:S(2)}) collective-permute-start(bf16[384,2048]{1,0:T(8,128)(2,1)S(1)} %get-tuple-element.38), channel_id=1, source_target_pairs={{0,6},{1,7},{2,4},{3,5},{4,2},{5,3},{6,0},{7,1},{8,14},{9,15},{10,... | collective-permute-start | bytes 4718600 | tf_op jit(solution)/shard_map/ppermute | solution.py:317
  746.8 62.8 %collective-permute-start.50 = (bf16[2048,1024]{1,0:T(8,128)(2,1)}, bf16[2048,1024]{1,0:T(8,128)(2,1)}, u32[]{:S(2)}, u32[]{:S(2)}) collective-permute-start(bf16[2048,1024]{1,0:T(8,128)(2,1)} %convolution_convert_fusion), channel_id=1, source_target_pairs={{0,1},{1,0},{2,3},{3,2},{4,5},{5,4},{6,7},{7,6},{8,9},{9,8},{10,11... | collective-permute-start | bytes 12582920 | tf_op jit(solution)/shard_map/ppermute | solution.py:331
  809.6 355.2 %reduce-scatter.14.cloned.1.call-start = ((), (), s32[]{:S(2)}) async-start(), calls=%async_computation.13 | async-start | bytes 5242880 | tf_op jit(solution)/shard_map/reduce_scatter | solution.py:428
  821.3 351.9 %reduce-scatter.12.cloned.1.call-start = ((), (), s32[]{:S(2)}) async-start(), calls=%async_computation.12 | async-start | bytes 5242880 | tf_op jit(solution)/shard_map/reduce_scatter | solution.py:428
  855.7 361.2 %reduce-scatter.10.cloned.1.call-start = ((), (), s32[]{:S(2)}) async-start(), calls=%async_computation.11 | async-start | bytes 5242880 | tf_op jit(solution)/shard_map/reduce_scatter | solution.py:428
  867.5 55.3 %collective-permute-start.46 = (bf16[2048,1024]{1,0:T(8,128)(2,1)}, bf16[2048,1024]{1,0:T(8,128)(2,1)}, u32[]{:S(2)}, u32[]{:S(2)}) collective-permute-start(bf16[2048,1024]{1,0:T(8,128)(2,1)} %convolution_convert_fusion.2), channel_id=1, source_target_pairs={{0,1},{1,0},{2,3},{3,2},{4,5},{5,4},{6,7},{7,6},{8,9},{9,8},{10,11... | collective-permute-start | bytes 12582920 | tf_op jit(solution)/shard_map/ppermute | solution.py:331
  934.0 308.1 %reduce-scatter.6.cloned.1.call-start = ((), (), s32[]{:S(2)}) async-start(), calls=%async_computation.9 | async-start | bytes 3932160 | tf_op jit(solution)/shard_map/reduce_scatter | solution.py:428
  950.9 104.5 %collective-permute-start.40 = (bf16[2048,768]{1,0:T(8,128)(2,1)}, bf16[2048,768]{1,0:T(8,128)(2,1)}, u32[]{:S(2)}, u32[]{:S(2)}) collective-permute-start(bf16[2048,768]{1,0:T(8,128)(2,1)} %convolution_convert_fusion.5), channel_id=1, source_target_pairs={{0,1},{1,0},{2,3},{3,2},{4,5},{5,4},{6,7},{7,6},{8,9},{9,8},{10,11... | collective-permute-start | bytes 9437192 | tf_op jit(solution)/shard_map/ppermute | solution.py:331
  1070.7 86.2 %collective-permute-start.33 = (bf16[384,2048]{1,0:T(8,128)(2,1)}, bf16[384,2048]{1,0:T(8,128)(2,1)}, u32[]{:S(2)}, u32[]{:S(2)}) collective-permute-start(bf16[384,2048]{1,0:T(8,128)(2,1)} %get-tuple-element.45), channel_id=1, source_target_pairs={{0,2},{1,3},{2,0},{3,1},{4,6},{5,7},{6,4},{7,5},{8,10},{9,11},{10,... | collective-permute-start | bytes 4718600 | tf_op jit(solution)/shard_map/ppermute | solution.py:317
  1071.5 85.4 %collective-permute-start.34 = (bf16[384,2048]{1,0:T(8,128)(2,1)}, bf16[384,2048]{1,0:T(8,128)(2,1)}, u32[]{:S(2)}, u32[]{:S(2)}) collective-permute-start(bf16[384,2048]{1,0:T(8,128)(2,1)} %get-tuple-element.47), channel_id=1, source_target_pairs={{0,4},{1,5},{2,6},{3,7},{4,0},{5,1},{6,2},{7,3},{8,12},{9,13},{10,... | collective-permute-start | bytes 4718600 | tf_op jit(solution)/shard_map/ppermute | solution.py:317
  1073.1 83.8 %collective-permute-start.35 = (bf16[384,2048]{1,0:T(8,128)(2,1)}, bf16[384,2048]{1,0:T(8,128)(2,1)}, u32[]{:S(2)}, u32[]{:S(2)}) collective-permute-start(bf16[384,2048]{1,0:T(8,128)(2,1)} %get-tuple-element.46), channel_id=1, source_target_pairs={{0,6},{1,7},{2,4},{3,5},{4,2},{5,3},{6,0},{7,1},{8,14},{9,15},{10,... | collective-permute-start | bytes 4718600 | tf_op jit(solution)/shard_map/ppermute | solution.py:317
  1076.8 73.1 %collective-permute-start.19 = (bf16[384,512]{1,0:T(8,128)(2,1)S(1)}, bf16[384,512]{1,0:T(8,128)(2,1)S(1)}, u32[]{:S(2)}, u32[]{:S(2)}) collective-permute-start(bf16[384,512]{1,0:T(8,128)(2,1)S(1)} %get-tuple-element.94), channel_id=1, source_target_pairs={{0,1},{1,5},{2,3},{3,7},{4,0},{5,4},{6,2},{7,6},{8,9},{9,13},{10,1... | collective-permute-start | bytes 1179656 | tf_op jit(solution)/shard_map/ppermute | solution.py:307
  1081.4 70.1 %collective-permute-start.20 = (bf16[384,512]{1,0:T(8,128)(2,1)S(1)}, bf16[384,512]{1,0:T(8,128)(2,1)S(1)}, u32[]{:S(2)}, u32[]{:S(2)}) collective-permute-start(bf16[384,512]{1,0:T(8,128)(2,1)S(1)} %get-tuple-element.93), channel_id=1, source_target_pairs={{0,2},{1,6},{2,0},{3,4},{4,3},{5,7},{6,1},{7,5},{8,10},{9,14},{10,... | collective-permute-start | bytes 1179656 | tf_op jit(solution)/shard_map/ppermute | solution.py:307
  1164.7 53.3 %collective-permute-start.51 = (bf16[512,1024]{1,0:T(8,128)(2,1)}, bf16[512,1024]{1,0:T(8,128)(2,1)}, u32[]{:S(2)}, u32[]{:S(2)}) collective-permute-start(bf16[512,1024]{1,0:T(8,128)(2,1)} %reduce-scatter.14.cloned.1.call-done), channel_id=1, source_target_pairs={{0,4},{4,0},{1,5},{5,1},{2,6},{6,2},{3,7},{7,3},{8,12},{12,8},{9,1... | collective-permute-start | bytes 3145736 | tf_op jit(solution)/shard_map/ppermute | solution.py:432
  1171.9 43.9 %collective-permute-start.39 = (bf16[384,512]{1,0:T(8,128)(2,1)}, bf16[384,512]{1,0:T(8,128)(2,1)}, u32[]{:S(2)}, u32[]{:S(2)}) collective-permute-start(bf16[384,512]{1,0:T(8,128)(2,1)} %get-tuple-element.84), channel_id=1, source_target_pairs={{0,3},{1,7},{2,1},{3,5},{4,2},{5,6},{6,0},{7,4},{8,11},{9,15},{10,... | collective-permute-start | bytes 1179656 | tf_op jit(solution)/shard_map/ppermute | solution.py:307
  1173.1 65.0 %collective-permute-start.49 = (bf16[512,1024]{1,0:T(8,128)(2,1)}, bf16[512,1024]{1,0:T(8,128)(2,1)}, u32[]{:S(2)}, u32[]{:S(2)}) collective-permute-start(bf16[512,1024]{1,0:T(8,128)(2,1)} %reduce-scatter.12.cloned.1.call-done), channel_id=1, source_target_pairs={{0,4},{4,0},{1,5},{5,1},{2,6},{6,2},{3,7},{7,3},{8,12},{12,8},{9,1... | collective-permute-start | bytes 3145736 | tf_op jit(solution)/shard_map/ppermute | solution.py:432
  1216.9 36.8 %collective-permute-start.47 = (bf16[512,1024]{1,0:T(8,128)(2,1)}, bf16[512,1024]{1,0:T(8,128)(2,1)}, u32[]{:S(2)}, u32[]{:S(2)}) collective-permute-start(bf16[512,1024]{1,0:T(8,128)(2,1)} %reduce-scatter.10.cloned.1.call-done), channel_id=1, source_target_pairs={{0,4},{4,0},{1,5},{5,1},{2,6},{6,2},{3,7},{7,3},{8,12},{12,8},{9,1... | collective-permute-start | bytes 3145736 | tf_op jit(solution)/shard_map/ppermute | solution.py:432
  (91 other events, 1891.5 us)
Sparse Core Ops, SparseCore 0:
  10.8 83.4 all-gather.4
  96.4 79.2 all-gather.6
  177.9 97.5 all-gather.10
  277.5 81.2 all-gather.8
  809.7 26.5 reduce-scatter.7
  839.1 75.4 reduce-scatter.13
  917.4 96.7 reduce-scatter.11
  1017.1 77.2 reduce-scatter.9
  1096.8 60.7 reduce-scatter.5

commit v2 on v1

v2 whole, which is shorter than its diff:
```python
import functools
import math

import jax
import jax.numpy as jnp
from jax import lax
from jax.experimental import pallas as pl
from jax.experimental.pallas import tpu as pltpu
from jax.sharding import PartitionSpec as P

HD = 128
HALO = 1024
EPSILON = 1e-05
NEG_FILL = -1e30
PLANE = ("ctx", "tp")
BF = jnp.bfloat16
F32 = jnp.float32


def takes(microseconds):
    return pl.CostEstimate(
        flops=int(microseconds * 30e6), bytes_accessed=1, transcendentals=0
    )


def dot_plain(left, right):
    return jnp.dot(left, right, preferred_element_type=F32)


def dot_last(left, right):
    return lax.dot_general(left, right, (((1,), (1,)), ((), ())), preferred_element_type=F32)


def dot_rows(left, right):
    return lax.dot_general(left, right, (((0,), (0,)), ((), ())), preferred_element_type=F32)


def normalize(values):
    average = jnp.mean(values, axis=-1, keepdims=True)
    centred = values - average
    spread = jnp.mean(centred * centred, axis=-1, keepdims=True)
    inv_dev = lax.rsqrt(spread + EPSILON)
    return (centred * inv_dev, inv_dev)


def norm_back(grad, normed, inv_dev):
    grad_mean = jnp.mean(grad, axis=-1, keepdims=True)
    cross_mean = jnp.mean(grad * normed, axis=-1, keepdims=True)
    return inv_dev * (grad - grad_mean - normed * cross_mean)


def slots(lengths, order):
    seq_len = lengths.reshape(-1)
    seq_ids = jnp.arange(seq_len.shape[0], dtype=jnp.int32)
    picks = order[:, None] == seq_ids[None, :]
    order_len = jnp.sum(jnp.where(picks, seq_len[None, :], 0), axis=1)
    return jnp.cumsum(order_len) - order_len


def first_of(index, starts):
    inside = index[:, None] >= starts[None, :]
    return jnp.max(jnp.where(inside, starts[None, :], 0), axis=1)


def qkv_kernel(heads, table, *refs):
    *pieces, own_ref, oth_ref, cos_ref, sin_ref, x_ref, h_ref, q_ref, k_ref, v_ref, e_ref = refs
    cols = pieces[0].shape[1]
    for i, piece in enumerate(pieces):
        x_ref[:, pl.ds(pl.multiple_of(table[i] * cols, cols), cols)] = piece[...]
    values = x_ref[...].astype(F32)
    normed, _ = normalize(values)
    hidden = normed.astype(BF)
    h_ref[...] = hidden
    cos, sin = cos_ref[...], sin_ref[...]
    width = heads * HD
    for piece, w_ref in enumerate((own_ref, oth_ref)):
        out = dot_plain(hidden, w_ref[...])
        for head in range(heads):
            to = (piece * heads + head) * HD
            swapped = ((1 - piece) * heads + head) * HD
            query = out[:, head * HD : (head + 1) * HD]
            key = out[:, width + head * HD : width + (head + 1) * HD]
            value = out[:, 2 * width + head * HD : 2 * width + (head + 1) * HD].astype(BF)
            query = (query * cos + pltpu.roll(query, HD // 2, 1) * sin).astype(BF)
            key = (key * cos + pltpu.roll(key, HD // 2, 1) * sin).astype(BF)
            q_ref[:, to : to + HD] = query
            k_ref[:, to : to + HD] = key
            v_ref[:, to : to + HD] = value
            e_ref[:, swapped : swapped + HD] = key
            e_ref[:, 2 * width + swapped : 2 * width + swapped + HD] = value


def project(pieces, places, w_own, w_oth, cos_tab, sin_tab, heads):
    rows, cols = pieces[0].shape
    width = cols * len(pieces)
    block = rows // 3
    skip = rows // block - HALO // block
    local = 2 * heads * HD
    row = lambda i, t: (i, 0)
    once = pl.BlockSpec((width, 3 * heads * HD), lambda i, t: (0, 0))
    table = pl.BlockSpec((block, HD), lambda i, t: (i + HALO // block, 0))
    part = pl.BlockSpec((block, local), row)
    return pl.pallas_call(
        functools.partial(qkv_kernel, heads),
        grid_spec=pltpu.PrefetchScalarGridSpec(
            num_scalar_prefetch=1,
            grid=(rows // block,),
            in_specs=[pl.BlockSpec((block, cols), row)] * len(pieces) + [once, once, table, table],
            out_specs=[pl.BlockSpec((block, width), row)] * 2
            + [part] * 3
            + [pl.BlockSpec((block, 2 * local), lambda i, t: (jnp.maximum(i - skip, 0), 0))],
        ),
        out_shape=[jax.ShapeDtypeStruct((rows, width), BF)] * 2
        + [jax.ShapeDtypeStruct((rows, local), BF)] * 3
        + [jax.ShapeDtypeStruct((HALO, 2 * local), BF)],
        cost_estimate=takes(20),
        name="norm_project",
    )(jnp.stack([jnp.asarray(p, jnp.int32) for p in places]), *pieces, w_own, w_oth, cos_tab, sin_tab)


def join_kernel(table, *refs):
    *pieces, out_ref = refs
    cols = pieces[0].shape[1]
    for i, piece in enumerate(pieces):
        out_ref[:, pl.ds(pl.multiple_of(table[i] * cols, cols), cols)] = piece[...]


def join(pieces, places, chunks):
    rows, cols = pieces[0].shape
    count, ranks = len(pieces), len(chunks)
    chunk = rows // ranks
    table = jnp.stack([jnp.asarray(v, jnp.int32) for v in list(places) + list(chunks)])
    piece = pl.BlockSpec((chunk, cols), lambda i, t: (t[count + i], 0))
    return pl.pallas_call(
        join_kernel,
        grid_spec=pltpu.PrefetchScalarGridSpec(
            num_scalar_prefetch=1,
            grid=(ranks,),
            in_specs=[piece] * count,
            out_specs=pl.BlockSpec((chunk, cols * count), lambda i, t: (i, 0)),
        ),
        out_shape=jax.ShapeDtypeStruct((rows, cols * count), pieces[0].dtype),
        cost_estimate=takes(5),
        name="join",
    )(table, *pieces)


def pack_kernel(table, *refs):
    *ins, out_ref = refs
    at = 0
    for ref in ins:
        out_ref[:, at : at + ref.shape[1]] = ref[...]
        at += ref.shape[1]


def pack(weights, c, at, size, steps):
    rows = weights[0].shape[0]
    cols = weights[0].shape[1] // 2
    table = jnp.asarray(c, jnp.int32).reshape(1)
    spec = pl.BlockSpec((rows, size), lambda n, t: (0, t[0] * (cols // size) + at // size + n))
    return pl.pallas_call(
        pack_kernel,
        grid_spec=pltpu.PrefetchScalarGridSpec(
            num_scalar_prefetch=1,
            grid=(steps,),
            in_specs=[spec] * len(weights),
            out_specs=pl.BlockSpec((rows, size * len(weights)), lambda n, t: (0, n)),
        ),
        out_shape=jax.ShapeDtypeStruct((rows, size * len(weights) * steps), weights[0].dtype),
        cost_estimate=takes(2),
        name="pack",
    )(table, *weights)


def allowed_keys(first_ref, step, block):
    span = block + HALO
    keys = lax.broadcasted_iota(jnp.int32, (block, span), 1)
    rows = lax.broadcasted_iota(jnp.int32, (block, span), 0)
    first = first_ref[...] - step * block
    return (keys >= first) & (keys <= rows + HALO)


def attend_kernel(late, base, q_ref, k_ref, v_ref, *refs):
    if late:
        first_ref, o_ref, lse_ref = refs
    else:
        ke_ref, ve_ref, first_ref, _, _, o_ref, lse_ref, keys, values = refs
    step = pl.program_id(1) + base
    block = q_ref.shape[0]
    if late:
        window = pl.ds(pl.multiple_of(step * block - HALO, block), block + HALO)
        key, value = k_ref[window, :], v_ref[window, :]
    else:

        @pl.when(pl.program_id(1) == 0)
        def _():
            keys[:HALO] = ke_ref[...]
            keys[HALO:] = k_ref[...]
            values[:HALO] = ve_ref[...]
            values[HALO:] = v_ref[...]

        window = pl.ds(pl.multiple_of(step * block, block), block + HALO)
        key, value = keys[window, :], values[window, :]
    raw = dot_last(q_ref[...], key) * (HD**-0.5)
    raw = jnp.where(allowed_keys(first_ref, step, block), raw, NEG_FILL)
    top = jnp.max(raw, axis=-1, keepdims=True)
    expo = jnp.exp(raw - top)
    denom = jnp.sum(expo, axis=-1, keepdims=True)
    probs = (expo * (1.0 / denom)).astype(BF)
    o_ref[...] = dot_plain(probs, value).astype(BF)
    lse_ref[...] = top + jnp.log(denom)


def attend(q, k, v, halo, first, done=None, block=256):
    rows, local = q.shape
    heads = local // HD
    late = halo is None
    base = HALO // block if late else 0
    steps = rows // block - base if late else HALO // block
    row = pl.BlockSpec((block, HD), lambda h, i: (base + i, h))
    column = pl.BlockSpec((rows, HD), lambda h, i: (0, h))
    bound = pl.BlockSpec((block, 1), lambda h, i: (base + i, 0))
    norm = pl.BlockSpec((None, block, 1), lambda h, i: (h, base + i, 0))
    if late:
        in_specs, operands, scratch, aliases = [row, column, column, bound], (q, k, v, first), [], {}
    else:
        edge = [pl.BlockSpec((HALO, HD), lambda h, i, at=at: (0, h + at)) for at in (0, heads)]
        whole = pl.BlockSpec(memory_space=pl.ANY)
        in_specs = [row, column, column] + edge + [bound, whole, whole]
        operands = (q, k, v, halo, halo, first) + tuple(done)
        scratch = [pltpu.VMEM((HALO + rows, HD), BF)] * 2
        aliases = {6: 0, 7: 1}
    return pl.pallas_call(
        functools.partial(attend_kernel, late, base),
        grid=(heads, steps),
        in_specs=in_specs,
        out_specs=[row, norm],
        out_shape=[
            jax.ShapeDtypeStruct((rows, local), BF),
            jax.ShapeDtypeStruct((heads, rows, 1), F32),
        ],
        scratch_shapes=scratch,
        input_output_aliases=aliases,
        cost_estimate=takes(10 if late else 20),
        name="attend_late" if late else "attend_early",
    )(*operands)


def rotate_back(grad, cos, sin):
    return grad * cos - pltpu.roll(grad, HD // 2, 1) * sin


def attend_back_kernel(
    q_ref, k_ref, v_ref, ke_ref, ve_ref, first_ref, lse_ref, do_ref, cos_ref, sin_ref,
    dq_ref, dk_ref, dv_ref, e_ref, keys, values, dkeys, dvalues,
):
    step = pl.program_id(1)
    block = q_ref.shape[0]
    scale = HD**-0.5

    @pl.when(step == 0)
    def _():
        keys[:HALO] = ke_ref[...]
        keys[HALO:] = k_ref[...]
        values[:HALO] = ve_ref[...]
        values[HALO:] = v_ref[...]
        dkeys[...] = jnp.zeros_like(dkeys)
        dvalues[...] = jnp.zeros_like(dvalues)

    window = pl.ds(pl.multiple_of(step * block, block), block + HALO)
    query, dout = q_ref[...], do_ref[...]
    raw = dot_last(query, keys[window, :]) * scale
    probs = jnp.where(allowed_keys(first_ref, step, block), jnp.exp(raw - lse_ref[...]), 0.0)
    dprob = dot_last(dout, values[window, :])
    delta = jnp.sum(probs * dprob, axis=-1, keepdims=True)
    dscore = (probs * (dprob - delta)).astype(BF)
    mine = pl.ds(pl.multiple_of(HALO + step * block, block), block)
    dquery = dot_plain(dscore, keys[window, :]) * scale
    dq_ref[...] = rotate_back(dquery, cos_ref[mine, :], sin_ref[mine, :]).astype(BF)
    dkeys[window, :] += dot_rows(dscore, query)
    dvalues[window, :] += dot_rows(probs.astype(BF), dout)

    @pl.when(step == pl.num_programs(1) - 1)
    def _():
        dkey = rotate_back(dkeys[...] * scale, cos_ref[...], sin_ref[...])
        e_ref[0] = dkey[:HALO].astype(BF)
        dk_ref[...] = dkey[HALO:]
        e_ref[1] = dvalues[:HALO].astype(BF)
        dv_ref[...] = dvalues[HALO:]


def attend_back(q, k, v, halo, first, lse, dout, cos_tab, sin_tab, block=256):
    rows, local = q.shape
    heads = local // HD
    span = block + HALO
    column = pl.BlockSpec((rows, HD), lambda h, i: (0, h))
    piece = pl.BlockSpec((block, HD), lambda h, i: (i, h))
    table = pl.BlockSpec((HALO + rows, HD), lambda h, i: (0, 0))
    edge = pl.BlockSpec((HALO, HD), lambda h, i: (0, h))
    return pl.pallas_call(
        attend_back_kernel,
        grid=(heads, rows // block),
        in_specs=[
            piece,
            column,
            column,
            edge,
            pl.BlockSpec((HALO, HD), lambda h, i: (0, h + heads)),
            pl.BlockSpec((block, 1), lambda h, i: (i, 0)),
            pl.BlockSpec((None, block, 1), lambda h, i: (h, i, 0)),
            piece,
            table,
            table,
        ],
        out_specs=[
            piece,
            column,
            column,
            pl.BlockSpec((2, HALO, HD), lambda h, i: (0, 0, (h + heads // 2) % heads)),
        ],
        out_shape=[
            jax.ShapeDtypeStruct((rows, local), BF),
            jax.ShapeDtypeStruct((rows, local), F32),
            jax.ShapeDtypeStruct((rows, local), F32),
            jax.ShapeDtypeStruct((2, HALO, local), BF),
        ],
        scratch_shapes=[pltpu.VMEM((HALO + rows, HD), BF)] * 2
        + [pltpu.VMEM((HALO + rows, HD), F32)] * 2,
        cost_estimate=takes(43),
        name="attend_back",
    )(q, k, v, halo, halo, first, lse, dout, cos_tab, sin_tab)


def ffn_kernel(first_half, seeded, shared_count, table, h_ref, g_ref, own_ref, oth_ref, *refs):
    count = 2 if not first_half else int(seeded)
    starts, refs = refs[:count], refs[count + shared_count :]
    back_ref, act_own, act_oth, d_own, d_oth, *outs, back, forth = refs
    step = pl.program_id(0)
    hidden, grad = h_ref[...], g_ref[...]
    size = own_ref.shape[1] // 3

    @pl.when(step == 0)
    def _():
        if first_half:
            outs[1][...] = hidden
            back[...] = jnp.zeros_like(back)
            forth[...] = starts[0][...] if seeded else jnp.zeros_like(forth)
        else:
            back[...] = starts[0][...]
            forth[...] = starts[1][...]

    for w_ref, act_ref, d_ref in ((own_ref, act_own, d_own), (oth_ref, act_oth, d_oth)):
        both = dot_plain(hidden, w_ref[:, : 2 * size])
        dact = dot_plain(grad, w_ref[:, 2 * size :]).astype(BF).astype(F32)
        gate, up = both[:, :size], both[:, size:]
        sig = jax.nn.sigmoid(gate)
        silu = gate * sig
        act = (silu * up).astype(BF)
        dgate = (dact * up * sig * (1.0 + gate * (1.0 - sig))).astype(BF)
        dup = (dact * silu).astype(BF)
        act_ref[...] = act
        d_ref[:, :size] = dgate
        d_ref[:, size:] = dup
        forth[...] += dot_last(act, w_ref[:, 2 * size :])
        back[...] += dot_last(d_ref[...], w_ref[:, : 2 * size])

    @pl.when(step == pl.num_programs(0) - 1)
    def _():
        back_ref[...] = back[...].astype(back_ref.dtype)
        if first_half:
            outs[0][...] = forth[...]
        else:
            for i, out_ref in enumerate(outs):
                cols = out_ref.shape[1]
                at = pl.multiple_of(table[1 + i] * cols, cols)
                out_ref[...] = forth[:, pl.ds(at, cols)].astype(BF)


def feed_forward(j, place, places, hidden, grad_rows, w_own, w_oth, half, size, starts, shared, kind):
    chunk, width = hidden.shape
    rows = grad_rows.shape[0]
    first_half = places is None
    steps = half // size
    fixed = pl.BlockSpec((chunk, width), lambda n, t: (0, 0))
    at_j = pl.BlockSpec((chunk, width), lambda n, t: (j, 0))
    weight = pl.BlockSpec((width, 3 * size), lambda n, t: (0, n))
    table = jnp.stack([jnp.asarray(p, jnp.int32) for p in [place] + list(places or [])])
    starts = [] if starts is None else list(starts)
    operands = [hidden, grad_rows, w_own, w_oth] + starts
    in_specs = [fixed, at_j, weight, weight] + [fixed] * len(starts)
    act = pl.BlockSpec((chunk, size), lambda n, t: (j, n))
    both = pl.BlockSpec((chunk, 2 * size), lambda n, t: (j, n))
    out_specs = [fixed, act, act, both, both]
    out_shape = (
        [jax.ShapeDtypeStruct((chunk, width), kind)]
        + [jax.ShapeDtypeStruct((rows, half), BF)] * 2
        + [jax.ShapeDtypeStruct((rows, 2 * half), BF)] * 2
    )
    shared_at = [1, 2, 3, 4]
    if first_half:
        out_specs += [fixed, at_j]
        out_shape += [
            jax.ShapeDtypeStruct((chunk, width), F32),
            jax.ShapeDtypeStruct((rows, width), BF),
        ]
        shared_at.append(6)
    else:
        cols = width // len(places)
        out_specs += [pl.BlockSpec((chunk, cols), lambda n, t: (t[0], 0))] * len(places)
        out_shape += [jax.ShapeDtypeStruct((rows, cols), BF)] * len(places)
        shared_at += [5 + i for i in range(len(places))]
    aliases = {}
    if shared is not None:
        aliases = {1 + len(operands) + i: at for i, at in enumerate(shared_at)}
        in_specs += [pl.BlockSpec(memory_space=pl.ANY)] * len(shared)
        operands += list(shared)
    out = pl.pallas_call(
        functools.partial(
            ffn_kernel, first_half, len(starts) == 1, 0 if shared is None else len(shared)
        ),
        grid_spec=pltpu.PrefetchScalarGridSpec(
            num_scalar_prefetch=1,
            grid=(steps,),
            in_specs=in_specs,
            out_specs=out_specs,
            scratch_shapes=[pltpu.VMEM((chunk, width), F32)] * 2,
        ),
        out_shape=out_shape,
        input_output_aliases=aliases,
        cost_estimate=takes(20),
        compiler_params=pltpu.CompilerParams(vmem_limit_bytes=60 << 20),
        name="feed_forward",
    )(table, *operands)
    sums = [out[0], out[5]] if first_half else out[0]
    return sums, [out[at] for at in shared_at]


def finish_kernel(dq, dk, dv, e_ref, d_own, d_oth, edges):
    step = pl.program_id(0)
    chunk, local = dq.shape
    lead = edges.shape[1] - e_ref.shape[1]

    @pl.when(step == 0)
    def _():
        edges[:, :lead] = jnp.zeros((2, lead, local), BF)
        edges[:, lead:] = e_ref[...]

    rows = pl.ds(pl.multiple_of(step * chunk, chunk), chunk)
    dkey = (dk[...] + edges[0, rows, :].astype(F32)).astype(BF)
    dvalue = (dv[...] + edges[1, rows, :].astype(F32)).astype(BF)
    cols = local // 2
    for ref, at in ((d_own, 0), (d_oth, cols)):
        ref[:, :cols] = dq[:, at : at + cols]
        ref[:, cols : 2 * cols] = dkey[:, at : at + cols]
        ref[:, 2 * cols :] = dvalue[:, at : at + cols]


def finish_attention(dq, dk, dv, edges, block=256):
    rows, local = dq.shape
    inner = 3 * local // 2
    row = lambda i: (i, 0)
    part = pl.BlockSpec((block, local), row)
    return pl.pallas_call(
        finish_kernel,
        grid=(rows // block,),
        in_specs=[part, part, part, pl.BlockSpec(edges.shape, lambda i: (0, 0, 0))],
        out_specs=[pl.BlockSpec((block, inner), row)] * 2,
        out_shape=[jax.ShapeDtypeStruct((rows, inner), BF)] * 2,
        scratch_shapes=[pltpu.VMEM((2, rows, local), BF)],
        cost_estimate=takes(4),
        name="finish_attention",
    )(dq, dk, dv, edges)


def input_kernel(table, d_own, d_oth, w_own, w_oth, x_ref, dx_ref, *outs):
    step = pl.program_id(0)
    grad = dot_last(d_own[...], w_own[...]) + dot_last(d_oth[...], w_oth[...])
    normed, inv_dev = normalize(x_ref[...].astype(F32))
    grad = norm_back(grad, normed, inv_dev)
    keep = jnp.where(step == table[0], 1.0, 0.0)
    grad = (grad + keep * dx_ref[...]).astype(BF)
    for i, out_ref in enumerate(outs):
        width = out_ref.shape[1]
        for t in range(len(outs)):

            @pl.when(table[1 + i] == t)
            def _():
                out_ref[...] = grad[:, t * width : (t + 1) * width]


def input_parts(rank, places, d_own, d_oth, w_own, w_oth, full_x, dx1):
    rows, width = full_x.shape
    chunk = dx1.shape[0]
    inner = w_own.shape[1]
    cols = width // len(places)
    row = lambda i, t: (i, 0)
    once = lambda i, t: (0, 0)
    return pl.pallas_call(
        input_kernel,
        grid_spec=pltpu.PrefetchScalarGridSpec(
            num_scalar_prefetch=1,
            grid=(rows // chunk,),
            in_specs=[
                pl.BlockSpec((chunk, inner), row),
                pl.BlockSpec((chunk, inner), row),
                pl.BlockSpec((width, inner), once),
                pl.BlockSpec((width, inner), once),
                pl.BlockSpec((chunk, width), row),
                pl.BlockSpec((chunk, width), once),
            ],
            out_specs=[pl.BlockSpec((chunk, cols), row)] * len(places),
        ),
        out_shape=[jax.ShapeDtypeStruct((rows, cols), BF)] * len(places),
        cost_estimate=takes(20),
        compiler_params=pltpu.CompilerParams(vmem_limit_bytes=60 << 20),
        name="input_parts",
    )(
        jnp.stack([jnp.asarray(p, jnp.int32) for p in [rank] + list(places)]),
        d_own, d_oth, w_own, w_oth, full_x, dx1,
    )


def shares_kernel(table, m_ref, w_own, w_oth, keep_ref, mine_ref, *refs):
    cols = w_own.shape[1]
    keep_ref[...] = m_ref[...]
    out = dot_last(m_ref[:, :cols], w_own[...]) + dot_last(m_ref[:, cols:], w_oth[...])
    for j, ref in enumerate((mine_ref,) + refs):

        @pl.when(pl.program_id(0) == j)
        def _():
            ref[...] = out.astype(ref.dtype)


def output_shares(mixed, w_own, w_oth, turned):
    rows, local = mixed.shape
    width, cols = w_own.shape
    ranks = len(turned)
    chunk = rows // ranks
    once = lambda j, t: (0, 0)
    return pl.pallas_call(
        shares_kernel,
        grid_spec=pltpu.PrefetchScalarGridSpec(
            num_scalar_prefetch=1,
            grid=(ranks,),
            in_specs=[
                pl.BlockSpec((chunk, local), lambda j, t: (t[j], 0)),
                pl.BlockSpec((width, cols), once),
                pl.BlockSpec((width, cols), once),
            ],
            out_specs=[pl.BlockSpec((chunk, local), lambda j, t: (j, 0))]
            + [pl.BlockSpec((chunk, width), once)] * ranks,
        ),
        out_shape=[
            jax.ShapeDtypeStruct((rows, local), BF),
            jax.ShapeDtypeStruct((chunk, width), F32),
        ]
        + [jax.ShapeDtypeStruct((chunk, width), BF)] * (ranks - 1),
        cost_estimate=takes(7),
        compiler_params=pltpu.CompilerParams(vmem_limit_bytes=60 << 20),
        name="output_shares",
    )(jnp.stack(turned).astype(jnp.int32), mixed, w_own, w_oth)


def dmixed_kernel(table, *refs):
    *chunks, w_own, w_oth, keep_ref, d_ref = refs
    cols = w_own.shape[1]
    for j in range(len(chunks)):

        @pl.when(pl.program_id(0) == j)
        def _():
            chunk = chunks[j][...]
            keep_ref[...] = chunk
            d_ref[:, :cols] = dot_plain(chunk, w_own[...]).astype(BF)
            d_ref[:, cols:] = dot_plain(chunk, w_oth[...]).astype(BF)


def dmixed(chunks, w_own, w_oth, turned):
    chunk, width = chunks[0].shape
    cols = w_own.shape[1]
    ranks = len(chunks)
    once = lambda j, t: (0, 0)
    return pl.pallas_call(
        dmixed_kernel,
        grid_spec=pltpu.PrefetchScalarGridSpec(
            num_scalar_prefetch=1,
            grid=(ranks,),
            in_specs=[pl.BlockSpec((chunk, width), once)] * ranks
            + [pl.BlockSpec((width, cols), once)] * 2,
            out_specs=[
                pl.BlockSpec((chunk, width), lambda j, t: (j, 0)),
                pl.BlockSpec((chunk, 2 * cols), lambda j, t: (t[j], 0)),
            ],
        ),
        out_shape=[
            jax.ShapeDtypeStruct((chunk * ranks, width), BF),
            jax.ShapeDtypeStruct((chunk * ranks, 2 * cols), BF),
        ],
        cost_estimate=takes(7),
        compiler_params=pltpu.CompilerParams(vmem_limit_bytes=60 << 20),
        name="dmixed",
    )(jnp.stack(turned).astype(jnp.int32), *chunks, w_own, w_oth)


def norm_kernel(table, x_ref, mine_ref, *refs):
    *others, resid_ref, h_ref = refs
    total = x_ref[...].astype(F32) + mine_ref[...]
    for ref in others:
        total = total + ref[...].astype(F32)
    resid_ref[...] = total
    h_ref[...] = normalize(total)[0].astype(BF)


def norm_chunk(rank, full_x, mine, others):
    chunk, width = mine.shape
    block = chunk // 3
    row = pl.BlockSpec((block, width), lambda i, t: (i, 0))
    return pl.pallas_call(
        norm_kernel,
        grid_spec=pltpu.PrefetchScalarGridSpec(
            num_scalar_prefetch=1,
            grid=(3,),
            in_specs=[pl.BlockSpec((block, width), lambda i, t: (t[0] * 3 + i, 0)), row]
            + [row] * len(others),
            out_specs=[row, row],
        ),
        out_shape=[
            jax.ShapeDtypeStruct((chunk, width), F32),
            jax.ShapeDtypeStruct((chunk, width), BF),
        ],
        cost_estimate=takes(4),
        name="norm_chunk",
    )(jnp.asarray(rank, jnp.int32).reshape(1), full_x, mine, *others)


def back_kernel(g_ref, resid_ref, mine_ref, *refs):
    *others, dx_ref, da_ref = refs
    total = mine_ref[...]
    for ref in others:
        total = total + ref[...].astype(F32)
    normed, inv_dev = normalize(resid_ref[...])
    dx = g_ref[...].astype(F32) + norm_back(total, normed, inv_dev)
    dx_ref[...] = dx
    da_ref[...] = dx.astype(BF)


def back_chunk(grad_rows, resid1, mine, others):
    chunk, width = mine.shape
    block = chunk // 3
    row = pl.BlockSpec((block, width), lambda i: (i, 0))
    return pl.pallas_call(
        back_kernel,
        grid=(3,),
        in_specs=[row] * (3 + len(others)),
        out_specs=[row, row],
        out_shape=[
            jax.ShapeDtypeStruct((chunk, width), F32),
            jax.ShapeDtypeStruct((chunk, width), BF),
        ],
        cost_estimate=takes(4),
        name="back_chunk",
    )(grad_rows, resid1, mine, *others)


def grads_kernel(count, *refs):
    *ins, out_ref = refs
    at = 0
    for left, right in zip(ins[:count], ins[count : 2 * count]):
        cols = right.shape[1]
        total = dot_rows(left[...], right[...])
        if len(ins) > 2 * count:
            total = total + ins[-1][:, at : at + cols].astype(F32)
        out_ref[:, at : at + cols] = total.astype(BF)
        at += cols


def grads(lefts, rights, other=None):
    rows, width = lefts[0].shape
    cols = sum(r.shape[1] for r in rights)
    block = 512
    in_specs = [pl.BlockSpec((rows, block), lambda m: (0, m))] * len(lefts)
    in_specs += [pl.BlockSpec(r.shape, lambda m: (0, 0)) for r in rights]
    out = pl.BlockSpec((block, cols), lambda m: (m, 0))
    operands = list(lefts) + list(rights)
    if other is not None:
        in_specs.append(out)
        operands.append(other)
    return pl.pallas_call(
        functools.partial(grads_kernel, len(lefts)),
        grid=(width // block,),
        in_specs=in_specs,
        out_specs=out,
        out_shape=jax.ShapeDtypeStruct((width, cols), BF),
        cost_estimate=takes(10),
        compiler_params=pltpu.CompilerParams(vmem_limit_bytes=60 << 20),
        name="grads",
    )(*operands)


def after(value, *others):
    return lax.optimization_barrier((value,) + others)[0]


class Plane:
    def __init__(self):
        self.nc, self.nt = lax.axis_size("ctx"), lax.axis_size("tp")
        assert self.nc == 2 and self.nt % 2 == 0
        self.hi = self.nt // self.nc
        self.ranks = self.nc * self.hi
        tp_place = lax.axis_index("tp")
        self.c = lax.axis_index("ctx")
        self.h, self.k = tp_place // self.nc, tp_place % self.nc
        self.r = self.c * self.hi + self.h

    def perm(self, move):
        pairs = []
        for c in range(self.nc):
            for h in range(self.hi):
                for k in range(self.nc):
                    c2, h2, k2 = move(c, h, k)
                    pairs.append((c * self.nt + h * self.nc + k, c2 * self.nt + h2 * self.nc + k2))
        return pairs

    def spread_rows(self, block):
        got = []
        for jh in range(self.hi):
            for jk in range(self.nc):
                move = lambda c, h, k: (k ^ jk, h ^ jh, c)
                place = (self.h ^ jh) * self.nc + (self.c ^ jk)
                got.append((place, lax.ppermute(block, PLANE, self.perm(move))))
        return got

    def block_places(self):
        return [
            (self.h ^ jh) * self.nc + (self.c ^ jk) for jh in range(self.hi) for jk in range(self.nc)
        ]

    def collect_blocks(self, pieces):
        moves = [
            lambda c, h, k, jh=jh, jk=jk: (k, h ^ jh, c ^ jk)
            for jh in range(self.hi)
            for jk in range(self.nc)
        ]
        return [lax.ppermute(p, PLANE, self.perm(m)) for p, m in zip(pieces, moves)]

    def swap(self, value, j):
        def move(c, h, k):
            rank = (c * self.hi + h) ^ j
            return rank // self.hi, rank % self.hi, k

        return lax.ppermute(value, PLANE, self.perm(move))

    def chunk_of(self, value, j):
        size = value.shape[0] // self.ranks
        return lax.dynamic_slice_in_dim(value, (self.r ^ j) * size, size, 0)

    def turn(self, value):
        return jnp.concatenate([self.chunk_of(value, j) for j in range(self.ranks)], axis=0)

    def gather(self, mine, use=None):
        use = use or (lambda j, chunk: chunk[:8, :128])
        out = [mine]
        if self.ranks != 4:
            out += [self.swap(mine, j) for j in range(1, self.ranks)]
            for j in range(self.ranks):
                use(j, out[j])
            return out
        near, far = self.swap(mine, 1), self.swap(mine, 2)
        near, far, _ = lax.optimization_barrier((near, far, use(0, mine)))
        half = mine.shape[0] // 2
        corner = [self.swap(near[:half], 2), self.swap(far[half:], 1)]
        use(1, near)
        last = use(2, far)
        corner = jnp.concatenate(lax.optimization_barrier((*corner, last))[:2], axis=0)
        use(3, corner)
        return [mine, near, far, corner]

    def pair(self, value):
        perm = [(t, t ^ 1) for t in range(self.nt)]
        return lax.ppermute(value, "tp", perm)


def body(
    tokens, cotangent, lengths, order, w_query, w_key, w_value, w_output, w_gate, w_up, w_down
):
    plane = Plane()
    rows = tokens.shape[0]
    nf, nc, nt, ranks = lax.axis_size("fsdp"), plane.nc, plane.nt, plane.ranks
    z = lax.axis_index("fsdp")
    chunk = rows // ranks
    head_cols = w_query.shape[1] // nc
    heads = head_cols // HD
    hidden_cols = w_gate.shape[1] // nc
    half = hidden_cols // 2
    size = min(256, half)

    def over_fsdp(shard):
        return lax.all_gather(shard, "fsdp", axis=0, tiled=True)

    fence = lambda *values: lax.optimization_barrier(values)
    turned = [plane.r ^ j for j in range(ranks)]

    qkv_own = over_fsdp(pack((w_query, w_key, w_value), plane.c, 0, head_cols, 1))
    places, got_x = zip(*plane.spread_rows(tokens))
    base = (z * nc + plane.k) * rows - HALO
    index = base + jnp.arange(HALO + rows, dtype=jnp.int32)
    starts = first_of(index, slots(lengths, order))
    within = index - starts
    first = (starts[HALO:] - base)[:, None]
    lane = jnp.arange(HD, dtype=jnp.int32)
    freq = jnp.exp((lane % (HD // 2)).astype(F32) * (-2.0 * math.log(10000.0) / HD))
    angle = within.astype(F32)[:, None] * freq[None, :]
    cos_tab = jnp.cos(angle)
    sin_tab = jnp.sin(angle) * jnp.where(lane < HD // 2, -1.0, 1.0)[None, :]
    qkv_own, cos_tab, sin_tab, first, *got_x = fence(qkv_own, cos_tab, sin_tab, first, *got_x)
    qkv_oth = plane.pair(qkv_own)
    w_output, cotangent = fence(w_output, cotangent, *got_x)[:2]
    wo_own = over_fsdp(pack((w_output,), plane.c, 0, head_cols, 1))
    _, got_g = zip(*plane.spread_rows(cotangent))

    full_x, hidden1, query, key, value, edge = project(
        got_x, places, qkv_own, qkv_oth, cos_tab, sin_tab, heads
    )
    onward = []
    for f in range(nf):
        for h in range(plane.hi):
            for k in range(nc):
                to = f * nc + k + 1
                if to < nf * nc:
                    onward.append((f * nt + h * nc + k, to // nc * nt + h * nc + to % nc))
    backward = [(b, a) for a, b in onward]
    halo = lax.ppermute(edge, ("fsdp", "tp"), onward)
    wo_oth = plane.pair(after(wo_own, edge))
    late = attend(query, key, value, None, first)
    halo, wo_own, wo_oth, *late = fence(halo, wo_own, wo_oth, *late)
    own0 = over_fsdp(
        pack(after((w_gate, w_up, w_down), halo), plane.c, 0, size, half // size)
    )
    mixed, lse = attend(query, key, value, halo, first, late)

    mixed_rows, mine, *shares = output_shares(mixed, wo_own, wo_oth, turned)
    sent = [plane.swap(shares[j - 1], j) for j in range(ranks - 1, 0, -1)]
    mine, *got_g = fence(mine, *got_g)
    grad_rows = join(got_g, places, turned)
    shard1 = pack(after((w_gate, w_up, w_down), mine), plane.c, half, size, half // size)
    own1 = over_fsdp(shard1)
    mine, grad_rows, *sent = fence(mine, grad_rows, *sent, shard1)[:-1]
    resid1, mine = norm_chunk(plane.r, full_x, mine, sent)
    oth0 = plane.pair(after(own0, mine))

    sums, shared = {}, None

    def first_half(j, piece):
        nonlocal shared
        sums[j], shared = feed_forward(
            j, turned[j], None, piece, grad_rows, own0, oth0, half, size,
            None if j else [resid1], shared, F32,
        )
        return sums[j][0]

    pieces = plane.gather(mine, first_half)
    act_own, act_oth, d_own, d_oth, hidden2 = shared

    def halves(lefts, rights_own, rights_oth):
        return grads(lefts, rights_own, plane.pair(grads(lefts, rights_oth)))

    def reduce_rows(total):
        return lax.psum_scatter(total, "fsdp", scatter_dimension=0, tiled=True)

    def exchange(mine):
        return lax.ppermute(mine, "ctx", [(0, 1), (1, 0)])

    def both_parts(mine, other):
        here = plane.c == 0
        return jnp.where(here, mine, other), jnp.where(here, other, mine)

    lefts = (grad_rows, hidden2)
    total0 = halves(lefts, (act_own, d_own), (act_oth, d_oth))
    share0 = reduce_rows(total0)

    oth1 = plane.pair(after(own1, act_own))
    own1, oth1 = fence(own1, oth1, total0)[:2]
    totals, sent, shared = {}, [], None
    for j in list(range(ranks - 1, 0, -1)) + [0]:
        totals[j], shared = feed_forward(
            j, turned[j], plane.block_places(), pieces[j], grad_rows, own1, oth1, half, size,
            sums[j], shared, BF if j else F32,
        )
        if j:
            sent.append(plane.swap(totals[j], j))
    act_own, act_oth, d_own, d_oth, *forth = shared
    total1 = halves(lefts, (act_own, d_own), (act_oth, d_oth))
    mine, *sent = fence(totals[0], *sent, total1)[:-1]
    dx1, da = back_chunk(grad_rows, resid1, mine, sent)
    share1 = reduce_rows(after(total1, da))

    da, dout = dmixed(plane.gather(da), wo_own, wo_oth, turned)
    dout, share0, *forth = fence(dout, share0, *forth)
    forth = plane.collect_blocks(forth)
    dquery, dkey, dvalue, edges = attend_back(
        query, key, value, halo, first, lse, dout, cos_tab, sin_tab
    )
    edges = lax.ppermute(edges, ("fsdp", "tp"), backward)
    da, *forth = fence(da, *forth, dquery)[:-1]
    others = [exchange(share) for share in fence(share0, share1, *forth)[:2]]
    total_out = halves(
        (da,), (mixed_rows[:, :head_cols],), (mixed_rows[:, head_cols:],)
    )
    share_out = reduce_rows(after(total_out, share0))
    edges = after(edges, total_out)
    d_own, d_oth = finish_attention(dquery, dkey, dvalue, edges)
    other_qkv = plane.pair(grads((hidden1,), (d_oth,)))
    layer_out = functools.reduce(jnp.add, [p.astype(F32) for p in forth]).astype(BF)
    other_qkv, layer_out, share_out, others[0] = fence(
        other_qkv, layer_out, share_out, others[0]
    )
    others.append(exchange(share_out))
    total_qkv = grads((hidden1,), (d_own,), other_qkv)
    share_qkv = reduce_rows(total_qkv)
    d_own, d_oth = fence(d_own, d_oth, total_qkv)[:2]
    parts = input_parts(
        plane.r, plane.block_places(), d_own, d_oth, qkv_own, qkv_oth, full_x, dx1
    )
    *parts, others[1], others[2] = fence(*parts, *others[1:])
    back = plane.collect_blocks(parts)

    done = [both_parts(share0, others[0]), both_parts(share1, others[1])]
    grad_down = jnp.concatenate([done[s][c][:, :half] for c in range(2) for s in range(2)], axis=1)
    grad_gate, grad_up = (
        jnp.concatenate(
            [
                done[s][c][:, half + (2 * n + which) * size : half + (2 * n + which + 1) * size]
                for c in range(2)
                for s in range(2)
                for n in range(half // size)
            ],
            axis=1,
        )
        for which in range(2)
    )
    grad_output = jnp.concatenate(both_parts(share_out, others[2]), axis=1)
    input_grad = functools.reduce(jnp.add, [p.astype(F32) for p in back]).astype(BF)
    qkv = both_parts(share_qkv, exchange(share_qkv))
    grad_query, grad_key, grad_value = (
        jnp.concatenate([p[:, i * head_cols : (i + 1) * head_cols] for p in qkv], axis=1)
        for i in range(3)
    )
    grads_out = (grad_query, grad_key, grad_value, grad_output, grad_gate, grad_up, grad_down)
    return (layer_out, input_grad) + tuple(g.astype(F32) for g in grads_out)


def solution(mesh):
    rows = P(("fsdp", "ctx"), "tp")
    weight = P("fsdp", "tp")
    return jax.shard_map(
        body,
        mesh=mesh,
        in_specs=(rows, rows, P(), P()) + (weight,) * 7,
        out_specs=(rows, rows) + (weight,) * 7,
        check_vma=False,
    )
```

time: 1290 us -> 992 us (0.77)
  Pallas kernels: 92.6 us -> 437 us
  matrix products: 304 us -> 0 us
  waiting for transfers between devices: 562 us -> 398 us
  starting transfers between devices: 182 us -> 74.6 us
  local copies, waits for them, and re-layouts: 69.7 us -> 22.4 us
  other arithmetic: 53.8 us -> 34.8 us
    pallas_call x2 -> x30, Pallas kernels: 49.8 us -> 393 us  [the longest x8 162 us: feed_forward(): pl.pallas_call(functools.partial(ffn_kernel, first_half, len(starts) == 1...]
    dot_general x29 -> x0, matrix products: 304 us -> none  [the longest x12 119 us: dot_last(): lax.dot_general(left, right, (((1,), (1,)), ((), ())), preferred_element_...]
    all_gather x4, waiting for transfers between devices: 127 us -> 0.04 us  [over_fsdp(): return lax.all_gather(shard, 'fsdp', axis=0, tiled=True)]
    ppermute x9 -> x8, starting transfers between devices: 81.3 us -> 3.63 us  [pair(): return lax.ppermute(value, 'tp', perm)]
    ppermute x18 -> x14, waiting for transfers between devices: 237 us -> 162 us  [swap(): return lax.ppermute(value, PLANE, self.perm(move))]
    ppermute x23 -> x20, starting transfers between devices: 74.2 us -> 47.2 us  [the longest x8 33.5 us: spread_rows(): got.append((place, lax.ppermute(block, PLANE, self.perm(move))))]
    reduce_scatter x5 -> x4, waiting for transfers between devices: 0.05 us -> 24.5 us  [reduce_rows(): return lax.psum_scatter(total, 'fsdp', scatter_dimension=0, tiled=True)]
    ppermute x9 -> x8, waiting for transfers between devices: 9.69 us -> 31.5 us  [pair(): return lax.ppermute(value, 'tp', perm)]
  transfers between devices with their start and end apart: 61 -> 52, of which waited for: 30 -> 29; matrix products, arithmetic and copies ran while one was open for 27% -> 5% of each run, Pallas kernels for 7% -> 43%
where the time goes in v2:
time: 992 us; the launch traced here: 981 us
  Pallas kernels  437 us (44%)
  waiting for transfers between devices  398 us (40%)
  starting transfers between devices  74.6 us (8%)
  other arithmetic  34.8 us (4%)
  local copies, waits for them, and re-layouts  22.4 us (2%)
  between operations  14.9 us (2%)
    ppermute x14, waiting for transfers between devices, swap(): return lax.ppermute(value, PLANE, self.perm(move))  162 us
    pallas_call x8, Pallas kernels, feed_forward(): pl.pallas_call(functools.partial(ffn_kernel, first_half, len(starts) == 1...  162 us
    pallas_call x8, Pallas kernels, grads(): pl.pallas_call(functools.partial(grads_kernel, len(lefts)), grid=(width /...  95 us
    ppermute x8, waiting for transfers between devices, collect_blocks(): return [lax.ppermute(p, PLANE, self.perm(m)) for p, m in zip(pieces, moves)]  80.7 us
    ppermute x8, waiting for transfers between devices, spread_rows(): got.append((place, lax.ppermute(block, PLANE, self.perm(move))))  75 us
    pallas_call x1, Pallas kernels, attend_back(): pl.pallas_call(attend_back_kernel, grid=(heads, rows // block), in_specs=...  43.4 us
    ppermute x8, starting transfers between devices, spread_rows(): got.append((place, lax.ppermute(block, PLANE, self.perm(move))))  33.5 us
    pallas_call x2, Pallas kernels, attend(): pl.pallas_call(functools.partial(attend_kernel, late, base), grid=(heads,...  31.8 us
  transfers between devices with their start and end apart: 52, of which 29 were waited for; matrix products, arithmetic and copies ran while one was open for 5% of the time, Pallas kernels for 43%

profile of v2, /device:TPU:0, one launch (start us, length us, event | category | flops | bytes accessed | tf_op | source)
XLA Modules:
  0.0 981.2 jit_solution(1775629121981141828)
XLA Ops:
  16.7 6.2 fusion
  22.9 23.1 %collective-permute-done.1.refs_1_ = bf16[1536,512]{1,0:T(8,128)(2,1)S(1)} collective-permute-done((bf16[1536,512]{1,0:T(8,128)(2,1)}, bf16[1536,512]{1,0:T(8,128)(2,1)S(1)}, u32[]{:S(2)}, u32[]{:S(2)}) %collective-permute-start.1) | collective-permute-done | bytes 1572896 | tf_op jit(solution)/shard_map/ppermute | solution.py:729
  46.0 36.9 %collective-permute-done.3.refs_3_ = bf16[1536,512]{1,0:T(8,128)(2,1)} collective-permute-done((bf16[1536,512]{1,0:T(8,128)(2,1)}, bf16[1536,512]{1,0:T(8,128)(2,1)}, u32[]{:S(2)}, u32[]{:S(2)}) %collective-permute-start.3) | collective-permute-done | bytes 1572896 | tf_op jit(solution)/shard_map/ppermute | solution.py:729
  92.7 21.2 %norm_project.1 = (bf16[1536,2048]{1,0:T(8,128)(2,1)}, bf16[1536,2048]{1,0:T(8,128)(2,1)}, bf16[1536,512]{1,0:T(8,128)(2,1)}, bf16[1536,512]{1,0:T(8,128)(2,1)},...) custom-call(s32[4]{0:T(128)} %pad_add_fusion.table, bf16[1536,512]{1,0:T(8,128)(2,1)} %copy-done.14, ...), custom_call_target="tpu_custom_call" | custom-call | flops 600000000 | bytes 1 | tf_op jit(solution)/shard_map/norm_project/pallas_call | solution.py:103
  118.8 10.8 %attend_late.1 = (bf16[1536,512]{1,0:T(8,128)(2,1)}, f32[4,1536,1]{2,1,0:T(8,128)}) custom-call(bf16[1536,512]{1,0:T(8,128)(2,1)} %get-tuple-element.188.q_ref, bf16[1536,512]{1,0:T(8,128)(2,1)} %get-tuple-element.189.k_ref, bf16[1536,512]{1,0:T(8,128)(2,1)} %get-tuple-element.190.v_ref, s32[1536,1]{1,0:T(8,128)} %copy.67.refs_0_.refs_2_.first_ref), custom_call_target="tpu_custom_call" | custom-call | flops 300000000 | bytes 1 | tf_op jit(solution)/shard_map/attend_late/pallas_call | solution.py:233
  135.5 11.8 %collective-permute-start.8 = (bf16[1536,512]{1,0:T(8,128)(2,1)}, bf16[1536,512]{1,0:T(8,128)(2,1)}, u32[]{:S(2)}, u32[]{:S(2)}) collective-permute-start(bf16[1536,512]{1,0:T(8,128)(2,1)} %param.12), channel_id=1, source_target_pairs={{0,4},{1,0},{2,6},{3,2},{4,5},{5,1},{6,7},{7,3},{8,12},{9,8},{10,1... | collective-permute-start | bytes 4718600 | tf_op jit(solution)/shard_map/ppermute | solution.py:729
  147.3 13.4 %collective-permute-start.7 = (bf16[1536,512]{1,0:T(8,128)(2,1)}, bf16[1536,512]{1,0:T(8,128)(2,1)}, u32[]{:S(2)}, u32[]{:S(2)}) collective-permute-start(bf16[1536,512]{1,0:T(8,128)(2,1)} %param.12), channel_id=1, source_target_pairs={{0,0},{1,4},{2,2},{3,6},{4,1},{5,5},{6,3},{7,7},{8,8},{9,12},{10,1... | collective-permute-start | bytes 4718600 | tf_op jit(solution)/shard_map/ppermute | solution.py:729
  160.7 20.9 %attend_early.1 = (bf16[1536,512]{1,0:T(8,128)(2,1)}, f32[4,1536,1]{2,1,0:T(8,128)}) custom-call(bf16[1536,512]{1,0:T(8,128)(2,1)} %get-tuple-element.188.q_ref, bf16[1536,512]{1,0:T(8,128)(2,1)} %get-tuple-element.189.k_ref, bf16[1536,512]{1,0:T(8,128)(2,1)} %get-tuple-element.190.v_ref, ...), custom_call_target="tpu_custom_call", output_to_operand_aliasing={{0}: (6, {}), {1}: (7, {})} | custom-call | flops 600000000 | bytes 1 | tf_op jit(solution)/shard_map/attend_early/pallas_call | solution.py:233
  181.7 10.6 %output_shares.1 = (bf16[1536,512]{1,0:T(8,128)(2,1)}, f32[384,2048]{1,0:T(8,128)}, bf16[384,2048]{1,0:T(8,128)(2,1)}, bf16[384,2048]{1,0:T(8,128)(2,1)}, bf16[384,2048]{1,0:T(8,128)(2,1)}) custom-call(s32[4]{0:T(128)} %pad_add_fusion.1.table, bf16[1536,512]{1,0:T(8,128)(2,1)} %get-tuple-element.201.m_ref, ...), custom_call_target="tpu_custom_call" | custom-call | flops 210000000 | bytes 1 | tf_op jit(solution)/shard_map/output_shares/pallas_call | solution.py:540
  192.3 12.8 %collective-permute-done.10.refs_3_ = bf16[1536,512]{1,0:T(8,128)(2,1)S(1)} collective-permute-done((bf16[1536,512]{1,0:T(8,128)(2,1)}, bf16[1536,512]{1,0:T(8,128)(2,1)S(1)}, u32[]{:S(2)}, u32[]{:S(2)}) %collective-permute-start.10) | collective-permute-done | bytes 1572896 | tf_op jit(solution)/shard_map/ppermute | solution.py:729
  205.1 7.3 collective-permute-start.12
  216.8 6.5 join.1.g_ref.refs_0_
  223.3 26.3 %collective-permute-done.11.refs_0_ = bf16[384,2048]{1,0:T(8,128)(2,1)} collective-permute-done((bf16[384,2048]{1,0:T(8,128)(2,1)}, bf16[384,2048]{1,0:T(8,128)(2,1)}, u32[]{:S(2)}, u32[]{:S(2)}) %collective-permute-start.11) | collective-permute-done | bytes 1572896 | tf_op jit(solution)/shard_map/ppermute | solution.py:750
  249.6 33.2 %collective-permute-done.12.refs_1_ = bf16[384,2048]{1,0:T(8,128)(2,1)} collective-permute-done((bf16[384,2048]{1,0:T(8,128)(2,1)}, bf16[384,2048]{1,0:T(8,128)(2,1)}, u32[]{:S(2)}, u32[]{:S(2)}) %collective-permute-start.12) | collective-permute-done | bytes 1572896 | tf_op jit(solution)/shard_map/ppermute | solution.py:750
  282.8 7.0 norm_chunk.1
  291.8 8.6 collective-permute-done.16.oth_ref
  300.4 20.8 %feed_forward.8 = (f32[384,2048]{1,0:T(8,128)}, bf16[1536,512]{1,0:T(8,128)(2,1)}, bf16[1536,512]{1,0:T(8,128)(2,1)}, bf16[1536,1024]{1,0:T(8,128)(2,1)}, bf16[1...) custom-call(s32[1]{0:T(128)} %bitcast.6.table, bf16[384,2048]{1,0:T(8,128)(2,1)} %get-tuple-element.224.h_ref, ...), custom_call_target="tpu_custom_call" | custom-call | flops 600000000 | bytes 1 | tf_op jit(solution)/shard_map/feed_forward/pallas_call | solution.py:417
  332.2 19.4 %feed_forward.9 = (f32[384,2048]{1,0:T(8,128)}, bf16[1536,512]{1,0:T(8,128)(2,1)}, bf16[1536,512]{1,0:T(8,128)(2,1)}, bf16[1536,1024]{1,0:T(8,128)(2,1)}, bf16[1...) custom-call(s32[1]{0:T(128)} %bitcast.7.table, ...), custom_call_target="tpu_custom_call", output_to_operand_aliasing={{1}: (5, {}), {2}: (6, {}), {3}: (7, {}), {4}: (8, {}), {6}... | custom-call | flops 600000000 | bytes 1 | tf_op jit(solution)/shard_map/feed_forward/pallas_call | solution.py:417
  351.6 19.9 %feed_forward.10 = (f32[384,2048]{1,0:T(8,128)}, bf16[1536,512]{1,0:T(8,128)(2,1)}, bf16[1536,512]{1,0:T(8,128)(2,1)}, bf16[1536,1024]{1,0:T(8,128)(2,1)}, bf16[...) custom-call(s32[1]{0:T(128)} %bitcast.8.table, ...), custom_call_target="tpu_custom_call", output_to_operand_aliasing={{1}: (5, {}), {2}: (6, {}), {3}: (7, {}), {4}: (8, {}), {6}... | custom-call | flops 600000000 | bytes 1 | tf_op jit(solution)/shard_map/feed_forward/pallas_call | solution.py:417
  375.1 19.2 %feed_forward.11 = (f32[384,2048]{1,0:T(8,128)}, bf16[1536,512]{1,0:T(8,128)(2,1)}, bf16[1536,512]{1,0:T(8,128)(2,1)}, bf16[1536,1024]{1,0:T(8,128)(2,1)}, bf16[...) custom-call(s32[1]{0:T(128)} %bitcast.9.table, ...), custom_call_target="tpu_custom_call", output_to_operand_aliasing={{1}: (5, {}), {2}: (6, {}), {3}: (7, {}), {4}: (8, {}), {6}... | custom-call | flops 600000000 | bytes 1 | tf_op jit(solution)/shard_map/feed_forward/pallas_call | solution.py:417
  394.3 15.3 %grads.8 = bf16[2048,1536]{1,0:T(8,128)(2,1)} custom-call(bf16[1536,2048]{1,0:T(8,128)(2,1)} %join.1.g_ref.refs_0_, bf16[1536,2048]{1,0:T(8,128)(2,1)} %get-tuple-element.252.refs_1_, bf16[1536,512]{1,0:T(8,128)(2,1)} %get-tuple-element.254.refs_2_, bf16[1536,1024]{1,0:T(8,128)(2,1)} %get-tuple-element.255.refs_3_), custom_call_target="tpu_custom_call" | custom-call | flops 300000000 | bytes 1 | tf_op jit(solution)/shard_map/grads/pallas_call | solution.py:687
  410.1 10.0 %collective-permute-done.20.refs_4_ = bf16[2048,1536]{1,0:T(8,128)(2,1)} collective-permute-done((bf16[2048,1536]{1,0:T(8,128)(2,1)}, bf16[2048,1536]{1,0:T(8,128)(2,1)}, u32[]{:S(2)}, u32[]{:S(2)}) %collective-permute-start.20) | collective-permute-done | bytes 6291488 | tf_op jit(solution)/shard_map/ppermute | solution.py:779
  420.1 16.4 %grads.9 = bf16[2048,1536]{1,0:T(8,128)(2,1)} custom-call(bf16[1536,2048]{1,0:T(8,128)(2,1)} %join.1.g_ref.refs_0_, bf16[1536,2048]{1,0:T(8,128)(2,1)} %get-tuple-element.252.refs_1_, bf16[1536,512]{1,0:T(8,128)(2,1)} %get-tuple-element.250.refs_2_, bf16[1536,1024]{1,0:T(8,128)(2,1)} %get-tuple-element.253.refs_3_, ...), custom_call_target="tpu_custom_call" | custom-call | flops 300000000 | bytes 1 | tf_op jit(solution)/shard_map/grads/pallas_call | solution.py:687
  439.1 21.2 %feed_forward.12 = (bf16[384,2048]{1,0:T(8,128)(2,1)}, bf16[1536,512]{1,0:T(8,128)(2,1)}, bf16[1536,512]{1,0:T(8,128)(2,1)}, bf16[1536,1024]{1,0:T(8,128)(2,1)},...) custom-call(s32[5]{0:T(128)} %stack.44.table, ...), custom_call_target="tpu_custom_call" | custom-call | flops 600000000 | bytes 1 | tf_op jit(solution)/shard_map/feed_forward/pallas_call | solution.py:417
  460.3 20.1 %feed_forward.13 = (bf16[384,2048]{1,0:T(8,128)(2,1)}, bf16[1536,512]{1,0:T(8,128)(2,1)}, bf16[1536,512]{1,0:T(8,128)(2,1)}, bf16[1536,1024]{1,0:T(8,128)(2,1)},...) custom-call(s32[5]{0:T(128)} %stack.43.table, ...), custom_call_target="tpu_custom_call", output_to_operand_aliasing={{1}: (7, {}), {2}: (8, {}), {3}: (9, {}), {4}: (10, {}), {5... | custom-call | flops 600000000 | bytes 1 | tf_op jit(solution)/shard_map/feed_forward/pallas_call | solution.py:417
  480.4 20.6 %feed_forward.14 = (bf16[384,2048]{1,0:T(8,128)(2,1)}, bf16[1536,512]{1,0:T(8,128)(2,1)}, bf16[1536,512]{1,0:T(8,128)(2,1)}, bf16[1536,1024]{1,0:T(8,128)(2,1)},...) custom-call(s32[5]{0:T(128)} %stack.42.table, ...), custom_call_target="tpu_custom_call", output_to_operand_aliasing={{1}: (7, {}), {2}: (8, {}), {3}: (9, {}), {4}: (10, {}), {5... | custom-call | flops 600000000 | bytes 1 | tf_op jit(solution)/shard_map/feed_forward/pallas_call | solution.py:417
  501.0 20.7 %feed_forward.15 = (f32[384,2048]{1,0:T(8,128)}, bf16[1536,512]{1,0:T(8,128)(2,1)}, bf16[1536,512]{1,0:T(8,128)(2,1)}, bf16[1536,1024]{1,0:T(8,128)(2,1)}, bf16[...) custom-call(s32[5]{0:T(128)} %stack.41.table, ...), custom_call_target="tpu_custom_call", output_to_operand_aliasing={{1}: (7, {}), {2}: (8, {}), {3}: (9, {}), {4}: (10, {}), {5... | custom-call | flops 600000000 | bytes 1 | tf_op jit(solution)/shard_map/feed_forward/pallas_call | solution.py:417
  521.8 15.3 %grads.10 = bf16[2048,1536]{1,0:T(8,128)(2,1)} custom-call(bf16[1536,2048]{1,0:T(8,128)(2,1)} %join.1.g_ref.refs_0_, bf16[1536,2048]{1,0:T(8,128)(2,1)} %get-tuple-element.252.refs_1_, bf16[1536,512]{1,0:T(8,128)(2,1)} %get-tuple-element.294.refs_2_, bf16[1536,1024]{1,0:T(8,128)(2,1)} %get-tuple-element.295.refs_3_), custom_call_target="tpu_custom_call" | custom-call | flops 300000000 | bytes 1 | tf_op jit(solution)/shard_map/grads/pallas_call | solution.py:687
  540.6 6.9 collective-permute-done.24.refs_4_
  547.6 16.4 %grads.11 = bf16[2048,1536]{1,0:T(8,128)(2,1)} custom-call(bf16[1536,2048]{1,0:T(8,128)(2,1)} %join.1.g_ref.refs_0_, bf16[1536,2048]{1,0:T(8,128)(2,1)} %get-tuple-element.252.refs_1_, bf16[1536,512]{1,0:T(8,128)(2,1)} %get-tuple-element.292.refs_2_, bf16[1536,1024]{1,0:T(8,128)(2,1)} %get-tuple-element.293.refs_3_, ...), custom_call_target="tpu_custom_call" | custom-call | flops 300000000 | bytes 1 | tf_op jit(solution)/shard_map/grads/pallas_call | solution.py:687
  563.9 10.2 %collective-permute-done.23.refs_2_ = bf16[384,2048]{1,0:T(8,128)(2,1)S(1)} collective-permute-done((bf16[384,2048]{1,0:T(8,128)(2,1)}, bf16[384,2048]{1,0:T(8,128)(2,1)S(1)}, u32[]{:S(2)}, u32[]{:S(2)}) %collective-permute-start.23) | collective-permute-done | bytes 1572896 | tf_op jit(solution)/shard_map/ppermute | solution.py:750
  575.4 33.7 %collective-permute-done.21.refs_0_ = bf16[384,2048]{1,0:T(8,128)(2,1)} collective-permute-done((bf16[384,2048]{1,0:T(8,128)(2,1)}, bf16[384,2048]{1,0:T(8,128)(2,1)}, u32[]{:S(2)}, u32[]{:S(2)}) %collective-permute-start.21) | collective-permute-done | bytes 1572896 | tf_op jit(solution)/shard_map/ppermute | solution.py:750
  609.1 8.4 back_chunk.1
  620.0 34.5 %collective-permute-done.26.refs_2_ = bf16[384,2048]{1,0:T(8,128)(2,1)S(1)} collective-permute-done((bf16[384,2048]{1,0:T(8,128)(2,1)S(1)}, bf16[384,2048]{1,0:T(8,128)(2,1)S(1)}, u32[]{:S(2)}, u32[]{:S(2)}) %collective-permute-start.26) | collective-permute-done | bytes 1572896 | tf_op jit(solution)/shard_map/ppermute | solution.py:750
  658.2 15.9 %collective-permute-done.28 = bf16[192,2048]{1,0:T(8,128)(2,1)S(1)} collective-permute-done((bf16[192,2048]{1,0:T(8,128)(2,1)S(1)}, bf16[192,2048]{1,0:T(8,128)(2,1)S(1)}, u32[]{:S(2)}, u32[]{:S(2)}) %collective-permute-start.28) | collective-permute-done | bytes 786464 | tf_op jit(solution)/shard_map/ppermute | solution.py:750
  676.0 10.0 %dmixed.1 = (bf16[1536,2048]{1,0:T(8,128)(2,1)}, bf16[1536,512]{1,0:T(8,128)(2,1)}) custom-call(s32[4]{0:T(128)} %pad_add_fusion.1.table, bf16[384,2048]{1,0:T(8,128)(2,1)} %get-tuple-element.300.refs_0_, bf16[384,2048]{1,0:T(8,128)(2,1)} %copy-done.9, bf16[384,2048]{1,0:T(8,128)(2,1)} %copy-done.8, bf16[384,2048]{1,0:T(8,128)(2,1)} %pad_maximum_fusion.refs_3_, ...), custom_call_target="tpu_custom_call" | custom-call | flops 210000000 | bytes 1 | tf_op jit(solution)/shard_map/dmixed/pallas_call | solution.py:582
  690.9 43.4 %attend_back.1 = (bf16[1536,512]{1,0:T(8,128)(2,1)}, f32[1536,512]{1,0:T(8,128)}, f32[1536,512]{1,0:T(8,128)}, bf16[2,1024,512]{2,1,0:T(8,128)(2,1)}) custom-call(bf16[1536,512]{1,0:T(8,128)(2,1)} %get-tuple-element.188.q_ref, bf16[1536,512]{1,0:T(8,128)(2,1)} %get-tuple-element.189.k_ref, bf16[1536,512]{1,0:T(8,128)(2,1)} %get-tuple-element.190.v_ref, ...), custom_call_target="tpu_custom_call" | custom-call | flops 1290000000 | bytes 1 | tf_op jit(solution)/shard_map/attend_back/pallas_call | solution.py:300
  738.2 20.8 %collective-permute-done.33 = bf16[1536,512]{1,0:T(8,128)(2,1)} collective-permute-done((bf16[1536,512]{1,0:T(8,128)(2,1)}, bf16[1536,512]{1,0:T(8,128)(2,1)}, u32[]{:S(2)}, u32[]{:S(2)}) %collective-permute-start.33) | collective-permute-done | bytes 1572896 | tf_op jit(solution)/shard_map/ppermute | solution.py:743
  769.6 6.5 grads.13
  776.1 7.8 finish_attention.1
  783.9 9.1 grads.14
  798.3 21.9 %reduce-scatter.7.cloned.1.call-done = bf16[512,256]{1,0:T(8,128)(2,1)} async-done(((bf16[2048,256]{1,0:T(8,128)(2,1)}), bf16[512,256]{1,0:T(8,128)(2,1)}) %reduce-scatter.7.cloned.1.call-update) | async-done | bytes 262160 | tf_op jit(solution)/shard_map/reduce_scatter | solution.py:867
  820.3 10.0 %collective-permute-done.36 = bf16[512,1536]{1,0:T(8,128)(2,1)} collective-permute-done((bf16[512,1536]{1,0:T(8,128)(2,1)}, bf16[512,1536]{1,0:T(8,128)(2,1)}, u32[]{:S(2)}, u32[]{:S(2)}) %collective-permute-start.36) | collective-permute-done | bytes 1572896 | tf_op jit(solution)/shard_map/ppermute | solution.py:870
  830.3 10.2 %grads.15 = bf16[2048,768]{1,0:T(8,128)(2,1)} custom-call(bf16[1536,2048]{1,0:T(8,128)(2,1)} %get-tuple-element.187.refs_0_, bf16[1536,768]{1,0:T(8,128)(2,1)} %get-tuple-element.335.refs_1_.d_own, bf16[2048,768]{1,0:T(8,128)(2,1)} %copy-done.10), custom_call_target="tpu_custom_call" | custom-call | flops 300000000 | bytes 1 | tf_op jit(solution)/shard_map/grads/pallas_call | solution.py:687
  845.5 23.5 %input_parts.1 = (bf16[1536,512]{1,0:T(8,128)(2,1)}, bf16[1536,512]{1,0:T(8,128)(2,1)}, bf16[1536,512]{1,0:T(8,128)(2,1)}, bf16[1536,512]{1,0:T(8,128)(2,1)}) custom-call(s32[5]{0:T(128)} %stack.41.table, bf16[1536,768]{1,0:T(8,128)(2,1)} %get-tuple-element.335.refs_1_.d_own, bf16[1536,768]{1,0:T(8,128)(2,1)} %get-tuple-element.336.refs_1_.d_oth, ...), custom_call_target="tpu_custom_call" | custom-call | flops 600000000 | bytes 1 | tf_op jit(solution)/shard_map/input_parts/pallas_call | solution.py:498
  871.4 6.8 collective-permute-done.37
  903.0 25.5 %collective-permute-done.40 = bf16[1536,512]{1,0:T(8,128)(2,1)} collective-permute-done((bf16[1536,512]{1,0:T(8,128)(2,1)}, bf16[1536,512]{1,0:T(8,128)(2,1)}, u32[]{:S(2)}, u32[]{:S(2)}) %collective-permute-start.40) | collective-permute-done | bytes 1572896 | tf_op jit(solution)/shard_map/ppermute | solution.py:743
  928.6 34.4 %collective-permute-done.42 = bf16[1536,512]{1,0:T(8,128)(2,1)} collective-permute-done((bf16[1536,512]{1,0:T(8,128)(2,1)}, bf16[1536,512]{1,0:T(8,128)(2,1)}, u32[]{:S(2)}, u32[]{:S(2)}) %collective-permute-start.42) | collective-permute-done | bytes 1572896 | tf_op jit(solution)/shard_map/ppermute | solution.py:743
  (201 shorter events, 134.9 us)
Async XLA Ops:
  7.2 77.9 %all-gather.5.cloned.1.call-start = ((), (), s32[]{:S(2)}) async-start(), calls=%async_computation.4 | async-start | bytes 3932160 | tf_op jit(solution)/shard_map/all_gather | solution.py:797
  9.3 106.8 %all-gather.7.cloned.1.call-start = ((), (), s32[]{:S(2)}) async-start(), calls=%async_computation.5 | async-start | bytes 1310720 | tf_op jit(solution)/shard_map/all_gather | solution.py:797
  9.4 36.7 %collective-permute-start.1 = (bf16[1536,512]{1,0:T(8,128)(2,1)}, bf16[1536,512]{1,0:T(8,128)(2,1)S(1)}, u32[]{:S(2)}, u32[]{:S(2)}) collective-permute-start(bf16[1536,512]{1,0:T(8,128)(2,1)} %param.11), channel_id=1, source_target_pairs={{0,4},{1,0},{2,6},{3,2},{4,5},{5,1},{6,7},{7,3},{8,12},{9,8},{10,1... | collective-permute-start | bytes 4718600 | tf_op jit(solution)/shard_map/ppermute | solution.py:729
  12.3 33.7 %collective-permute-start = (bf16[1536,512]{1,0:T(8,128)(2,1)}, bf16[1536,512]{1,0:T(8,128)(2,1)S(1)}, u32[]{:S(2)}, u32[]{:S(2)}) collective-permute-start(bf16[1536,512]{1,0:T(8,128)(2,1)} %param.11), channel_id=1, source_target_pairs={{0,0},{1,4},{2,2},{3,6},{4,1},{5,5},{6,3},{7,7},{8,8},{9,12},{10,1... | collective-permute-start | bytes 4718600 | tf_op jit(solution)/shard_map/ppermute | solution.py:729
  14.4 68.6 %collective-permute-start.3 = (bf16[1536,512]{1,0:T(8,128)(2,1)}, bf16[1536,512]{1,0:T(8,128)(2,1)}, u32[]{:S(2)}, u32[]{:S(2)}) collective-permute-start(bf16[1536,512]{1,0:T(8,128)(2,1)} %param.11), channel_id=1, source_target_pairs={{0,6},{1,2},{2,4},{3,0},{4,7},{5,3},{6,5},{7,1},{8,14},{9,10},{10,... | collective-permute-start | bytes 4718600 | tf_op jit(solution)/shard_map/ppermute | solution.py:729
  15.9 69.2 %collective-permute-start.2 = (bf16[1536,512]{1,0:T(8,128)(2,1)}, bf16[1536,512]{1,0:T(8,128)(2,1)}, u32[]{:S(2)}, u32[]{:S(2)}) collective-permute-start(bf16[1536,512]{1,0:T(8,128)(2,1)} %param.11), channel_id=1, source_target_pairs={{0,2},{1,6},{2,0},{3,4},{4,3},{5,7},{6,1},{7,5},{8,10},{9,14},{10,... | collective-permute-start | bytes 4718600 | tf_op jit(solution)/shard_map/ppermute | solution.py:729
  86.9 203.0 %all-gather.11.cloned.1.call-start = ((), (), s32[]{:S(2)}) async-start(), calls=%async_computation.7 | async-start | bytes 7864320 | tf_op jit(solution)/shard_map/all_gather | solution.py:797
  113.9 15.8 %collective-permute-start.5 = (bf16[1024,1024]{1,0:T(8,128)(2,1)}, bf16[1024,1024]{1,0:T(8,128)(2,1)S(1)}, u32[]{:S(2)}, u32[]{:S(2)}) collective-permute-start(bf16[1024,1024]{1,0:T(8,128)(2,1)} %get-tuple-element.191), channel_id=1, source_target_pairs={{0,1},{1,8},{2,3},{3,10},{8,9},{9,16},{10,11},{11,18},{16,17},{17,... | collective-permute-start | bytes 6291464 | tf_op jit(solution)/shard_map/ppermute | solution.py:831
  116.1 13.5 %collective-permute-start.6 = (bf16[2048,256]{1,0:T(8,128)(2,1)}, bf16[2048,256]{1,0:T(8,128)(2,1)S(1)}, u32[]{:S(2)}, u32[]{:S(2)}) collective-permute-start(bf16[2048,256]{1,0:T(8,128)(2,1)} %all-gather.7.cloned.1.call-done.w_own.refs_4_), channel_id=1, source_target_pairs={{0,1},{1,0},{2,3},{3,2},{4,5},{5,4},{6,7},{7,6},{8,9},{9,8},{10,11... | collective-permute-start | bytes 3145736 | tf_op jit(solution)/shard_map/ppermute | solution.py:779
  133.2 276.4 %all-gather.9.cloned.1.call-start = ((), (), s32[]{:S(2)}) async-start(), calls=%async_computation.6 | async-start | bytes 7864320 | tf_op jit(solution)/shard_map/all_gather | solution.py:797
  133.2 71.8 %collective-permute-start.10 = (bf16[1536,512]{1,0:T(8,128)(2,1)}, bf16[1536,512]{1,0:T(8,128)(2,1)S(1)}, u32[]{:S(2)}, u32[]{:S(2)}) collective-permute-start(bf16[1536,512]{1,0:T(8,128)(2,1)} %param.12), channel_id=1, source_target_pairs={{0,6},{1,2},{2,4},{3,0},{4,7},{5,3},{6,5},{7,1},{8,14},{9,10},{10,... | collective-permute-start | bytes 4718600 | tf_op jit(solution)/shard_map/ppermute | solution.py:729
  133.9 78.5 %collective-permute-start.9 = (bf16[1536,512]{1,0:T(8,128)(2,1)}, bf16[1536,512]{1,0:T(8,128)(2,1)S(1)}, u32[]{:S(2)}, u32[]{:S(2)}) collective-permute-start(bf16[1536,512]{1,0:T(8,128)(2,1)} %param.12), channel_id=1, source_target_pairs={{0,2},{1,6},{2,0},{3,4},{4,3},{5,7},{6,1},{7,5},{8,10},{9,14},{10,... | collective-permute-start | bytes 4718600 | tf_op jit(solution)/shard_map/ppermute | solution.py:729
  135.5 78.9 %collective-permute-start.8 = (bf16[1536,512]{1,0:T(8,128)(2,1)}, bf16[1536,512]{1,0:T(8,128)(2,1)}, u32[]{:S(2)}, u32[]{:S(2)}) collective-permute-start(bf16[1536,512]{1,0:T(8,128)(2,1)} %param.12), channel_id=1, source_target_pairs={{0,4},{1,0},{2,6},{3,2},{4,5},{5,1},{6,7},{7,3},{8,12},{9,8},{10,1... | collective-permute-start | bytes 4718600 | tf_op jit(solution)/shard_map/ppermute | solution.py:729
  147.3 67.1 %collective-permute-start.7 = (bf16[1536,512]{1,0:T(8,128)(2,1)}, bf16[1536,512]{1,0:T(8,128)(2,1)}, u32[]{:S(2)}, u32[]{:S(2)}) collective-permute-start(bf16[1536,512]{1,0:T(8,128)(2,1)} %param.12), channel_id=1, source_target_pairs={{0,0},{1,4},{2,2},{3,6},{4,1},{5,5},{6,3},{7,7},{8,8},{9,12},{10,1... | collective-permute-start | bytes 4718600 | tf_op jit(solution)/shard_map/ppermute | solution.py:729
  192.3 57.4 %collective-permute-start.11 = (bf16[384,2048]{1,0:T(8,128)(2,1)}, bf16[384,2048]{1,0:T(8,128)(2,1)}, u32[]{:S(2)}, u32[]{:S(2)}) collective-permute-start(bf16[384,2048]{1,0:T(8,128)(2,1)} %get-tuple-element.211), channel_id=1, source_target_pairs={{0,6},{1,7},{2,4},{3,5},{4,2},{5,3},{6,0},{7,1},{8,14},{9,15},{10,... | collective-permute-start | bytes 4718600 | tf_op jit(solution)/shard_map/ppermute | solution.py:750
  205.1 77.8 %collective-permute-start.12 = (bf16[384,2048]{1,0:T(8,128)(2,1)}, bf16[384,2048]{1,0:T(8,128)(2,1)}, u32[]{:S(2)}, u32[]{:S(2)}) collective-permute-start(bf16[384,2048]{1,0:T(8,128)(2,1)} %get-tuple-element.212), channel_id=1, source_target_pairs={{0,4},{1,5},{2,6},{3,7},{4,0},{5,1},{6,2},{7,3},{8,12},{9,13},{10,... | collective-permute-start | bytes 4718600 | tf_op jit(solution)/shard_map/ppermute | solution.py:750
  212.4 70.4 %collective-permute-start.13 = (bf16[384,2048]{1,0:T(8,128)(2,1)}, bf16[384,2048]{1,0:T(8,128)(2,1)}, u32[]{:S(2)}, u32[]{:S(2)}) collective-permute-start(bf16[384,2048]{1,0:T(8,128)(2,1)} %get-tuple-element.213), channel_id=1, source_target_pairs={{0,2},{1,3},{2,0},{3,1},{4,6},{5,7},{6,4},{7,5},{8,10},{9,11},{10,... | collective-permute-start | bytes 4718600 | tf_op jit(solution)/shard_map/ppermute | solution.py:750
  289.9 10.5 %collective-permute-start.16 = (bf16[2048,1536]{1,0:T(8,128)(2,1)}, bf16[2048,1536]{1,0:T(8,128)(2,1)}, u32[]{:S(2)}, u32[]{:S(2)}) collective-permute-start(bf16[2048,1536]{1,0:T(8,128)(2,1)} %all-gather.11.cloned.1.call-done.own_ref), channel_id=1, source_target_pairs={{0,1},{1,0},{2,3},{3,2},{4,5},{5,4},{6,7},{7,6},{8,9},{9,8},{10,11... | collective-permute-start | bytes 18874376 | tf_op jit(solution)/shard_map/ppermute | solution.py:779
  289.9 396.0 %reduce-scatter.5.cloned.1.call-start = ((), (), s32[]{:S(2)}) async-start(), calls=%async_computation.8 | async-start | bytes 7864320 | tf_op jit(solution)/shard_map/reduce_scatter | solution.py:867
  290.1 37.1 %collective-permute-start.15 = (bf16[384,2048]{1,0:T(8,128)(2,1)}, bf16[384,2048]{1,0:T(8,128)(2,1)S(1)}, u32[]{:S(2)}, u32[]{:S(2)}) collective-permute-start(bf16[384,2048]{1,0:T(8,128)(2,1)} %get-tuple-element.224.h_ref), channel_id=1, source_target_pairs={{0,4},{1,5},{2,6},{3,7},{4,0},{5,1},{6,2},{7,3},{8,12},{9,13},{10,... | collective-permute-start | bytes 4718600 | tf_op jit(solution)/shard_map/ppermute | solution.py:750
  290.2 37.1 %collective-permute-start.14 = (bf16[384,2048]{1,0:T(8,128)(2,1)}, bf16[384,2048]{1,0:T(8,128)(2,1)S(1)}, u32[]{:S(2)}, u32[]{:S(2)}) collective-permute-start(bf16[384,2048]{1,0:T(8,128)(2,1)} %get-tuple-element.224.h_ref), channel_id=1, source_target_pairs={{0,2},{1,3},{2,0},{3,1},{4,6},{5,7},{6,4},{7,5},{8,10},{9,11},{10,... | collective-permute-start | bytes 4718600 | tf_op jit(solution)/shard_map/ppermute | solution.py:750
  329.4 42.2 %collective-permute-start.18 = (bf16[192,2048]{1,0:T(8,128)(2,1)}, bf16[192,2048]{1,0:T(8,128)(2,1)}, u32[]{:S(2)}, u32[]{:S(2)}) collective-permute-start(bf16[192,2048]{1,0:T(8,128)(2,1)} %slice.103), channel_id=1, source_target_pairs={{0,2},{1,3},{2,0},{3,1},{4,6},{5,7},{6,4},{7,5},{8,10},{9,11},{10,... | collective-permute-start | bytes 2359304 | tf_op jit(solution)/shard_map/ppermute | solution.py:750
  330.7 40.8 %collective-permute-start.17 = (bf16[192,2048]{1,0:T(8,128)(2,1)}, bf16[192,2048]{1,0:T(8,128)(2,1)}, u32[]{:S(2)}, u32[]{:S(2)}) collective-permute-start(bf16[192,2048]{1,0:T(8,128)(2,1)} %slice.102), channel_id=1, source_target_pairs={{0,4},{1,5},{2,6},{3,7},{4,0},{5,1},{6,2},{7,3},{8,12},{9,13},{10,... | collective-permute-start | bytes 2359304 | tf_op jit(solution)/shard_map/ppermute | solution.py:750
  409.6 29.5 %collective-permute-start.19 = (bf16[2048,1536]{1,0:T(8,128)(2,1)}, bf16[2048,1536]{1,0:T(8,128)(2,1)}, u32[]{:S(2)}, u32[]{:S(2)}) collective-permute-start(bf16[2048,1536]{1,0:T(8,128)(2,1)} %all-gather.9.cloned.1.call-done.own_ref), channel_id=1, source_target_pairs={{0,1},{1,0},{2,3},{3,2},{4,5},{5,4},{6,7},{7,6},{8,9},{9,8},{10,11... | collective-permute-start | bytes 18874376 | tf_op jit(solution)/shard_map/ppermute | solution.py:779
  436.5 357.0 %reduce-scatter.9.cloned.1.call-start = ((), (), s32[]{:S(2)}) async-start(), calls=%async_computation.10 | async-start | bytes 7864320 | tf_op jit(solution)/shard_map/reduce_scatter | solution.py:867
  537.2 36.9 %collective-permute-start.23 = (bf16[384,2048]{1,0:T(8,128)(2,1)}, bf16[384,2048]{1,0:T(8,128)(2,1)S(1)}, u32[]{:S(2)}, u32[]{:S(2)}) collective-permute-start(bf16[384,2048]{1,0:T(8,128)(2,1)} %get-tuple-element.291), channel_id=1, source_target_pairs={{0,2},{1,3},{2,0},{3,1},{4,6},{5,7},{6,4},{7,5},{8,10},{9,11},{10,... | collective-permute-start | bytes 4718600 | tf_op jit(solution)/shard_map/ppermute | solution.py:750
  538.0 37.4 %collective-permute-start.22 = (bf16[384,2048]{1,0:T(8,128)(2,1)}, bf16[384,2048]{1,0:T(8,128)(2,1)S(1)}, u32[]{:S(2)}, u32[]{:S(2)}) collective-permute-start(bf16[384,2048]{1,0:T(8,128)(2,1)} %get-tuple-element.290), channel_id=1, source_target_pairs={{0,4},{1,5},{2,6},{3,7},{4,0},{5,1},{6,2},{7,3},{8,12},{9,13},{10,... | collective-permute-start | bytes 4718600 | tf_op jit(solution)/shard_map/ppermute | solution.py:750
  538.1 71.0 %collective-permute-start.21 = (bf16[384,2048]{1,0:T(8,128)(2,1)}, bf16[384,2048]{1,0:T(8,128)(2,1)}, u32[]{:S(2)}, u32[]{:S(2)}) collective-permute-start(bf16[384,2048]{1,0:T(8,128)(2,1)} %get-tuple-element.289), channel_id=1, source_target_pairs={{0,6},{1,7},{2,4},{3,5},{4,2},{5,3},{6,0},{7,1},{8,14},{9,15},{10,... | collective-permute-start | bytes 4718600 | tf_op jit(solution)/shard_map/ppermute | solution.py:750
  617.5 202.8 %reduce-scatter.7.cloned.1.call-start = ((), (), s32[]{:S(2)}) async-start(), calls=%async_computation.9 | async-start | bytes 1310720 | tf_op jit(solution)/shard_map/reduce_scatter | solution.py:867
  618.9 35.6 %collective-permute-start.26 = (bf16[384,2048]{1,0:T(8,128)(2,1)S(1)}, bf16[384,2048]{1,0:T(8,128)(2,1)S(1)}, u32[]{:S(2)}, u32[]{:S(2)}) collective-permute-start(bf16[384,2048]{1,0:T(8,128)(2,1)S(1)} %copy-done.17), channel_id=1, source_target_pairs={{0,4},{1,5},{2,6},{3,7},{4,0},{5,1},{6,2},{7,3},{8,12},{9,13},{10,... | collective-permute-start | bytes 4718600 | tf_op jit(solution)/shard_map/ppermute | solution.py:750
  619.6 35.4 %collective-permute-start.25 = (bf16[384,2048]{1,0:T(8,128)(2,1)S(1)}, bf16[384,2048]{1,0:T(8,128)(2,1)S(1)}, u32[]{:S(2)}, u32[]{:S(2)}) collective-permute-start(bf16[384,2048]{1,0:T(8,128)(2,1)S(1)} %copy-done.17), channel_id=1, source_target_pairs={{0,2},{1,3},{2,0},{3,1},{4,6},{5,7},{6,4},{7,5},{8,10},{9,11},{10,... | collective-permute-start | bytes 4718600 | tf_op jit(solution)/shard_map/ppermute | solution.py:750
  656.2 17.9 %collective-permute-start.28 = (bf16[192,2048]{1,0:T(8,128)(2,1)S(1)}, bf16[192,2048]{1,0:T(8,128)(2,1)S(1)}, u32[]{:S(2)}, u32[]{:S(2)}) collective-permute-start(bf16[192,2048]{1,0:T(8,128)(2,1)S(1)} %slice.105), channel_id=1, source_target_pairs={{0,2},{1,3},{2,0},{3,1},{4,6},{5,7},{6,4},{7,5},{8,10},{9,11},{10,... | collective-permute-start | bytes 2359304 | tf_op jit(solution)/shard_map/ppermute | solution.py:750
  657.0 17.7 %collective-permute-start.27 = (bf16[192,2048]{1,0:T(8,128)(2,1)S(1)}, bf16[192,2048]{1,0:T(8,128)(2,1)S(1)}, u32[]{:S(2)}, u32[]{:S(2)}) collective-permute-start(bf16[192,2048]{1,0:T(8,128)(2,1)S(1)} %slice.104), channel_id=1, source_target_pairs={{0,4},{1,5},{2,6},{3,7},{4,0},{5,1},{6,2},{7,3},{8,12},{9,13},{10,... | collective-permute-start | bytes 2359304 | tf_op jit(solution)/shard_map/ppermute | solution.py:750
  685.9 52.3 %collective-permute-start.30 = (bf16[1536,512]{1,0:T(8,128)(2,1)S(1)}, bf16[1536,512]{1,0:T(8,128)(2,1)}, u32[]{:S(2)}, u32[]{:S(2)}) collective-permute-start(bf16[1536,512]{1,0:T(8,128)(2,1)S(1)} %copy-done.1), channel_id=1, source_target_pairs={{0,0},{1,4},{2,2},{3,6},{4,1},{5,5},{6,3},{7,7},{8,8},{9,12},{10,1... | collective-permute-start | bytes 4718600 | tf_op jit(solution)/shard_map/ppermute | solution.py:743
  687.7 50.5 %collective-permute-start.31 = (bf16[1536,512]{1,0:T(8,128)(2,1)S(1)}, bf16[1536,512]{1,0:T(8,128)(2,1)}, u32[]{:S(2)}, u32[]{:S(2)}) collective-permute-start(bf16[1536,512]{1,0:T(8,128)(2,1)S(1)} %copy-done.2), channel_id=1, source_target_pairs={{0,1},{1,5},{2,3},{3,7},{4,0},{5,4},{6,2},{7,6},{8,9},{9,13},{10,1... | collective-permute-start | bytes 4718600 | tf_op jit(solution)/shard_map/ppermute | solution.py:743
  689.0 49.2 %collective-permute-start.32 = (bf16[1536,512]{1,0:T(8,128)(2,1)}, bf16[1536,512]{1,0:T(8,128)(2,1)}, u32[]{:S(2)}, u32[]{:S(2)}) collective-permute-start(bf16[1536,512]{1,0:T(8,128)(2,1)} %get-tuple-element.318), channel_id=1, source_target_pairs={{0,2},{1,6},{2,0},{3,4},{4,3},{5,7},{6,1},{7,5},{8,10},{9,14},{10,... | collective-permute-start | bytes 4718600 | tf_op jit(solution)/shard_map/ppermute | solution.py:743
  690.2 68.8 %collective-permute-start.33 = (bf16[1536,512]{1,0:T(8,128)(2,1)}, bf16[1536,512]{1,0:T(8,128)(2,1)}, u32[]{:S(2)}, u32[]{:S(2)}) collective-permute-start(bf16[1536,512]{1,0:T(8,128)(2,1)} %get-tuple-element.319), channel_id=1, source_target_pairs={{0,3},{1,7},{2,1},{3,5},{4,2},{5,6},{6,0},{7,4},{8,11},{9,15},{10,... | collective-permute-start | bytes 4718600 | tf_op jit(solution)/shard_map/ppermute | solution.py:743
  734.3 41.8 %collective-permute-start.29 = (bf16[2,1024,512]{2,1,0:T(8,128)(2,1)}, bf16[2,1024,512]{2,1,0:T(8,128)(2,1)}, u32[]{:S(2)}, u32[]{:S(2)}) collective-permute-start(bf16[2,1024,512]{2,1,0:T(8,128)(2,1)} %get-tuple-element.314), channel_id=1, source_target_pairs={{1,0},{8,1},{3,2},{10,3},{9,8},{16,9},{11,10},{18,11},{17,16},{24,... | collective-permute-start | bytes 6291464 | tf_op jit(solution)/shard_map/ppermute | solution.py:902
  793.0 27.3 %collective-permute-start.35 = (bf16[2048,768]{1,0:T(8,128)(2,1)}, bf16[2048,768]{1,0:T(8,128)(2,1)S(1)}, u32[]{:S(2)}, u32[]{:S(2)}) collective-permute-start(bf16[2048,768]{1,0:T(8,128)(2,1)} %grads.14), channel_id=1, source_target_pairs={{0,1},{1,0},{2,3},{3,2},{4,5},{5,4},{6,7},{7,6},{8,9},{9,8},{10,11... | collective-permute-start | bytes 9437192 | tf_op jit(solution)/shard_map/ppermute | solution.py:779
  793.4 107.1 %reduce-scatter.11.cloned.1.call-start = ((), (), s32[]{:S(2)}) async-start(), calls=%async_computation.11 | async-start | bytes 3932160 | tf_op jit(solution)/shard_map/reduce_scatter | solution.py:867
  793.4 36.8 %collective-permute-start.36 = (bf16[512,1536]{1,0:T(8,128)(2,1)}, bf16[512,1536]{1,0:T(8,128)(2,1)}, u32[]{:S(2)}, u32[]{:S(2)}) collective-permute-start(bf16[512,1536]{1,0:T(8,128)(2,1)} %reduce-scatter.5.cloned.1.call-done), channel_id=1, source_target_pairs={{0,4},{4,0},{1,5},{5,1},{2,6},{6,2},{3,7},{7,3},{8,12},{12,8},{9,1... | collective-permute-start | bytes 4718600 | tf_op jit(solution)/shard_map/ppermute | solution.py:870
  840.5 37.7 %collective-permute-start.37 = (bf16[512,1536]{1,0:T(8,128)(2,1)}, bf16[512,1536]{1,0:T(8,128)(2,1)}, u32[]{:S(2)}, u32[]{:S(2)}) collective-permute-start(bf16[512,1536]{1,0:T(8,128)(2,1)} %reduce-scatter.9.cloned.1.call-done), channel_id=1, source_target_pairs={{0,4},{4,0},{1,5},{5,1},{2,6},{6,2},{3,7},{7,3},{8,12},{12,8},{9,1... | collective-permute-start | bytes 4718600 | tf_op jit(solution)/shard_map/ppermute | solution.py:870
  841.4 40.6 %collective-permute-start.38 = (bf16[512,256]{1,0:T(8,128)(2,1)S(1)}, bf16[512,256]{1,0:T(8,128)(2,1)S(1)}, u32[]{:S(2)}, u32[]{:S(2)}) collective-permute-start(bf16[512,256]{1,0:T(8,128)(2,1)S(1)} %copy-done.22), channel_id=1, source_target_pairs={{0,4},{4,0},{1,5},{5,1},{2,6},{6,2},{3,7},{7,3},{8,12},{12,8},{9,1... | collective-permute-start | bytes 786440 | tf_op jit(solution)/shard_map/ppermute | solution.py:870
  882.0 21.1 %collective-permute-start.39 = (bf16[1536,512]{1,0:T(8,128)(2,1)}, bf16[1536,512]{1,0:T(8,128)(2,1)S(1)}, u32[]{:S(2)}, u32[]{:S(2)}) collective-permute-start(bf16[1536,512]{1,0:T(8,128)(2,1)} %get-tuple-element.344), channel_id=1, source_target_pairs={{0,0},{1,4},{2,2},{3,6},{4,1},{5,5},{6,3},{7,7},{8,8},{9,12},{10,1... | collective-permute-start | bytes 4718600 | tf_op jit(solution)/shard_map/ppermute | solution.py:743
  884.1 44.4 %collective-permute-start.40 = (bf16[1536,512]{1,0:T(8,128)(2,1)}, bf16[1536,512]{1,0:T(8,128)(2,1)}, u32[]{:S(2)}, u32[]{:S(2)}) collective-permute-start(bf16[1536,512]{1,0:T(8,128)(2,1)} %get-tuple-element.345), channel_id=1, source_target_pairs={{0,1},{1,5},{2,3},{3,7},{4,0},{5,4},{6,2},{7,6},{8,9},{9,13},{10,1... | collective-permute-start | bytes 4718600 | tf_op jit(solution)/shard_map/ppermute | solution.py:743
  884.7 43.8 %collective-permute-start.41 = (bf16[1536,512]{1,0:T(8,128)(2,1)}, bf16[1536,512]{1,0:T(8,128)(2,1)}, u32[]{:S(2)}, u32[]{:S(2)}) collective-permute-start(bf16[1536,512]{1,0:T(8,128)(2,1)} %get-tuple-element.346), channel_id=1, source_target_pairs={{0,2},{1,6},{2,0},{3,4},{4,3},{5,7},{6,1},{7,5},{8,10},{9,14},{10,... | collective-permute-start | bytes 4718600 | tf_op jit(solution)/shard_map/ppermute | solution.py:743
  885.9 77.0 %collective-permute-start.42 = (bf16[1536,512]{1,0:T(8,128)(2,1)}, bf16[1536,512]{1,0:T(8,128)(2,1)}, u32[]{:S(2)}, u32[]{:S(2)}) collective-permute-start(bf16[1536,512]{1,0:T(8,128)(2,1)} %get-tuple-element.347), channel_id=1, source_target_pairs={{0,3},{1,7},{2,1},{3,5},{4,2},{5,6},{6,0},{7,4},{8,11},{9,15},{10,... | collective-permute-start | bytes 4718600 | tf_op jit(solution)/shard_map/ppermute | solution.py:743
  900.5 70.1 %collective-permute-start.43 = (bf16[512,768]{1,0:T(8,128)(2,1)}, bf16[512,768]{1,0:T(8,128)(2,1)S(1)}, u32[]{:S(2)}, u32[]{:S(2)}) collective-permute-start(bf16[512,768]{1,0:T(8,128)(2,1)} %reduce-scatter.11.cloned.1.call-done), channel_id=1, source_target_pairs={{0,4},{4,0},{1,5},{5,1},{2,6},{6,2},{3,7},{7,3},{8,12},{12,8},{9,1... | collective-permute-start | bytes 2359304 | tf_op jit(solution)/shard_map/ppermute | solution.py:870
  (29 other events, 364.6 us)
Sparse Core Ops, SparseCore 0:
  10.2 66.2 all-gather.4
  87.0 28.3 all-gather.6
  133.3 127.0 all-gather.10
  290.0 115.8 all-gather.8
  436.6 110.6 reduce-scatter.4
  617.6 110.6 reduce-scatter.8
  793.5 26.7 reduce-scatter.6
  840.6 59.8 reduce-scatter.10

commit v3 on v2

--- a/solution.py
+++ b/solution.py
@@ -114,6 +114,7 @@
         + [jax.ShapeDtypeStruct((rows, local), BF)] * 3
         + [jax.ShapeDtypeStruct((HALO, 2 * local), BF)],
         cost_estimate=takes(20),
+        compiler_params=pltpu.CompilerParams(vmem_limit_bytes=60 << 20),
         name="norm_project",
     )(jnp.stack([jnp.asarray(p, jnp.int32) for p in places]), *pieces, w_own, w_oth, cos_tab, sin_tab)
 
@@ -141,6 +142,7 @@
         ),
         out_shape=jax.ShapeDtypeStruct((rows, cols * count), pieces[0].dtype),
         cost_estimate=takes(5),
+        compiler_params=pltpu.CompilerParams(vmem_limit_bytes=60 << 20),
         name="join",
     )(table, *pieces)
 
@@ -168,19 +170,32 @@
         ),
         out_shape=jax.ShapeDtypeStruct((rows, size * len(weights) * steps), weights[0].dtype),
         cost_estimate=takes(2),
+        compiler_params=pltpu.CompilerParams(vmem_limit_bytes=60 << 20),
         name="pack",
     )(table, *weights)
 
 
-def allowed_keys(first_ref, step, block):
-    span = block + HALO
+def allowed_keys(first_ref, step, block, span):
     keys = lax.broadcasted_iota(jnp.int32, (block, span), 1)
     rows = lax.broadcasted_iota(jnp.int32, (block, span), 0)
-    first = first_ref[...] - step * block
-    return (keys >= first) & (keys <= rows + HALO)
-
-
-def attend_kernel(late, base, q_ref, k_ref, v_ref, *refs):
+    skip = block + HALO - span
+    first = first_ref[...] - (step * block + skip)
+    return (keys >= first) & (keys <= rows + (HALO - skip))
+
+
+def spans_of(first, block):
+    steps = first.shape[0] // block
+    lowest = jnp.min(first.reshape(steps, block), axis=1)
+    own = jnp.arange(steps, dtype=jnp.int32) + HALO // block
+    return own - lowest // block + 1
+
+
+def by_span(need, block, body):
+    for count in range(1, HALO // block + 2):
+        pl.when(need == count)(functools.partial(body, count * block))
+
+
+def attend_kernel(late, base, need, q_ref, k_ref, v_ref, *refs):
     if late:
         first_ref, o_ref, lse_ref = refs
     else:
@@ -188,8 +203,7 @@
     step = pl.program_id(1) + base
     block = q_ref.shape[0]
     if late:
-        window = pl.ds(pl.multiple_of(step * block - HALO, block), block + HALO)
-        key, value = k_ref[window, :], v_ref[window, :]
+        keys, values = k_ref, v_ref
     else:
 
         @pl.when(pl.program_id(1) == 0)
@@ -199,16 +213,19 @@
             values[:HALO] = ve_ref[...]
             values[HALO:] = v_ref[...]
 
-        window = pl.ds(pl.multiple_of(step * block, block), block + HALO)
-        key, value = keys[window, :], values[window, :]
-    raw = dot_last(q_ref[...], key) * (HD**-0.5)
-    raw = jnp.where(allowed_keys(first_ref, step, block), raw, NEG_FILL)
-    top = jnp.max(raw, axis=-1, keepdims=True)
-    expo = jnp.exp(raw - top)
-    denom = jnp.sum(expo, axis=-1, keepdims=True)
-    probs = (expo * (1.0 / denom)).astype(BF)
-    o_ref[...] = dot_plain(probs, value).astype(BF)
-    lse_ref[...] = top + jnp.log(denom)
+    def body(span):
+        at = (step + 1) * block + (0 if late else HALO) - span
+        window = pl.ds(pl.multiple_of(at, block), span)
+        raw = dot_last(q_ref[...], keys[window, :]) * (HD**-0.5)
+        raw = jnp.where(allowed_keys(first_ref, step, block, span), raw, NEG_FILL)
+        top = jnp.max(raw, axis=-1, keepdims=True)
+        expo = jnp.exp(raw - top)
+        denom = jnp.sum(expo, axis=-1, keepdims=True)
+        probs = (expo * (1.0 / denom)).astype(BF)
+        o_ref[...] = dot_plain(probs, values[window, :]).astype(BF)
+        lse_ref[...] = top + jnp.log(denom)
+
+    by_span(need[step], block, body)
 
 
 def attend(q, k, v, halo, first, done=None, block=256):
@@ -217,33 +234,37 @@
     late = halo is None
     base = HALO // block if late else 0
     steps = rows // block - base if late else HALO // block
-    row = pl.BlockSpec((block, HD), lambda h, i: (base + i, h))
-    column = pl.BlockSpec((rows, HD), lambda h, i: (0, h))
-    bound = pl.BlockSpec((block, 1), lambda h, i: (base + i, 0))
-    norm = pl.BlockSpec((None, block, 1), lambda h, i: (h, base + i, 0))
+    row = pl.BlockSpec((block, HD), lambda h, i, t: (base + i, h))
+    column = pl.BlockSpec((rows, HD), lambda h, i, t: (0, h))
+    bound = pl.BlockSpec((block, 1), lambda h, i, t: (base + i, 0))
+    norm = pl.BlockSpec((None, block, 1), lambda h, i, t: (h, base + i, 0))
     if late:
         in_specs, operands, scratch, aliases = [row, column, column, bound], (q, k, v, first), [], {}
     else:
-        edge = [pl.BlockSpec((HALO, HD), lambda h, i, at=at: (0, h + at)) for at in (0, heads)]
+        edge = [pl.BlockSpec((HALO, HD), lambda h, i, t, at=at: (0, h + at)) for at in (0, heads)]
         whole = pl.BlockSpec(memory_space=pl.ANY)
         in_specs = [row, column, column] + edge + [bound, whole, whole]
         operands = (q, k, v, halo, halo, first) + tuple(done)
         scratch = [pltpu.VMEM((HALO + rows, HD), BF)] * 2
-        aliases = {6: 0, 7: 1}
+        aliases = {7: 0, 8: 1}
     return pl.pallas_call(
         functools.partial(attend_kernel, late, base),
-        grid=(heads, steps),
-        in_specs=in_specs,
-        out_specs=[row, norm],
+        grid_spec=pltpu.PrefetchScalarGridSpec(
+            num_scalar_prefetch=1,
+            grid=(heads, steps),
+            in_specs=in_specs,
+            out_specs=[row, norm],
+            scratch_shapes=scratch,
+        ),
         out_shape=[
             jax.ShapeDtypeStruct((rows, local), BF),
             jax.ShapeDtypeStruct((heads, rows, 1), F32),
         ],
-        scratch_shapes=scratch,
         input_output_aliases=aliases,
         cost_estimate=takes(10 if late else 20),
+        compiler_params=pltpu.CompilerParams(vmem_limit_bytes=60 << 20),
         name="attend_late" if late else "attend_early",
-    )(*operands)
+    )(spans_of(first[:, 0], block), *operands)
 
 
 def rotate_back(grad, cos, sin):
@@ -251,7 +272,7 @@
 
 
 def attend_back_kernel(
-    q_ref, k_ref, v_ref, ke_ref, ve_ref, first_ref, lse_ref, do_ref, cos_ref, sin_ref,
+    need, q_ref, k_ref, v_ref, ke_ref, ve_ref, first_ref, lse_ref, do_ref, cos_ref, sin_ref,
     dq_ref, dk_ref, dv_ref, e_ref, keys, values, dkeys, dvalues,
 ):
     step = pl.program_id(1)
@@ -267,18 +288,22 @@
         dkeys[...] = jnp.zeros_like(dkeys)
         dvalues[...] = jnp.zeros_like(dvalues)
 
-    window = pl.ds(pl.multiple_of(step * block, block), block + HALO)
-    query, dout = q_ref[...], do_ref[...]
-    raw = dot_last(query, keys[window, :]) * scale
-    probs = jnp.where(allowed_keys(first_ref, step, block), jnp.exp(raw - lse_ref[...]), 0.0)
-    dprob = dot_last(dout, values[window, :])
-    delta = jnp.sum(probs * dprob, axis=-1, keepdims=True)
-    dscore = (probs * (dprob - delta)).astype(BF)
-    mine = pl.ds(pl.multiple_of(HALO + step * block, block), block)
-    dquery = dot_plain(dscore, keys[window, :]) * scale
-    dq_ref[...] = rotate_back(dquery, cos_ref[mine, :], sin_ref[mine, :]).astype(BF)
-    dkeys[window, :] += dot_rows(dscore, query)
-    dvalues[window, :] += dot_rows(probs.astype(BF), dout)
+    def body(span):
+        window = pl.ds(pl.multiple_of((step + 1) * block + HALO - span, block), span)
+        query, dout = q_ref[...], do_ref[...]
+        raw = dot_last(query, keys[window, :]) * scale
+        allowed = allowed_keys(first_ref, step, block, span)
+        probs = jnp.where(allowed, jnp.exp(raw - lse_ref[...]), 0.0)
+        dprob = dot_last(dout, values[window, :])
+        delta = jnp.sum(probs * dprob, axis=-1, keepdims=True)
+        dscore = (probs * (dprob - delta)).astype(BF)
+        mine = pl.ds(pl.multiple_of(HALO + step * block, block), block)
+        dquery = dot_plain(dscore, keys[window, :]) * scale
+        dq_ref[...] = rotate_back(dquery, cos_ref[mine, :], sin_ref[mine, :]).astype(BF)
+        dkeys[window, :] += dot_rows(dscore, query)
+        dvalues[window, :] += dot_rows(probs.astype(BF), dout)
+
+    by_span(need[step], block, body)
 
     @pl.when(step == pl.num_programs(1) - 1)
     def _():
@@ -293,61 +318,66 @@
     rows, local = q.shape
     heads = local // HD
     span = block + HALO
-    column = pl.BlockSpec((rows, HD), lambda h, i: (0, h))
-    piece = pl.BlockSpec((block, HD), lambda h, i: (i, h))
-    table = pl.BlockSpec((HALO + rows, HD), lambda h, i: (0, 0))
-    edge = pl.BlockSpec((HALO, HD), lambda h, i: (0, h))
+    column = pl.BlockSpec((rows, HD), lambda h, i, t: (0, h))
+    piece = pl.BlockSpec((block, HD), lambda h, i, t: (i, h))
+    table = pl.BlockSpec((HALO + rows, HD), lambda h, i, t: (0, 0))
+    edge = pl.BlockSpec((HALO, HD), lambda h, i, t: (0, h))
     return pl.pallas_call(
         attend_back_kernel,
-        grid=(heads, rows // block),
-        in_specs=[
-            piece,
-            column,
-            column,
-            edge,
-            pl.BlockSpec((HALO, HD), lambda h, i: (0, h + heads)),
-            pl.BlockSpec((block, 1), lambda h, i: (i, 0)),
-            pl.BlockSpec((None, block, 1), lambda h, i: (h, i, 0)),
-            piece,
-            table,
-            table,
-        ],
-        out_specs=[
-            piece,
-            column,
-            column,
-            pl.BlockSpec((2, HALO, HD), lambda h, i: (0, 0, (h + heads // 2) % heads)),
-        ],
+        grid_spec=pltpu.PrefetchScalarGridSpec(
+            num_scalar_prefetch=1,
+            grid=(heads, rows // block),
+            in_specs=[
+                piece,
+                column,
+                column,
+                edge,
+                pl.BlockSpec((HALO, HD), lambda h, i, t: (0, h + heads)),
+                pl.BlockSpec((block, 1), lambda h, i, t: (i, 0)),
+                pl.BlockSpec((None, block, 1), lambda h, i, t: (h, i, 0)),
+                piece,
+                table,
+                table,
+            ],
+            out_specs=[
+                piece,
+                column,
+                column,
+                pl.BlockSpec((2, HALO, HD), lambda h, i, t: (0, 0, (h + heads // 2) % heads)),
+            ],
+            scratch_shapes=[pltpu.VMEM((HALO + rows, HD), BF)] * 2
+            + [pltpu.VMEM((HALO + rows, HD), F32)] * 2,
+        ),
         out_shape=[
             jax.ShapeDtypeStruct((rows, local), BF),
             jax.ShapeDtypeStruct((rows, local), F32),
             jax.ShapeDtypeStruct((rows, local), F32),
             jax.ShapeDtypeStruct((2, HALO, local), BF),
         ],
-        scratch_shapes=[pltpu.VMEM((HALO + rows, HD), BF)] * 2
-        + [pltpu.VMEM((HALO + rows, HD), F32)] * 2,
         cost_estimate=takes(43),
+        compiler_params=pltpu.CompilerParams(vmem_limit_bytes=60 << 20),
         name="attend_back",
-    )(q, k, v, halo, halo, first, lse, dout, cos_tab, sin_tab)
-
-
-def ffn_kernel(first_half, seeded, shared_count, table, h_ref, g_ref, own_ref, oth_ref, *refs):
+    )(spans_of(first[:, 0], block), q, k, v, halo, halo, first, lse, dout, cos_tab, sin_tab)
+
+
+def ffn_kernel(first_half, seeded, shared_count, steps, table, h_ref, g_ref, own_ref, oth_ref, *refs):
     count = 2 if not first_half else int(seeded)
     starts, refs = refs[:count], refs[count + shared_count :]
-    back_ref, act_own, act_oth, d_own, d_oth, *outs, back, forth = refs
+    back_ref, act_own, act_oth, d_own, d_oth, *refs = refs
+    if first_half:
+        forth_ref, keep_ref = refs
+        back, forth = back_ref, forth_ref
+    else:
+        *outs, back, forth = refs
     step = pl.program_id(0)
     hidden, grad = h_ref[...], g_ref[...]
     size = own_ref.shape[1] // 3
 
-    @pl.when(step == 0)
-    def _():
-        if first_half:
-            outs[1][...] = hidden
-            back[...] = jnp.zeros_like(back)
-            forth[...] = starts[0][...] if seeded else jnp.zeros_like(forth)
-        else:
-            back[...] = starts[0][...]
-            forth[...] = starts[1][...]
+    if first_half:
+
+        @pl.when(step == 0)
+        def _():
+            keep_ref[...] = hidden
 
     for w_ref, act_ref, d_ref in ((own_ref, act_own, d_own), (oth_ref, act_oth, d_oth)):
         both = dot_plain(hidden, w_ref[:, : 2 * size])
@@ -355,25 +385,53 @@
         gate, up = both[:, :size], both[:, size:]
         sig = jax.nn.sigmoid(gate)
         silu = gate * sig
-        act = (silu * up).astype(BF)
-        dgate = (dact * up * sig * (1.0 + gate * (1.0 - sig))).astype(BF)
-        dup = (dact * silu).astype(BF)
-        act_ref[...] = act
-        d_ref[:, :size] = dgate
-        d_ref[:, size:] = dup
-        forth[...] += dot_last(act, w_ref[:, 2 * size :])
-        back[...] += dot_last(d_ref[...], w_ref[:, : 2 * size])
-
-    @pl.when(step == pl.num_programs(0) - 1)
-    def _():
-        back_ref[...] = back[...].astype(back_ref.dtype)
-        if first_half:
-            outs[0][...] = forth[...]
-        else:
+        act_ref[...] = (silu * up).astype(BF)
+        d_ref[:, :size] = (dact * up * sig * (1.0 + gate * (1.0 - sig))).astype(BF)
+        d_ref[:, size:] = (dact * silu).astype(BF)
+
+    def add(first, last):
+        tile = back_ref.shape[1] // 4
+        for at in range(0, 4 * tile, tile):
+            cols = slice(at, at + tile)
+            more = dot_last(act_own[...], own_ref[cols, 2 * size :])
+            more += dot_last(act_oth[...], oth_ref[cols, 2 * size :])
+            grad = dot_last(d_own[...], own_ref[cols, : 2 * size])
+            grad += dot_last(d_oth[...], oth_ref[cols, : 2 * size])
+            if not first:
+                more += forth[:, cols]
+                grad += back[:, cols]
+            elif not first_half:
+                more += starts[1][:, cols]
+                grad += starts[0][:, cols]
+            elif seeded:
+                more += starts[0][:, cols]
+            if first_half or not last:
+                forth[:, cols] = more
+                back[:, cols] = grad
+                continue
+            back_ref[:, cols] = grad.astype(back_ref.dtype)
+            if steps == 1 or len(outs) != 4:
+                forth[:, cols] = more
+                continue
+            for i, out_ref in enumerate(outs):
+
+                @pl.when(table[1 + i] == at // tile)
+                def _():
+                    out_ref[...] = more.astype(BF)
+
+        if last and not first_half and (steps == 1 or len(outs) != 4):
             for i, out_ref in enumerate(outs):
                 cols = out_ref.shape[1]
                 at = pl.multiple_of(table[1 + i] * cols, cols)
                 out_ref[...] = forth[:, pl.ds(at, cols)].astype(BF)
+
+    if steps == 1:
+        add(True, True)
+    else:
+        pl.when(step == 0)(lambda: add(True, False))
+        if steps > 2:
+            pl.when((step > 0) & (step < steps - 1))(lambda: add(False, False))
+        pl.when(step == steps - 1)(lambda: add(False, True))
 
 
 def feed_forward(j, place, places, hidden, grad_rows, w_own, w_oth, half, size, starts, shared, kind):
@@ -416,14 +474,14 @@
         operands += list(shared)
     out = pl.pallas_call(
         functools.partial(
-            ffn_kernel, first_half, len(starts) == 1, 0 if shared is None else len(shared)
+            ffn_kernel, first_half, len(starts) == 1, 0 if shared is None else len(shared), steps
         ),
         grid_spec=pltpu.PrefetchScalarGridSpec(
             num_scalar_prefetch=1,
             grid=(steps,),
             in_specs=in_specs,
             out_specs=out_specs,
-            scratch_shapes=[pltpu.VMEM((chunk, width), F32)] * 2,
+            scratch_shapes=[] if first_half else [pltpu.VMEM((chunk, width), F32)] * 2,
         ),
         out_shape=out_shape,
         input_output_aliases=aliases,
@@ -468,6 +526,7 @@
         out_shape=[jax.ShapeDtypeStruct((rows, inner), BF)] * 2,
         scratch_shapes=[pltpu.VMEM((2, rows, local), BF)],
         cost_estimate=takes(4),
+        compiler_params=pltpu.CompilerParams(vmem_limit_bytes=60 << 20),
         name="finish_attention",
     )(dq, dk, dv, edges)
 
@@ -628,6 +687,7 @@
             jax.ShapeDtypeStruct((chunk, width), BF),
         ],
         cost_estimate=takes(4),
+        compiler_params=pltpu.CompilerParams(vmem_limit_bytes=60 << 20),
         name="norm_chunk",
     )(jnp.asarray(rank, jnp.int32).reshape(1), full_x, mine, *others)
 
@@ -657,6 +717,7 @@
             jax.ShapeDtypeStruct((chunk, width), BF),
         ],
         cost_estimate=takes(4),
+        compiler_params=pltpu.CompilerParams(vmem_limit_bytes=60 << 20),
         name="back_chunk",
     )(grad_rows, resid1, mine, *others)
 
@@ -729,6 +790,17 @@
                 got.append((place, lax.ppermute(block, PLANE, self.perm(move))))
         return got
 
+    def spread_own(self, block, jh=0):
+        got = []
+        for jk in range(self.nc):
+            move = lambda c, h, k: (k ^ jk, h, c)
+            place = (self.h ^ jh) * self.nc + (self.c ^ jk)
+            got.append((place, lax.ppermute(block, PLANE, self.perm(move))))
+        return got
+
+    def turn_pairs(self, block, jh):
+        return lax.ppermute(block, PLANE, self.perm(lambda c, h, k: (c, h ^ jh, k)))
+
     def block_places(self):
         return [
             (self.h ^ jh) * self.nc + (self.c ^ jk) for jh in range(self.hi) for jk in range(self.nc)
@@ -741,6 +813,24 @@
             for jk in range(self.nc)
         ]
         return [lax.ppermute(p, PLANE, self.perm(m)) for p, m in zip(pieces, moves)]
+
+    def sum_pairs(self, pieces):
+        sent = [
+            lax.ppermute(
+                pieces[jh * self.nc + jk],
+                PLANE,
+                self.perm(lambda c, h, k, jh=jh: (c, h ^ jh, k)),
+            )
+            for jh in range(1, self.hi)
+            for jk in range(self.nc)
+        ]
+        return [sent[jk :: self.nc] for jk in range(self.nc)]
+
+    def sum_blocks(self, own):
+        return [
+            lax.ppermute(own[jk], PLANE, self.perm(lambda c, h, k, jk=jk: (k, h, c ^ jk)))
+            for jk in range(self.nc)
+        ]
 
     def swap(self, value, j):
         def move(c, h, k):
@@ -815,7 +905,9 @@
     qkv_oth = plane.pair(qkv_own)
     w_output, cotangent = fence(w_output, cotangent, *got_x)[:2]
     wo_own = over_fsdp(pack((w_output,), plane.c, 0, head_cols, 1))
-    _, got_g = zip(*plane.spread_rows(cotangent))
+    own_g = plane.spread_own(cotangent)
+    far_g = [plane.turn_pairs(cotangent, jh) for jh in range(1, plane.hi)]
+    places_g = [place for place, _ in own_g]
 
     full_x, hidden1, query, key, value, edge = project(
         got_x, places, qkv_own, qkv_oth, cos_tab, sin_tab, heads
@@ -831,21 +923,28 @@
     halo = lax.ppermute(edge, ("fsdp", "tp"), onward)
     wo_oth = plane.pair(after(wo_own, edge))
     late = attend(query, key, value, None, first)
+    late, far_g, own_g = fence(late, far_g, [piece for _, piece in own_g])
+    got_g = []
+    for jh in range(1, plane.hi):
+        for place, piece in plane.spread_own(far_g[jh - 1], jh):
+            places_g.append(place)
+            got_g.append(piece)
     halo, wo_own, wo_oth, *late = fence(halo, wo_own, wo_oth, *late)
-    own0 = over_fsdp(
-        pack(after((w_gate, w_up, w_down), halo), plane.c, 0, size, half // size)
-    )
-    mixed, lse = attend(query, key, value, halo, first, late)
+    shard0 = pack(after((w_gate, w_up, w_down), halo), plane.c, 0, size, half // size)
+    own0 = over_fsdp(shard0)
+    mixed, lse = attend(query, key, value, after(halo, shard0), first, late)
+    early = len(got_g) // 2
+    mixed, got_g[:early] = fence(mixed, got_g[:early])
 
     mixed_rows, mine, *shares = output_shares(mixed, wo_own, wo_oth, turned)
     sent = [plane.swap(shares[j - 1], j) for j in range(ranks - 1, 0, -1)]
-    mine, *got_g = fence(mine, *got_g)
-    grad_rows = join(got_g, places, turned)
+    mine, *got_g = fence(mine, *own_g, *got_g)
+    grad_rows = join(got_g, places_g, turned)
     shard1 = pack(after((w_gate, w_up, w_down), mine), plane.c, half, size, half // size)
     own1 = over_fsdp(shard1)
     mine, grad_rows, *sent = fence(mine, grad_rows, *sent, shard1)[:-1]
+    oth0 = plane.pair(after(own0, sent[0]))
     resid1, mine = norm_chunk(plane.r, full_x, mine, sent)
-    oth0 = plane.pair(after(own0, mine))
 
     sums, shared = {}, None
 
@@ -880,47 +979,65 @@
     oth1 = plane.pair(after(own1, act_own))
     own1, oth1 = fence(own1, oth1, total0)[:2]
     totals, sent, shared = {}, [], None
-    for j in list(range(ranks - 1, 0, -1)) + [0]:
+    for at, j in enumerate(list(range(ranks - 1, 0, -1)) + [0]):
+        piece = pieces[j]
+        if at > 2:
+            piece, sent[at - 3] = fence(piece, sent[at - 3])
         totals[j], shared = feed_forward(
-            j, turned[j], plane.block_places(), pieces[j], grad_rows, own1, oth1, half, size,
+            j, turned[j], plane.block_places(), piece, grad_rows, own1, oth1, half, size,
             sums[j], shared, BF if j else F32,
         )
         if j:
             sent.append(plane.swap(totals[j], j))
     act_own, act_oth, d_own, d_oth, *forth = shared
-    total1 = halves(lefts, (act_own, d_own), (act_oth, d_oth))
-    mine, *sent = fence(totals[0], *sent, total1)[:-1]
+    act_oth, *sent[:-1] = fence(act_oth, *sent[:-1])
+    other1 = grads(lefts, (act_oth, d_oth))
+    mine, sent[-1], other1 = fence(totals[0], sent[-1], other1)
+    other1 = plane.pair(other1)
     dx1, da = back_chunk(grad_rows, resid1, mine, sent)
-    share1 = reduce_rows(after(total1, da))
-
-    da, dout = dmixed(plane.gather(da), wo_own, wo_oth, turned)
+
+    def own_grads(j, _):
+        nonlocal total1
+        if total1 is None:
+            total1 = grads(lefts, fence(act_own, d_own, da)[:2], other1)
+        return total1
+
+    total1 = None
+    da_pieces = plane.gather(da, own_grads)
+    share1 = reduce_rows(fence(total1, *da_pieces[1:3])[0])
+
+    da, dout = dmixed(da_pieces, wo_own, wo_oth, turned)
     dout, share0, *forth = fence(dout, share0, *forth)
-    forth = plane.collect_blocks(forth)
+    others = [exchange(share0)]
+    pairs = plane.sum_pairs(forth)
     dquery, dkey, dvalue, edges = attend_back(
         query, key, value, halo, first, lse, dout, cos_tab, sin_tab
     )
     edges = lax.ppermute(edges, ("fsdp", "tp"), backward)
-    da, *forth = fence(da, *forth, dquery)[:-1]
-    others = [exchange(share) for share in fence(share0, share1, *forth)[:2]]
-    total_out = halves(
-        (da,), (mixed_rows[:, :head_cols],), (mixed_rows[:, head_cols:],)
-    )
-    share_out = reduce_rows(after(total_out, share0))
+    dquery, pairs, others[0] = fence(dquery, pairs, others[0])
+    own = [
+        functools.reduce(jnp.add, [p.astype(F32) for p in [forth[jk]] + pairs[jk]]).astype(BF)
+        for jk in range(nc)
+    ]
+    forth = plane.sum_blocks(own)
+    da, mixed_rows = fence(da, mixed_rows, *own)[:2]
+    total_out = halves((da,), (mixed_rows[:, :head_cols],), (mixed_rows[:, head_cols:],))
+    share_out = reduce_rows(total_out)
     edges = after(edges, total_out)
+    others.append(exchange(after(share1, *forth)))
     d_own, d_oth = finish_attention(dquery, dkey, dvalue, edges)
-    other_qkv = plane.pair(grads((hidden1,), (d_oth,)))
+    other2 = grads((hidden1,), (d_oth,))
+    other2, *forth = fence(other2, *forth)
+    other2 = plane.pair(other2)
     layer_out = functools.reduce(jnp.add, [p.astype(F32) for p in forth]).astype(BF)
-    other_qkv, layer_out, share_out, others[0] = fence(
-        other_qkv, layer_out, share_out, others[0]
-    )
-    others.append(exchange(share_out))
-    total_qkv = grads((hidden1,), (d_own,), other_qkv)
-    share_qkv = reduce_rows(total_qkv)
-    d_own, d_oth = fence(d_own, d_oth, total_qkv)[:2]
+    other2, layer_out = fence(other2, layer_out)
+    total2 = grads((hidden1,), (d_own,), other2)
+    share2 = reduce_rows(total2)
+    d_own, d_oth = fence(d_own, d_oth, total2)[:2]
     parts = input_parts(
         plane.r, plane.block_places(), d_own, d_oth, qkv_own, qkv_oth, full_x, dx1
     )
-    *parts, others[1], others[2] = fence(*parts, *others[1:])
+    *parts, others[1] = fence(*parts, others[1])
     back = plane.collect_blocks(parts)
 
     done = [both_parts(share0, others[0]), both_parts(share1, others[1])]
@@ -937,13 +1054,17 @@
         )
         for which in range(2)
     )
-    grad_output = jnp.concatenate(both_parts(share_out, others[2]), axis=1)
-    input_grad = functools.reduce(jnp.add, [p.astype(F32) for p in back]).astype(BF)
-    qkv = both_parts(share_qkv, exchange(share_qkv))
+    other2 = exchange(share2)
+    back, other2, share2 = fence(back, other2, share2)
+    last = both_parts(share2, other2)
     grad_query, grad_key, grad_value = (
-        jnp.concatenate([p[:, i * head_cols : (i + 1) * head_cols] for p in qkv], axis=1)
+        jnp.concatenate([p[:, i * head_cols : (i + 1) * head_cols] for p in last], axis=1)
         for i in range(3)
     )
+    grad_output = jnp.concatenate(
+        both_parts(share_out, exchange(after(share_out, back[0]))), axis=1
+    )
+    input_grad = functools.reduce(jnp.add, [p.astype(F32) for p in back]).astype(BF)
     grads_out = (grad_query, grad_key, grad_value, grad_output, grad_gate, grad_up, grad_down)
     return (layer_out, input_grad) + tuple(g.astype(F32) for g in grads_out)
 

time: 992 us -> 901 us (0.908)
  waiting for transfers between devices: 398 us -> 302 us
  Pallas kernels: 437 us -> 419 us
  starting transfers between devices: 74.6 us -> 84.8 us
    ppermute x14, waiting for transfers between devices: 162 us -> 116 us  [swap(): return lax.ppermute(value, PLANE, self.perm(move))]
    ppermute x0 -> x9, waiting for transfers between devices: none -> 44.9 us  [the longest x2 31.7 us: sum_pairs(): lax.ppermute(pieces[jh * self.nc + jk], PLANE, self.perm(lambda c, h, k,...]
    ppermute x8 -> x4, waiting for transfers between devices: 80.7 us -> 45.8 us  [collect_blocks(): return [lax.ppermute(p, PLANE, self.perm(m)) for p, m in zip(pieces, moves)]]
    ppermute x8 -> x4, starting transfers between devices: 33.5 us -> 6.56 us  [spread_rows(): got.append((place, lax.ppermute(block, PLANE, self.perm(move))))]
    reduce_scatter x4, waiting for transfers between devices: 24.5 us -> 0.02 us  [reduce_rows(): return lax.psum_scatter(total, 'fsdp', scatter_dimension=0, tiled=True)]
    ppermute x0 -> x9, starting transfers between devices: none -> 22.7 us  [the longest x4 15.8 us: spread_own(): got.append((place, lax.ppermute(block, PLANE, self.perm(move))))]
    pallas_call x3, Pallas kernels: 75.1 us -> 60.6 us  [the longest x1 32.3 us: attend_back(): pl.pallas_call(attend_back_kernel, grid_spec=pltpu.PrefetchScalarGridSpec...]
    ppermute x8, waiting for transfers between devices: 31.5 us -> 18.6 us  [pair(): return lax.ppermute(value, 'tp', perm)]
  transfers between devices with their start and end apart: 52 -> 53, of which waited for: 29 -> 27; matrix products, arithmetic and copies ran while one was open for 5% -> 7% of each run, Pallas kernels for 43% -> 46%
where the time goes in v3:
time: 901 us; the launch traced here: 890 us
  Pallas kernels  419 us (47%)
  waiting for transfers between devices  302 us (34%)
  starting transfers between devices  84.8 us (9%)
  other arithmetic  42.6 us (5%)
  local copies, waits for them, and re-layouts  26.5 us (3%)
  between operations  15.1 us (2%)
    pallas_call x8, Pallas kernels, feed_forward(): pl.pallas_call(functools.partial(ffn_kernel, first_half, len(starts) == 1...  158 us
    ppermute x14, waiting for transfers between devices, swap(): return lax.ppermute(value, PLANE, self.perm(move))  116 us
    pallas_call x8, Pallas kernels, grads(): pl.pallas_call(functools.partial(grads_kernel, len(lefts)), grid=(width /...  95.4 us
    ppermute x4, waiting for transfers between devices, spread_rows(): got.append((place, lax.ppermute(block, PLANE, self.perm(move))))  62.2 us
    ppermute x4, waiting for transfers between devices, collect_blocks(): return [lax.ppermute(p, PLANE, self.perm(m)) for p, m in zip(pieces, moves)]  45.8 us
    pallas_call x1, Pallas kernels, attend_back(): pl.pallas_call(attend_back_kernel, grid_spec=pltpu.PrefetchScalarGridSpec...  32.3 us
    ppermute x2, waiting for transfers between devices, sum_pairs(): lax.ppermute(pieces[jh * self.nc + jk], PLANE, self.perm(lambda c, h, k,...  31.7 us
    pallas_call x2, Pallas kernels, attend(): pl.pallas_call(functools.partial(attend_kernel, late, base), grid_spec=pl...  28.3 us
  transfers between devices with their start and end apart: 53, of which 27 were waited for; matrix products, arithmetic and copies ran while one was open for 7% of the time, Pallas kernels for 46%

profile of v3, /device:TPU:0, one launch (start us, length us, event | category | flops | bytes accessed | tf_op | source)
XLA Modules:
  0.0 890.3 jit_solution(9425910752738970343)
XLA Ops:
  16.7 6.3 fusion
  22.9 23.1 %collective-permute-done.1.refs_1_ = bf16[1536,512]{1,0:T(8,128)(2,1)S(1)} collective-permute-done((bf16[1536,512]{1,0:T(8,128)(2,1)}, bf16[1536,512]{1,0:T(8,128)(2,1)S(1)}, u32[]{:S(2)}, u32[]{:S(2)}) %collective-permute-start.1) | collective-permute-done | bytes 1572896 | tf_op jit(solution)/shard_map/ppermute | solution.py:790
  46.0 36.9 %collective-permute-done.3.refs_3_ = bf16[1536,512]{1,0:T(8,128)(2,1)} collective-permute-done((bf16[1536,512]{1,0:T(8,128)(2,1)}, bf16[1536,512]{1,0:T(8,128)(2,1)}, u32[]{:S(2)}, u32[]{:S(2)}) %collective-permute-start.3) | collective-permute-done | bytes 1572896 | tf_op jit(solution)/shard_map/ppermute | solution.py:790
  92.7 21.2 %norm_project.1 = (bf16[1536,2048]{1,0:T(8,128)(2,1)}, bf16[1536,2048]{1,0:T(8,128)(2,1)}, bf16[1536,512]{1,0:T(8,128)(2,1)}, bf16[1536,512]{1,0:T(8,128)(2,1)},...) custom-call(s32[4]{0:T(128)} %pad_add_fusion.table, bf16[1536,512]{1,0:T(8,128)(2,1)} %copy-done.17, ...), custom_call_target="tpu_custom_call" | custom-call | flops 600000000 | bytes 1 | tf_op jit(solution)/shard_map/norm_project/pallas_call | solution.py:103
  116.4 13.3 %collective-permute-start.8 = (bf16[1536,512]{1,0:T(8,128)(2,1)}, bf16[1536,512]{1,0:T(8,128)(2,1)}, u32[]{:S(2)}, u32[]{:S(2)}) collective-permute-start(bf16[1536,512]{1,0:T(8,128)(2,1)} %param.12), channel_id=1, source_target_pairs={{0,0},{1,4},{2,2},{3,6},{4,1},{5,5},{6,3},{7,7},{8,8},{9,12},{10,1... | collective-permute-start | bytes 4718600 | tf_op jit(solution)/shard_map/ppermute | solution.py:798
  132.8 10.2 %attend_late.1 = (bf16[1536,512]{1,0:T(8,128)(2,1)}, f32[4,1536,1]{2,1,0:T(8,128)}) custom-call(s32[6]{0:T(128)} %subtract_add_fusion.need, bf16[1536,512]{1,0:T(8,128)(2,1)} %get-tuple-element.209.q_ref, bf16[1536,512]{1,0:T(8,128)(2,1)} %get-tuple-element.210.k_ref, bf16[1536,512]{1,0:T(8,128)(2,1)} %get-tuple-element.211.v_ref, ...), custom_call_target="tpu_custom_call" | custom-call | flops 300000000 | bytes 1 | tf_op jit(solution)/shard_map/attend_late/pallas_call | solution.py:250
  143.0 5.9 collective-permute-done.9.refs_1_
  148.9 7.3 collective-permute-done.7
  162.8 18.1 %attend_early.1 = (bf16[1536,512]{1,0:T(8,128)(2,1)}, f32[4,1536,1]{2,1,0:T(8,128)}) custom-call(s32[6]{0:T(128)} %subtract_add_fusion.need, bf16[1536,512]{1,0:T(8,128)(2,1)} %get-tuple-element.209.q_ref, bf16[1536,512]{1,0:T(8,128)(2,1)} %get-tuple-element.210.k_ref, ...), custom_call_target="tpu_custom_call", output_to_operand_aliasing={{0}: (7, {}), {1}: (8, {})} | custom-call | flops 600000000 | bytes 1 | tf_op jit(solution)/shard_map/attend_early/pallas_call | solution.py:250
  180.9 10.6 %output_shares.1 = (bf16[1536,512]{1,0:T(8,128)(2,1)}, f32[384,2048]{1,0:T(8,128)}, bf16[384,2048]{1,0:T(8,128)(2,1)}, bf16[384,2048]{1,0:T(8,128)(2,1)}, bf16[384,2048]{1,0:T(8,128)(2,1)}) custom-call(s32[4]{0:T(128)} %pad_add_fusion.1.table, bf16[1536,512]{1,0:T(8,128)(2,1)} %get-tuple-element.230.m_ref, ...), custom_call_target="tpu_custom_call" | custom-call | flops 210000000 | bytes 1 | tf_op jit(solution)/shard_map/output_shares/pallas_call | solution.py:599
  191.6 13.5 %collective-permute-start.12 = (bf16[384,2048]{1,0:T(8,128)(2,1)}, bf16[384,2048]{1,0:T(8,128)(2,1)}, u32[]{:S(2)}, u32[]{:S(2)}) collective-permute-start(bf16[384,2048]{1,0:T(8,128)(2,1)} %get-tuple-element.242), channel_id=1, source_target_pairs={{0,6},{1,7},{2,4},{3,5},{4,2},{5,3},{6,0},{7,1},{8,14},{9,15},{10,... | collective-permute-start | bytes 4718600 | tf_op jit(solution)/shard_map/ppermute | solution.py:840
  209.2 6.5 join.1.g_ref.refs_0_
  215.7 24.5 %collective-permute-done.12.refs_0_ = bf16[384,2048]{1,0:T(8,128)(2,1)} collective-permute-done((bf16[384,2048]{1,0:T(8,128)(2,1)}, bf16[384,2048]{1,0:T(8,128)(2,1)}, u32[]{:S(2)}, u32[]{:S(2)}) %collective-permute-start.12) | collective-permute-done | bytes 1572896 | tf_op jit(solution)/shard_map/ppermute | solution.py:840
  240.2 32.6 %collective-permute-done.13.refs_1_ = bf16[384,2048]{1,0:T(8,128)(2,1)} collective-permute-done((bf16[384,2048]{1,0:T(8,128)(2,1)}, bf16[384,2048]{1,0:T(8,128)(2,1)}, u32[]{:S(2)}, u32[]{:S(2)}) %collective-permute-start.13) | collective-permute-done | bytes 1572896 | tf_op jit(solution)/shard_map/ppermute | solution.py:840
  276.4 7.1 norm_chunk.1
  286.5 19.6 %feed_forward.8 = (f32[384,2048]{1,0:T(8,128)}, bf16[1536,512]{1,0:T(8,128)(2,1)}, bf16[1536,512]{1,0:T(8,128)(2,1)}, bf16[1536,1024]{1,0:T(8,128)(2,1)}, bf16[1...) custom-call(s32[1]{0:T(128)} %bitcast.6.table, bf16[384,2048]{1,0:T(8,128)(2,1)} %get-tuple-element.289.h_ref, ...), custom_call_target="tpu_custom_call" | custom-call | flops 600000000 | bytes 1 | tf_op jit(solution)/shard_map/feed_forward/pallas_call | solution.py:475
  306.1 14.3 %collective-permute-done.16.h_ref = bf16[384,2048]{1,0:T(8,128)(2,1)S(1)} collective-permute-done((bf16[384,2048]{1,0:T(8,128)(2,1)}, bf16[384,2048]{1,0:T(8,128)(2,1)S(1)}, u32[]{:S(2)}, u32[]{:S(2)}) %collective-permute-start.16) | collective-permute-done | bytes 1572896 | tf_op jit(solution)/shard_map/ppermute | solution.py:840
  325.8 18.9 %feed_forward.9 = (f32[384,2048]{1,0:T(8,128)}, bf16[1536,512]{1,0:T(8,128)(2,1)}, bf16[1536,512]{1,0:T(8,128)(2,1)}, bf16[1536,1024]{1,0:T(8,128)(2,1)}, bf16[1...) custom-call(s32[1]{0:T(128)} %bitcast.7.table, ...), custom_call_target="tpu_custom_call", output_to_operand_aliasing={{1}: (5, {}), {2}: (6, {}), {3}: (7, {}), {4}: (8, {}), {6}... | custom-call | flops 600000000 | bytes 1 | tf_op jit(solution)/shard_map/feed_forward/pallas_call | solution.py:475
  344.7 18.9 %feed_forward.10 = (f32[384,2048]{1,0:T(8,128)}, bf16[1536,512]{1,0:T(8,128)(2,1)}, bf16[1536,512]{1,0:T(8,128)(2,1)}, bf16[1536,1024]{1,0:T(8,128)(2,1)}, bf16[...) custom-call(s32[1]{0:T(128)} %bitcast.8.table, ...), custom_call_target="tpu_custom_call", output_to_operand_aliasing={{1}: (5, {}), {2}: (6, {}), {3}: (7, {}), {4}: (8, {}), {6}... | custom-call | flops 600000000 | bytes 1 | tf_op jit(solution)/shard_map/feed_forward/pallas_call | solution.py:475
  366.1 18.5 %feed_forward.11 = (f32[384,2048]{1,0:T(8,128)}, bf16[1536,512]{1,0:T(8,128)(2,1)}, bf16[1536,512]{1,0:T(8,128)(2,1)}, bf16[1536,1024]{1,0:T(8,128)(2,1)}, bf16[...) custom-call(s32[1]{0:T(128)} %bitcast.9.table, ...), custom_call_target="tpu_custom_call", output_to_operand_aliasing={{1}: (5, {}), {2}: (6, {}), {3}: (7, {}), {4}: (8, {}), {6}... | custom-call | flops 600000000 | bytes 1 | tf_op jit(solution)/shard_map/feed_forward/pallas_call | solution.py:475
  384.6 15.1 %grads.8 = bf16[2048,1536]{1,0:T(8,128)(2,1)} custom-call(bf16[1536,2048]{1,0:T(8,128)(2,1)} %join.1.g_ref.refs_0_, bf16[1536,2048]{1,0:T(8,128)(2,1)} %get-tuple-element.280.refs_1_, bf16[1536,512]{1,0:T(8,128)(2,1)} %get-tuple-element.282.refs_2_, bf16[1536,1024]{1,0:T(8,128)(2,1)} %get-tuple-element.283.refs_3_), custom_call_target="tpu_custom_call" | custom-call | flops 300000000 | bytes 1 | tf_op jit(solution)/shard_map/grads/pallas_call | solution.py:748
  400.2 10.0 %collective-permute-done.21.refs_4_ = bf16[2048,1536]{1,0:T(8,128)(2,1)} collective-permute-done((bf16[2048,1536]{1,0:T(8,128)(2,1)}, bf16[2048,1536]{1,0:T(8,128)(2,1)}, u32[]{:S(2)}, u32[]{:S(2)}) %collective-permute-start.21) | collective-permute-done | bytes 6291488 | tf_op jit(solution)/shard_map/ppermute | solution.py:869
  410.2 16.3 %grads.9 = bf16[2048,1536]{1,0:T(8,128)(2,1)} custom-call(bf16[1536,2048]{1,0:T(8,128)(2,1)} %join.1.g_ref.refs_0_, bf16[1536,2048]{1,0:T(8,128)(2,1)} %get-tuple-element.280.refs_1_, bf16[1536,512]{1,0:T(8,128)(2,1)} %get-tuple-element.278.refs_2_, bf16[1536,1024]{1,0:T(8,128)(2,1)} %get-tuple-element.281.refs_3_, ...), custom_call_target="tpu_custom_call" | custom-call | flops 300000000 | bytes 1 | tf_op jit(solution)/shard_map/grads/pallas_call | solution.py:748
  428.5 21.1 %feed_forward.12 = (bf16[384,2048]{1,0:T(8,128)(2,1)}, bf16[1536,512]{1,0:T(8,128)(2,1)}, bf16[1536,512]{1,0:T(8,128)(2,1)}, bf16[1536,1024]{1,0:T(8,128)(2,1)},...) custom-call(s32[5]{0:T(128)} %stack.42.table, ...), custom_call_target="tpu_custom_call" | custom-call | flops 600000000 | bytes 1 | tf_op jit(solution)/shard_map/feed_forward/pallas_call | solution.py:475
  451.0 19.9 %feed_forward.13 = (bf16[384,2048]{1,0:T(8,128)(2,1)}, bf16[1536,512]{1,0:T(8,128)(2,1)}, bf16[1536,512]{1,0:T(8,128)(2,1)}, bf16[1536,1024]{1,0:T(8,128)(2,1)},...) custom-call(s32[5]{0:T(128)} %stack.44.table, ...), custom_call_target="tpu_custom_call", output_to_operand_aliasing={{1}: (7, {}), {2}: (8, {}), {3}: (9, {}), {4}: (10, {}), {5... | custom-call | flops 600000000 | bytes 1 | tf_op jit(solution)/shard_map/feed_forward/pallas_call | solution.py:475
  471.9 20.3 %feed_forward.14 = (bf16[384,2048]{1,0:T(8,128)(2,1)}, bf16[1536,512]{1,0:T(8,128)(2,1)}, bf16[1536,512]{1,0:T(8,128)(2,1)}, bf16[1536,1024]{1,0:T(8,128)(2,1)},...) custom-call(s32[5]{0:T(128)} %stack.43.table, ...), custom_call_target="tpu_custom_call", output_to_operand_aliasing={{1}: (7, {}), {2}: (8, {}), {3}: (9, {}), {4}: (10, {}), {5... | custom-call | flops 600000000 | bytes 1 | tf_op jit(solution)/shard_map/feed_forward/pallas_call | solution.py:475
  494.3 20.5 %feed_forward.15 = (f32[384,2048]{1,0:T(8,128)}, bf16[1536,512]{1,0:T(8,128)(2,1)}, bf16[1536,512]{1,0:T(8,128)(2,1)}, bf16[1536,1024]{1,0:T(8,128)(2,1)}, bf16[...) custom-call(s32[5]{0:T(128)} %stack.41.table, ...), custom_call_target="tpu_custom_call", output_to_operand_aliasing={{1}: (7, {}), {2}: (8, {}), {3}: (9, {}), {4}: (10, {}), {5... | custom-call | flops 600000000 | bytes 1 | tf_op jit(solution)/shard_map/feed_forward/pallas_call | solution.py:475
  514.8 5.2 collective-permute-done.24.refs_1_
  520.1 15.7 %grads.10 = bf16[2048,1536]{1,0:T(8,128)(2,1)} custom-call(bf16[1536,2048]{1,0:T(8,128)(2,1)} %join.1.g_ref.refs_0_, bf16[1536,2048]{1,0:T(8,128)(2,1)} %get-tuple-element.280.refs_1_, bf16[1536,512]{1,0:T(8,128)(2,1)} %get-tuple-element.323.refs_2_, bf16[1536,1024]{1,0:T(8,128)(2,1)} %get-tuple-element.324.refs_3_), custom_call_target="tpu_custom_call" | custom-call | flops 300000000 | bytes 1 | tf_op jit(solution)/shard_map/grads/pallas_call | solution.py:748
  535.8 8.4 back_chunk.1
  547.0 16.4 %grads.11 = bf16[2048,1536]{1,0:T(8,128)(2,1)} custom-call(bf16[1536,2048]{1,0:T(8,128)(2,1)} %join.1.g_ref.refs_0_, bf16[1536,2048]{1,0:T(8,128)(2,1)} %get-tuple-element.280.refs_1_, bf16[1536,512]{1,0:T(8,128)(2,1)} %get-tuple-element.332.refs_2_, bf16[1536,1024]{1,0:T(8,128)(2,1)} %get-tuple-element.333.refs_3_, ...), custom_call_target="tpu_custom_call" | custom-call | flops 300000000 | bytes 1 | tf_op jit(solution)/shard_map/grads/pallas_call | solution.py:748
  563.4 17.9 %collective-permute-done.26.refs_2_ = bf16[384,2048]{1,0:T(8,128)(2,1)S(1)} collective-permute-done((bf16[384,2048]{1,0:T(8,128)(2,1)}, bf16[384,2048]{1,0:T(8,128)(2,1)S(1)}, u32[]{:S(2)}, u32[]{:S(2)}) %collective-permute-start.26) | collective-permute-done | bytes 1572896 | tf_op jit(solution)/shard_map/ppermute | solution.py:840
  585.8 16.6 %collective-permute-done.29 = bf16[192,2048]{1,0:T(8,128)(2,1)S(1)} collective-permute-done((bf16[192,2048]{1,0:T(8,128)(2,1)S(1)}, bf16[192,2048]{1,0:T(8,128)(2,1)S(1)}, u32[]{:S(2)}, u32[]{:S(2)}) %collective-permute-start.29) | collective-permute-done | bytes 786464 | tf_op jit(solution)/shard_map/ppermute | solution.py:840
  604.9 10.2 %dmixed.1 = (bf16[1536,2048]{1,0:T(8,128)(2,1)}, bf16[1536,512]{1,0:T(8,128)(2,1)}) custom-call(s32[4]{0:T(128)} %pad_add_fusion.1.table, bf16[384,2048]{1,0:T(8,128)(2,1)} %get-tuple-element.329.refs_0_, bf16[384,2048]{1,0:T(8,128)(2,1)} %copy-done.10, bf16[384,2048]{1,0:T(8,128)(2,1)} %copy-done.9, bf16[384,2048]{1,0:T(8,128)(2,1)} %pad_maximum_fusion.refs_3_, ...), custom_call_target="tpu_custom_call" | custom-call | flops 210000000 | bytes 1 | tf_op jit(solution)/shard_map/dmixed/pallas_call | solution.py:641
  618.2 32.3 %attend_back.1 = (bf16[1536,512]{1,0:T(8,128)(2,1)}, f32[1536,512]{1,0:T(8,128)}, f32[1536,512]{1,0:T(8,128)}, bf16[2,1024,512]{2,1,0:T(8,128)(2,1)}) custom-call(s32[6]{0:T(128)} %subtract_add_fusion.need, bf16[1536,512]{1,0:T(8,128)(2,1)} %get-tuple-element.209.q_ref, bf16[1536,512]{1,0:T(8,128)(2,1)} %get-tuple-element.210.k_ref, ...), custom_call_target="tpu_custom_call" | custom-call | flops 1290000000 | bytes 1 | tf_op jit(solution)/shard_map/attend_back/pallas_call | solution.py:325
  652.6 31.0 %collective-permute-done.31 = bf16[1536,512]{1,0:T(8,128)(2,1)} collective-permute-done((bf16[1536,512]{1,0:T(8,128)(2,1)}, bf16[1536,512]{1,0:T(8,128)(2,1)}, u32[]{:S(2)}, u32[]{:S(2)}) %collective-permute-start.31) | collective-permute-done | bytes 1572896 | tf_op jit(solution)/shard_map/ppermute | solution.py:819
  693.3 6.1 grads.12
  702.4 6.6 grads.13
  708.9 7.8 finish_attention.1
  716.7 9.1 %grads.14 = bf16[2048,768]{1,0:T(8,128)(2,1)} custom-call(bf16[1536,2048]{1,0:T(8,128)(2,1)} %get-tuple-element.207.refs_0_, bf16[1536,768]{1,0:T(8,128)(2,1)} %get-tuple-element.370.refs_1_.d_oth), custom_call_target="tpu_custom_call" | custom-call | flops 300000000 | bytes 1 | tf_op jit(solution)/shard_map/grads/pallas_call | solution.py:748
  737.0 10.1 %grads.15 = bf16[2048,768]{1,0:T(8,128)(2,1)} custom-call(bf16[1536,2048]{1,0:T(8,128)(2,1)} %get-tuple-element.207.refs_0_, bf16[1536,768]{1,0:T(8,128)(2,1)} %get-tuple-element.369.refs_1_.d_own, bf16[2048,768]{1,0:T(8,128)(2,1)} %copy-done.11), custom_call_target="tpu_custom_call" | custom-call | flops 300000000 | bytes 1 | tf_op jit(solution)/shard_map/grads/pallas_call | solution.py:748
  753.6 23.4 %input_parts.1 = (bf16[1536,512]{1,0:T(8,128)(2,1)}, bf16[1536,512]{1,0:T(8,128)(2,1)}, bf16[1536,512]{1,0:T(8,128)(2,1)}, bf16[1536,512]{1,0:T(8,128)(2,1)}) custom-call(s32[5]{0:T(128)} %stack.41.table, bf16[1536,768]{1,0:T(8,128)(2,1)} %get-tuple-element.369.refs_1_.d_own, bf16[1536,768]{1,0:T(8,128)(2,1)} %get-tuple-element.370.refs_1_.d_oth, ...), custom_call_target="tpu_custom_call" | custom-call | flops 600000000 | bytes 1 | tf_op jit(solution)/shard_map/input_parts/pallas_call | solution.py:557
  777.1 7.2 collective-permute-done.38
  784.3 13.3 %collective-permute-start.39 = (bf16[1536,512]{1,0:T(8,128)(2,1)}, bf16[1536,512]{1,0:T(8,128)(2,1)}, u32[]{:S(2)}, u32[]{:S(2)}) collective-permute-start(bf16[1536,512]{1,0:T(8,128)(2,1)} %get-tuple-element.378), channel_id=1, source_target_pairs={{0,0},{1,4},{2,2},{3,6},{4,1},{5,5},{6,3},{7,7},{8,8},{9,12},{10,1... | collective-permute-start | bytes 4718600 | tf_op jit(solution)/shard_map/ppermute | solution.py:815
  822.0 9.3 %collective-permute-done.40 = bf16[1536,512]{1,0:T(8,128)(2,1)} collective-permute-done((bf16[1536,512]{1,0:T(8,128)(2,1)}, bf16[1536,512]{1,0:T(8,128)(2,1)}, u32[]{:S(2)}, u32[]{:S(2)}) %collective-permute-start.40) | collective-permute-done | bytes 1572896 | tf_op jit(solution)/shard_map/ppermute | solution.py:815
  831.3 36.5 %collective-permute-done.42 = bf16[1536,512]{1,0:T(8,128)(2,1)} collective-permute-done((bf16[1536,512]{1,0:T(8,128)(2,1)}, bf16[1536,512]{1,0:T(8,128)(2,1)}, u32[]{:S(2)}, u32[]{:S(2)}) %collective-permute-start.42) | collective-permute-done | bytes 1572896 | tf_op jit(solution)/shard_map/ppermute | solution.py:815
  867.8 5.6 collective-permute-done.43
  874.8 4.8 add_convert_fusion
  (217 shorter events, 131.2 us)
Async XLA Ops:
  7.2 77.9 %all-gather.5.cloned.1.call-start = ((), (), s32[]{:S(2)}) async-start(), calls=%async_computation.4 | async-start | bytes 3932160 | tf_op jit(solution)/shard_map/all_gather | solution.py:887
  9.3 121.6 %all-gather.7.cloned.1.call-start = ((), (), s32[]{:S(2)}) async-start(), calls=%async_computation.5 | async-start | bytes 1310720 | tf_op jit(solution)/shard_map/all_gather | solution.py:887
  9.4 36.7 %collective-permute-start.1 = (bf16[1536,512]{1,0:T(8,128)(2,1)}, bf16[1536,512]{1,0:T(8,128)(2,1)S(1)}, u32[]{:S(2)}, u32[]{:S(2)}) collective-permute-start(bf16[1536,512]{1,0:T(8,128)(2,1)} %param.11), channel_id=1, source_target_pairs={{0,4},{1,0},{2,6},{3,2},{4,5},{5,1},{6,7},{7,3},{8,12},{9,8},{10,1... | collective-permute-start | bytes 4718600 | tf_op jit(solution)/shard_map/ppermute | solution.py:790
  12.3 33.7 %collective-permute-start = (bf16[1536,512]{1,0:T(8,128)(2,1)}, bf16[1536,512]{1,0:T(8,128)(2,1)S(1)}, u32[]{:S(2)}, u32[]{:S(2)}) collective-permute-start(bf16[1536,512]{1,0:T(8,128)(2,1)} %param.11), channel_id=1, source_target_pairs={{0,0},{1,4},{2,2},{3,6},{4,1},{5,5},{6,3},{7,7},{8,8},{9,12},{10,1... | collective-permute-start | bytes 4718600 | tf_op jit(solution)/shard_map/ppermute | solution.py:790
  14.4 68.6 %collective-permute-start.3 = (bf16[1536,512]{1,0:T(8,128)(2,1)}, bf16[1536,512]{1,0:T(8,128)(2,1)}, u32[]{:S(2)}, u32[]{:S(2)}) collective-permute-start(bf16[1536,512]{1,0:T(8,128)(2,1)} %param.11), channel_id=1, source_target_pairs={{0,6},{1,2},{2,4},{3,0},{4,7},{5,3},{6,5},{7,1},{8,14},{9,10},{10,... | collective-permute-start | bytes 4718600 | tf_op jit(solution)/shard_map/ppermute | solution.py:790
  15.9 69.2 %collective-permute-start.2 = (bf16[1536,512]{1,0:T(8,128)(2,1)}, bf16[1536,512]{1,0:T(8,128)(2,1)}, u32[]{:S(2)}, u32[]{:S(2)}) collective-permute-start(bf16[1536,512]{1,0:T(8,128)(2,1)} %param.11), channel_id=1, source_target_pairs={{0,2},{1,6},{2,0},{3,4},{4,3},{5,7},{6,1},{7,5},{8,10},{9,14},{10,... | collective-permute-start | bytes 4718600 | tf_op jit(solution)/shard_map/ppermute | solution.py:790
  86.9 189.2 %all-gather.9.cloned.1.call-start = ((), (), s32[]{:S(2)}) async-start(), calls=%async_computation.6 | async-start | bytes 7864320 | tf_op jit(solution)/shard_map/all_gather | solution.py:887
  113.9 42.4 %collective-permute-start.5 = (bf16[1024,1024]{1,0:T(8,128)(2,1)}, bf16[1024,1024]{1,0:T(8,128)(2,1)S(1)}, u32[]{:S(2)}, u32[]{:S(2)}) collective-permute-start(bf16[1024,1024]{1,0:T(8,128)(2,1)} %get-tuple-element.212), channel_id=1, source_target_pairs={{0,1},{1,8},{2,3},{3,10},{8,9},{9,16},{10,11},{11,18},{16,17},{17,... | collective-permute-start | bytes 6291464 | tf_op jit(solution)/shard_map/ppermute | solution.py:923
  116.1 32.8 %collective-permute-start.9 = (bf16[1536,512]{1,0:T(8,128)(2,1)}, bf16[1536,512]{1,0:T(8,128)(2,1)}, u32[]{:S(2)}, u32[]{:S(2)}) collective-permute-start(bf16[1536,512]{1,0:T(8,128)(2,1)} %param.12), channel_id=1, source_target_pairs={{0,4},{1,0},{2,6},{3,2},{4,5},{5,1},{6,7},{7,3},{8,12},{9,8},{10,1... | collective-permute-start | bytes 4718600 | tf_op jit(solution)/shard_map/ppermute | solution.py:798
  116.4 32.5 %collective-permute-start.8 = (bf16[1536,512]{1,0:T(8,128)(2,1)}, bf16[1536,512]{1,0:T(8,128)(2,1)}, u32[]{:S(2)}, u32[]{:S(2)}) collective-permute-start(bf16[1536,512]{1,0:T(8,128)(2,1)} %param.12), channel_id=1, source_target_pairs={{0,0},{1,4},{2,2},{3,6},{4,1},{5,5},{6,3},{7,7},{8,8},{9,12},{10,1... | collective-permute-start | bytes 4718600 | tf_op jit(solution)/shard_map/ppermute | solution.py:798
  129.6 26.6 %collective-permute-start.7 = (bf16[1536,512]{1,0:T(8,128)(2,1)}, bf16[1536,512]{1,0:T(8,128)(2,1)}, u32[]{:S(2)}, u32[]{:S(2)}) collective-permute-start(bf16[1536,512]{1,0:T(8,128)(2,1)} %param.12), channel_id=1, source_target_pairs={{0,2},{1,3},{2,0},{3,1},{4,6},{5,7},{6,4},{7,5},{8,10},{9,11},{10,... | collective-permute-start | bytes 4718600 | tf_op jit(solution)/shard_map/ppermute | solution.py:802
  130.9 25.3 %collective-permute-start.6 = (bf16[2048,256]{1,0:T(8,128)(2,1)}, bf16[2048,256]{1,0:T(8,128)(2,1)S(1)}, u32[]{:S(2)}, u32[]{:S(2)}) collective-permute-start(bf16[2048,256]{1,0:T(8,128)(2,1)} %all-gather.7.cloned.1.call-done.w_own.refs_4_), channel_id=1, source_target_pairs={{0,1},{1,0},{2,3},{3,2},{4,5},{5,4},{6,7},{7,6},{8,9},{9,8},{10,11... | collective-permute-start | bytes 3145736 | tf_op jit(solution)/shard_map/ppermute | solution.py:869
  159.8 239.9 %all-gather.11.cloned.1.call-start = ((), (), s32[]{:S(2)}) async-start(), calls=%async_computation.7 | async-start | bytes 7864320 | tf_op jit(solution)/shard_map/all_gather | solution.py:887
  159.9 21.0 %collective-permute-start.10 = (bf16[1536,512]{1,0:T(8,128)(2,1)}, bf16[1536,512]{1,0:T(8,128)(2,1)S(1)}, u32[]{:S(2)}, u32[]{:S(2)}) collective-permute-start(bf16[1536,512]{1,0:T(8,128)(2,1)} %collective-permute-done.7), channel_id=1, source_target_pairs={{0,0},{1,4},{2,2},{3,6},{4,1},{5,5},{6,3},{7,7},{8,8},{9,12},{10,1... | collective-permute-start | bytes 4718600 | tf_op jit(solution)/shard_map/ppermute | solution.py:798
  162.8 43.5 %collective-permute-start.11 = (bf16[1536,512]{1,0:T(8,128)(2,1)}, bf16[1536,512]{1,0:T(8,128)(2,1)S(1)}, u32[]{:S(2)}, u32[]{:S(2)}) collective-permute-start(bf16[1536,512]{1,0:T(8,128)(2,1)} %collective-permute-done.7), channel_id=1, source_target_pairs={{0,4},{1,0},{2,6},{3,2},{4,5},{5,1},{6,7},{7,3},{8,12},{9,8},{10,1... | collective-permute-start | bytes 4718600 | tf_op jit(solution)/shard_map/ppermute | solution.py:798
  191.6 48.6 %collective-permute-start.12 = (bf16[384,2048]{1,0:T(8,128)(2,1)}, bf16[384,2048]{1,0:T(8,128)(2,1)}, u32[]{:S(2)}, u32[]{:S(2)}) collective-permute-start(bf16[384,2048]{1,0:T(8,128)(2,1)} %get-tuple-element.242), channel_id=1, source_target_pairs={{0,6},{1,7},{2,4},{3,5},{4,2},{5,3},{6,0},{7,1},{8,14},{9,15},{10,... | collective-permute-start | bytes 4718600 | tf_op jit(solution)/shard_map/ppermute | solution.py:840
  205.1 67.8 %collective-permute-start.13 = (bf16[384,2048]{1,0:T(8,128)(2,1)}, bf16[384,2048]{1,0:T(8,128)(2,1)}, u32[]{:S(2)}, u32[]{:S(2)}) collective-permute-start(bf16[384,2048]{1,0:T(8,128)(2,1)} %get-tuple-element.243), channel_id=1, source_target_pairs={{0,4},{1,5},{2,6},{3,7},{4,0},{5,1},{6,2},{7,3},{8,12},{9,13},{10,... | collective-permute-start | bytes 4718600 | tf_op jit(solution)/shard_map/ppermute | solution.py:840
  205.1 69.2 %collective-permute-start.14 = (bf16[384,2048]{1,0:T(8,128)(2,1)}, bf16[384,2048]{1,0:T(8,128)(2,1)}, u32[]{:S(2)}, u32[]{:S(2)}) collective-permute-start(bf16[384,2048]{1,0:T(8,128)(2,1)} %get-tuple-element.244), channel_id=1, source_target_pairs={{0,2},{1,3},{2,0},{3,1},{4,6},{5,7},{6,4},{7,5},{8,10},{9,11},{10,... | collective-permute-start | bytes 4718600 | tf_op jit(solution)/shard_map/ppermute | solution.py:840
  276.0 10.5 %collective-permute-start.17 = (bf16[2048,1536]{1,0:T(8,128)(2,1)}, bf16[2048,1536]{1,0:T(8,128)(2,1)}, u32[]{:S(2)}, u32[]{:S(2)}) collective-permute-start(bf16[2048,1536]{1,0:T(8,128)(2,1)} %all-gather.9.cloned.1.call-done.own_ref), channel_id=1, source_target_pairs={{0,1},{1,0},{2,3},{3,2},{4,5},{5,4},{6,7},{7,6},{8,9},{9,8},{10,11... | collective-permute-start | bytes 18874376 | tf_op jit(solution)/shard_map/ppermute | solution.py:869
  276.1 338.9 %reduce-scatter.5.cloned.1.call-start = ((), (), s32[]{:S(2)}) async-start(), calls=%async_computation.8 | async-start | bytes 7864320 | tf_op jit(solution)/shard_map/reduce_scatter | solution.py:966
  283.5 37.0 %collective-permute-start.16 = (bf16[384,2048]{1,0:T(8,128)(2,1)}, bf16[384,2048]{1,0:T(8,128)(2,1)S(1)}, u32[]{:S(2)}, u32[]{:S(2)}) collective-permute-start(bf16[384,2048]{1,0:T(8,128)(2,1)} %get-tuple-element.289.h_ref), channel_id=1, source_target_pairs={{0,4},{1,5},{2,6},{3,7},{4,0},{5,1},{6,2},{7,3},{8,12},{9,13},{10,... | collective-permute-start | bytes 4718600 | tf_op jit(solution)/shard_map/ppermute | solution.py:840
  284.9 36.7 %collective-permute-start.15 = (bf16[384,2048]{1,0:T(8,128)(2,1)}, bf16[384,2048]{1,0:T(8,128)(2,1)S(1)}, u32[]{:S(2)}, u32[]{:S(2)}) collective-permute-start(bf16[384,2048]{1,0:T(8,128)(2,1)} %get-tuple-element.289.h_ref), channel_id=1, source_target_pairs={{0,2},{1,3},{2,0},{3,1},{4,6},{5,7},{6,4},{7,5},{8,10},{9,11},{10,... | collective-permute-start | bytes 4718600 | tf_op jit(solution)/shard_map/ppermute | solution.py:840
  323.6 40.0 %collective-permute-start.19 = (bf16[192,2048]{1,0:T(8,128)(2,1)}, bf16[192,2048]{1,0:T(8,128)(2,1)S(1)}, u32[]{:S(2)}, u32[]{:S(2)}) collective-permute-start(bf16[192,2048]{1,0:T(8,128)(2,1)} %slice.101), channel_id=1, source_target_pairs={{0,2},{1,3},{2,0},{3,1},{4,6},{5,7},{6,4},{7,5},{8,10},{9,11},{10,... | collective-permute-start | bytes 2359304 | tf_op jit(solution)/shard_map/ppermute | solution.py:840
  325.1 38.5 %collective-permute-start.18 = (bf16[192,2048]{1,0:T(8,128)(2,1)}, bf16[192,2048]{1,0:T(8,128)(2,1)}, u32[]{:S(2)}, u32[]{:S(2)}) collective-permute-start(bf16[192,2048]{1,0:T(8,128)(2,1)} %slice.100), channel_id=1, source_target_pairs={{0,4},{1,5},{2,6},{3,7},{4,0},{5,1},{6,2},{7,3},{8,12},{9,13},{10,... | collective-permute-start | bytes 2359304 | tf_op jit(solution)/shard_map/ppermute | solution.py:840
  399.7 28.8 %collective-permute-start.20 = (bf16[2048,1536]{1,0:T(8,128)(2,1)}, bf16[2048,1536]{1,0:T(8,128)(2,1)}, u32[]{:S(2)}, u32[]{:S(2)}) collective-permute-start(bf16[2048,1536]{1,0:T(8,128)(2,1)} %all-gather.11.cloned.1.call-done.own_ref), channel_id=1, source_target_pairs={{0,1},{1,0},{2,3},{3,2},{4,5},{5,4},{6,7},{7,6},{8,9},{9,8},{10,11... | collective-permute-start | bytes 18874376 | tf_op jit(solution)/shard_map/ppermute | solution.py:869
  426.6 320.7 %reduce-scatter.7.cloned.1.call-start = ((), (), s32[]{:S(2)}) async-start(), calls=%async_computation.9 | async-start | bytes 7864320 | tf_op jit(solution)/shard_map/reduce_scatter | solution.py:966
  449.6 44.7 %collective-permute-start.22 = (bf16[384,2048]{1,0:T(8,128)(2,1)}, bf16[384,2048]{1,0:T(8,128)(2,1)S(1)}, u32[]{:S(2)}, u32[]{:S(2)}) collective-permute-start(bf16[384,2048]{1,0:T(8,128)(2,1)} %get-tuple-element.288), channel_id=1, source_target_pairs={{0,6},{1,7},{2,4},{3,5},{4,2},{5,3},{6,0},{7,1},{8,14},{9,15},{10,... | collective-permute-start | bytes 4718600 | tf_op jit(solution)/shard_map/ppermute | solution.py:840
  471.0 49.1 %collective-permute-start.24 = (bf16[384,2048]{1,0:T(8,128)(2,1)}, bf16[384,2048]{1,0:T(8,128)(2,1)S(1)}, u32[]{:S(2)}, u32[]{:S(2)}) collective-permute-start(bf16[384,2048]{1,0:T(8,128)(2,1)} %get-tuple-element.322), channel_id=1, source_target_pairs={{0,4},{1,5},{2,6},{3,7},{4,0},{5,1},{6,2},{7,3},{8,12},{9,13},{10,... | collective-permute-start | bytes 4718600 | tf_op jit(solution)/shard_map/ppermute | solution.py:840
  492.2 43.5 %collective-permute-start.23 = (bf16[384,2048]{1,0:T(8,128)(2,1)}, bf16[384,2048]{1,0:T(8,128)(2,1)}, u32[]{:S(2)}, u32[]{:S(2)}) collective-permute-start(bf16[384,2048]{1,0:T(8,128)(2,1)} %get-tuple-element.319), channel_id=1, source_target_pairs={{0,2},{1,3},{2,0},{3,1},{4,6},{5,7},{6,4},{7,5},{8,10},{9,11},{10,... | collective-permute-start | bytes 4718600 | tf_op jit(solution)/shard_map/ppermute | solution.py:840
  535.8 11.2 %collective-permute-start.27 = (bf16[2048,1536]{1,0:T(8,128)(2,1)}, bf16[2048,1536]{1,0:T(8,128)(2,1)}, u32[]{:S(2)}, u32[]{:S(2)}) collective-permute-start(bf16[2048,1536]{1,0:T(8,128)(2,1)} %grads.10), channel_id=1, source_target_pairs={{0,1},{1,0},{2,3},{3,2},{4,5},{5,4},{6,7},{7,6},{8,9},{9,8},{10,11... | collective-permute-start | bytes 18874376 | tf_op jit(solution)/shard_map/ppermute | solution.py:869
  544.2 37.0 %collective-permute-start.26 = (bf16[384,2048]{1,0:T(8,128)(2,1)}, bf16[384,2048]{1,0:T(8,128)(2,1)S(1)}, u32[]{:S(2)}, u32[]{:S(2)}) collective-permute-start(bf16[384,2048]{1,0:T(8,128)(2,1)} %get-tuple-element.329.refs_0_), channel_id=1, source_target_pairs={{0,4},{1,5},{2,6},{3,7},{4,0},{5,1},{6,2},{7,3},{8,12},{9,13},{10,... | collective-permute-start | bytes 4718600 | tf_op jit(solution)/shard_map/ppermute | solution.py:840
  545.5 36.7 %collective-permute-start.25 = (bf16[384,2048]{1,0:T(8,128)(2,1)}, bf16[384,2048]{1,0:T(8,128)(2,1)S(1)}, u32[]{:S(2)}, u32[]{:S(2)}) collective-permute-start(bf16[384,2048]{1,0:T(8,128)(2,1)} %get-tuple-element.329.refs_0_), channel_id=1, source_target_pairs={{0,2},{1,3},{2,0},{3,1},{4,6},{5,7},{6,4},{7,5},{8,10},{9,11},{10,... | collective-permute-start | bytes 4718600 | tf_op jit(solution)/shard_map/ppermute | solution.py:840
  582.3 226.1 %reduce-scatter.9.cloned.1.call-start = ((), (), s32[]{:S(2)}) async-start(), calls=%async_computation.10 | async-start | bytes 3932160 | tf_op jit(solution)/shard_map/reduce_scatter | solution.py:966
  583.5 18.9 %collective-permute-start.29 = (bf16[192,2048]{1,0:T(8,128)(2,1)S(1)}, bf16[192,2048]{1,0:T(8,128)(2,1)S(1)}, u32[]{:S(2)}, u32[]{:S(2)}) collective-permute-start(bf16[192,2048]{1,0:T(8,128)(2,1)S(1)} %slice.103), channel_id=1, source_target_pairs={{0,2},{1,3},{2,0},{3,1},{4,6},{5,7},{6,4},{7,5},{8,10},{9,11},{10,... | collective-permute-start | bytes 2359304 | tf_op jit(solution)/shard_map/ppermute | solution.py:840
  585.0 18.5 %collective-permute-start.28 = (bf16[192,2048]{1,0:T(8,128)(2,1)S(1)}, bf16[192,2048]{1,0:T(8,128)(2,1)S(1)}, u32[]{:S(2)}, u32[]{:S(2)}) collective-permute-start(bf16[192,2048]{1,0:T(8,128)(2,1)S(1)} %slice.102), channel_id=1, source_target_pairs={{0,4},{1,5},{2,6},{3,7},{4,0},{5,1},{6,2},{7,3},{8,12},{9,13},{10,... | collective-permute-start | bytes 2359304 | tf_op jit(solution)/shard_map/ppermute | solution.py:840
  615.1 37.5 %collective-permute-start.30 = (bf16[1536,512]{1,0:T(8,128)(2,1)S(1)}, bf16[1536,512]{1,0:T(8,128)(2,1)}, u32[]{:S(2)}, u32[]{:S(2)}) collective-permute-start(bf16[1536,512]{1,0:T(8,128)(2,1)S(1)} %copy-done.3), channel_id=1, source_target_pairs={{0,2},{1,3},{2,0},{3,1},{4,6},{5,7},{6,4},{7,5},{8,10},{9,11},{10,... | collective-permute-start | bytes 4718600 | tf_op jit(solution)/shard_map/ppermute | solution.py:819
  615.7 67.8 %collective-permute-start.31 = (bf16[1536,512]{1,0:T(8,128)(2,1)}, bf16[1536,512]{1,0:T(8,128)(2,1)}, u32[]{:S(2)}, u32[]{:S(2)}) collective-permute-start(bf16[1536,512]{1,0:T(8,128)(2,1)} %get-tuple-element.347), channel_id=1, source_target_pairs={{0,2},{1,3},{2,0},{3,1},{4,6},{5,7},{6,4},{7,5},{8,10},{9,11},{10,... | collective-permute-start | bytes 4718600 | tf_op jit(solution)/shard_map/ppermute | solution.py:819
  617.1 66.4 %collective-permute-start.32 = (bf16[512,1536]{1,0:T(8,128)(2,1)}, bf16[512,1536]{1,0:T(8,128)(2,1)}, u32[]{:S(2)}, u32[]{:S(2)}) collective-permute-start(bf16[512,1536]{1,0:T(8,128)(2,1)} %reduce-scatter.5.cloned.1.call-done), channel_id=1, source_target_pairs={{0,4},{4,0},{1,5},{5,1},{2,6},{6,2},{3,7},{7,3},{8,12},{12,8},{9,1... | collective-permute-start | bytes 4718600 | tf_op jit(solution)/shard_map/ppermute | solution.py:969
  650.5 58.4 %collective-permute-start.33 = (bf16[2,1024,512]{2,1,0:T(8,128)(2,1)}, bf16[2,1024,512]{2,1,0:T(8,128)(2,1)}, u32[]{:S(2)}, u32[]{:S(2)}) collective-permute-start(bf16[2,1024,512]{2,1,0:T(8,128)(2,1)} %get-tuple-element.352), channel_id=1, source_target_pairs={{1,0},{8,1},{3,2},{10,3},{9,8},{16,9},{11,10},{18,11},{17,16},{24,... | collective-permute-start | bytes 6291464 | tf_op jit(solution)/shard_map/ppermute | solution.py:1016
  686.6 39.2 %collective-permute-start.35 = (bf16[1536,512]{1,0:T(8,128)(2,1)}, bf16[1536,512]{1,0:T(8,128)(2,1)S(1)}, u32[]{:S(2)}, u32[]{:S(2)}) collective-permute-start(bf16[1536,512]{1,0:T(8,128)(2,1)} %add_convert_fusion.3), channel_id=1, source_target_pairs={{0,0},{1,4},{2,2},{3,6},{4,1},{5,5},{6,3},{7,7},{8,8},{9,12},{10,1... | collective-permute-start | bytes 4718600 | tf_op jit(solution)/shard_map/ppermute | solution.py:831
  690.7 36.3 %collective-permute-start.36 = (bf16[1536,512]{1,0:T(8,128)(2,1)S(1)}, bf16[1536,512]{1,0:T(8,128)(2,1)}, u32[]{:S(2)}, u32[]{:S(2)}) collective-permute-start(bf16[1536,512]{1,0:T(8,128)(2,1)S(1)} %add_convert_fusion.2), channel_id=1, source_target_pairs={{0,1},{1,5},{2,3},{3,7},{4,0},{5,4},{6,2},{7,6},{8,9},{9,13},{10,1... | collective-permute-start | bytes 4718600 | tf_op jit(solution)/shard_map/ppermute | solution.py:831
  747.2 126.3 %reduce-scatter.11.cloned.1.call-start = ((), (), s32[]{:S(2)}) async-start(), calls=%async_computation.11 | async-start | bytes 1310720 | tf_op jit(solution)/shard_map/reduce_scatter | solution.py:966
  747.2 37.1 %collective-permute-start.38 = (bf16[512,1536]{1,0:T(8,128)(2,1)}, bf16[512,1536]{1,0:T(8,128)(2,1)}, u32[]{:S(2)}, u32[]{:S(2)}) collective-permute-start(bf16[512,1536]{1,0:T(8,128)(2,1)} %reduce-scatter.7.cloned.1.call-done), channel_id=1, source_target_pairs={{0,4},{4,0},{1,5},{5,1},{2,6},{6,2},{3,7},{7,3},{8,12},{12,8},{9,1... | collective-permute-start | bytes 4718600 | tf_op jit(solution)/shard_map/ppermute | solution.py:969
  784.3 37.8 %collective-permute-start.39 = (bf16[1536,512]{1,0:T(8,128)(2,1)}, bf16[1536,512]{1,0:T(8,128)(2,1)}, u32[]{:S(2)}, u32[]{:S(2)}) collective-permute-start(bf16[1536,512]{1,0:T(8,128)(2,1)} %get-tuple-element.378), channel_id=1, source_target_pairs={{0,0},{1,4},{2,2},{3,6},{4,1},{5,5},{6,3},{7,7},{8,8},{9,12},{10,1... | collective-permute-start | bytes 4718600 | tf_op jit(solution)/shard_map/ppermute | solution.py:815
  797.5 33.8 %collective-permute-start.40 = (bf16[1536,512]{1,0:T(8,128)(2,1)}, bf16[1536,512]{1,0:T(8,128)(2,1)}, u32[]{:S(2)}, u32[]{:S(2)}) collective-permute-start(bf16[1536,512]{1,0:T(8,128)(2,1)} %get-tuple-element.379), channel_id=1, source_target_pairs={{0,1},{1,5},{2,3},{3,7},{4,0},{5,4},{6,2},{7,6},{8,9},{9,13},{10,1... | collective-permute-start | bytes 4718600 | tf_op jit(solution)/shard_map/ppermute | solution.py:815
  797.5 33.8 %collective-permute-start.41 = (bf16[1536,512]{1,0:T(8,128)(2,1)}, bf16[1536,512]{1,0:T(8,128)(2,1)}, u32[]{:S(2)}, u32[]{:S(2)}) collective-permute-start(bf16[1536,512]{1,0:T(8,128)(2,1)} %get-tuple-element.380), channel_id=1, source_target_pairs={{0,2},{1,6},{2,0},{3,4},{4,3},{5,7},{6,1},{7,5},{8,10},{9,14},{10,... | collective-permute-start | bytes 4718600 | tf_op jit(solution)/shard_map/ppermute | solution.py:815
  799.0 68.8 %collective-permute-start.42 = (bf16[1536,512]{1,0:T(8,128)(2,1)}, bf16[1536,512]{1,0:T(8,128)(2,1)}, u32[]{:S(2)}, u32[]{:S(2)}) collective-permute-start(bf16[1536,512]{1,0:T(8,128)(2,1)} %get-tuple-element.381), channel_id=1, source_target_pairs={{0,3},{1,7},{2,1},{3,5},{4,2},{5,6},{6,0},{7,4},{8,11},{9,15},{10,... | collective-permute-start | bytes 4718600 | tf_op jit(solution)/shard_map/ppermute | solution.py:815
  808.3 65.1 %collective-permute-start.43 = (bf16[512,768]{1,0:T(8,128)(2,1)}, bf16[512,768]{1,0:T(8,128)(2,1)S(1)}, u32[]{:S(2)}, u32[]{:S(2)}) collective-permute-start(bf16[512,768]{1,0:T(8,128)(2,1)} %reduce-scatter.9.cloned.1.call-done), channel_id=1, source_target_pairs={{0,4},{4,0},{1,5},{5,1},{2,6},{6,2},{3,7},{7,3},{8,12},{12,8},{9,1... | collective-permute-start | bytes 2359304 | tf_op jit(solution)/shard_map/ppermute | solution.py:969
  (34 other events, 405.2 us)
Sparse Core Ops, SparseCore 0:
  10.2 66.1 all-gather.4
  87.0 28.3 all-gather.6
  160.0 116.0 all-gather.8
  277.5 113.5 all-gather.10
  426.7 108.5 reduce-scatter.4
  582.4 121.5 reduce-scatter.6
  747.3 60.3 reduce-scatter.8
  810.5 27.1 reduce-scatter.10

commit v4 on v3

--- a/solution.py
+++ b/solution.py
@@ -973,14 +973,19 @@
         return jnp.where(here, mine, other), jnp.where(here, other, mine)
 
     lefts = (grad_rows, hidden2)
-    total0 = halves(lefts, (act_own, d_own), (act_oth, d_oth))
-    share0 = reduce_rows(total0)
+    rights0, other0 = (act_own, d_own), grads(lefts, (act_oth, d_oth))
 
     oth1 = plane.pair(after(own1, act_own))
-    own1, oth1 = fence(own1, oth1, total0)[:2]
+    other0, oth1 = fence(other0, oth1)
+    other0 = plane.pair(other0)
     totals, sent, shared = {}, [], None
     for at, j in enumerate(list(range(ranks - 1, 0, -1)) + [0]):
         piece = pieces[j]
+        if at == 1:
+            rights0 = after(rights0, totals[ranks - 1])
+            total0 = grads(lefts, rights0, other0)
+            share0 = reduce_rows(total0)
+            piece = after(piece, total0)
         if at > 2:
             piece, sent[at - 3] = fence(piece, sent[at - 3])
         totals[j], shared = feed_forward(

time: 901 us -> 897 us (level)
    ppermute x8, waiting for transfers between devices: 18.6 us -> 8.53 us  [pair(): return lax.ppermute(value, 'tp', perm)]
  transfers between devices with their start and end apart: 53 -> 53, of which waited for: 27 -> 26; matrix products, arithmetic and copies ran while one was open for 7% -> 7% of each run, Pallas kernels for 46% -> 45%
where the time goes in v4:
time: 897 us; the launch traced here: 886 us
  Pallas kernels  418 us (47%)
  waiting for transfers between devices  302 us (34%)
  starting transfers between devices  81.8 us (9%)
  other arithmetic  42.4 us (5%)
  local copies, waits for them, and re-layouts  26.4 us (3%)
  between operations  15.2 us (2%)
    pallas_call x8, Pallas kernels, feed_forward(): pl.pallas_call(functools.partial(ffn_kernel, first_half, len(starts) == 1...  158 us
    ppermute x14, waiting for transfers between devices, swap(): return lax.ppermute(value, PLANE, self.perm(move))  119 us
    pallas_call x8, Pallas kernels, grads(): pl.pallas_call(functools.partial(grads_kernel, len(lefts)), grid=(width /...  95.5 us
    ppermute x4, waiting for transfers between devices, spread_rows(): got.append((place, lax.ppermute(block, PLANE, self.perm(move))))  62.2 us
    ppermute x4, waiting for transfers between devices, collect_blocks(): return [lax.ppermute(p, PLANE, self.perm(m)) for p, m in zip(pieces, moves)]  45.8 us
    ppermute x2, waiting for transfers between devices, sum_pairs(): lax.ppermute(pieces[jh * self.nc + jk], PLANE, self.perm(lambda c, h, k,...  32.7 us
    pallas_call x1, Pallas kernels, attend_back(): pl.pallas_call(attend_back_kernel, grid_spec=pltpu.PrefetchScalarGridSpec...  31.4 us
    pallas_call x2, Pallas kernels, attend(): pl.pallas_call(functools.partial(attend_kernel, late, base), grid_spec=pl...  27.6 us
  transfers between devices with their start and end apart: 53, of which 26 were waited for; matrix products, arithmetic and copies ran while one was open for 7% of the time, Pallas kernels for 45%

profile of v4, /device:TPU:0, one launch (start us, length us, event | category | flops | bytes accessed | tf_op | source)
XLA Modules:
  0.0 885.6 jit_solution(17971606347654456628)
XLA Ops:
  16.7 6.2 fusion
  22.9 23.1 %collective-permute-done.1.refs_1_ = bf16[1536,512]{1,0:T(8,128)(2,1)S(1)} collective-permute-done((bf16[1536,512]{1,0:T(8,128)(2,1)}, bf16[1536,512]{1,0:T(8,128)(2,1)S(1)}, u32[]{:S(2)}, u32[]{:S(2)}) %collective-permute-start.1) | collective-permute-done | bytes 1572896 | tf_op jit(solution)/shard_map/ppermute | solution.py:790
  46.0 36.9 %collective-permute-done.3.refs_3_ = bf16[1536,512]{1,0:T(8,128)(2,1)} collective-permute-done((bf16[1536,512]{1,0:T(8,128)(2,1)}, bf16[1536,512]{1,0:T(8,128)(2,1)}, u32[]{:S(2)}, u32[]{:S(2)}) %collective-permute-start.3) | collective-permute-done | bytes 1572896 | tf_op jit(solution)/shard_map/ppermute | solution.py:790
  92.7 21.2 %norm_project.1 = (bf16[1536,2048]{1,0:T(8,128)(2,1)}, bf16[1536,2048]{1,0:T(8,128)(2,1)}, bf16[1536,512]{1,0:T(8,128)(2,1)}, bf16[1536,512]{1,0:T(8,128)(2,1)},...) custom-call(s32[4]{0:T(128)} %pad_add_fusion.table, bf16[1536,512]{1,0:T(8,128)(2,1)} %copy-done.17, ...), custom_call_target="tpu_custom_call" | custom-call | flops 600000000 | bytes 1 | tf_op jit(solution)/shard_map/norm_project/pallas_call | solution.py:103
  116.4 13.3 %collective-permute-start.8 = (bf16[1536,512]{1,0:T(8,128)(2,1)}, bf16[1536,512]{1,0:T(8,128)(2,1)}, u32[]{:S(2)}, u32[]{:S(2)}) collective-permute-start(bf16[1536,512]{1,0:T(8,128)(2,1)} %param.12), channel_id=1, source_target_pairs={{0,0},{1,4},{2,2},{3,6},{4,1},{5,5},{6,3},{7,7},{8,8},{9,12},{10,1... | collective-permute-start | bytes 4718600 | tf_op jit(solution)/shard_map/ppermute | solution.py:798
  132.8 9.5 %attend_late.1 = (bf16[1536,512]{1,0:T(8,128)(2,1)}, f32[4,1536,1]{2,1,0:T(8,128)}) custom-call(s32[6]{0:T(128)} %subtract_add_fusion.need, bf16[1536,512]{1,0:T(8,128)(2,1)} %get-tuple-element.212.q_ref, bf16[1536,512]{1,0:T(8,128)(2,1)} %get-tuple-element.213.k_ref, bf16[1536,512]{1,0:T(8,128)(2,1)} %get-tuple-element.214.v_ref, ...), custom_call_target="tpu_custom_call" | custom-call | flops 300000000 | bytes 1 | tf_op jit(solution)/shard_map/attend_late/pallas_call | solution.py:250
  142.3 6.6 collective-permute-done.9.refs_1_
  148.9 7.3 collective-permute-done.7
  162.7 18.2 %attend_early.1 = (bf16[1536,512]{1,0:T(8,128)(2,1)}, f32[4,1536,1]{2,1,0:T(8,128)}) custom-call(s32[6]{0:T(128)} %subtract_add_fusion.need, bf16[1536,512]{1,0:T(8,128)(2,1)} %get-tuple-element.212.q_ref, bf16[1536,512]{1,0:T(8,128)(2,1)} %get-tuple-element.213.k_ref, ...), custom_call_target="tpu_custom_call", output_to_operand_aliasing={{0}: (7, {}), {1}: (8, {})} | custom-call | flops 600000000 | bytes 1 | tf_op jit(solution)/shard_map/attend_early/pallas_call | solution.py:250
  180.9 10.6 %output_shares.1 = (bf16[1536,512]{1,0:T(8,128)(2,1)}, f32[384,2048]{1,0:T(8,128)}, bf16[384,2048]{1,0:T(8,128)(2,1)}, bf16[384,2048]{1,0:T(8,128)(2,1)}, bf16[384,2048]{1,0:T(8,128)(2,1)}) custom-call(s32[4]{0:T(128)} %pad_add_fusion.1.table, bf16[1536,512]{1,0:T(8,128)(2,1)} %get-tuple-element.233.m_ref, ...), custom_call_target="tpu_custom_call" | custom-call | flops 210000000 | bytes 1 | tf_op jit(solution)/shard_map/output_shares/pallas_call | solution.py:599
  197.2 11.5 %collective-permute-start.12 = (bf16[384,2048]{1,0:T(8,128)(2,1)}, bf16[384,2048]{1,0:T(8,128)(2,1)S(1)}, u32[]{:S(2)}, u32[]{:S(2)}) collective-permute-start(bf16[384,2048]{1,0:T(8,128)(2,1)} %get-tuple-element.245), channel_id=1, source_target_pairs={{0,6},{1,7},{2,4},{3,5},{4,2},{5,3},{6,0},{7,1},{8,14},{9,15},{10,... | collective-permute-start | bytes 4718600 | tf_op jit(solution)/shard_map/ppermute | solution.py:840
  209.9 6.5 join.1.g_ref.refs_0_
  216.5 27.4 %collective-permute-done.12.refs_0_ = bf16[384,2048]{1,0:T(8,128)(2,1)S(1)} collective-permute-done((bf16[384,2048]{1,0:T(8,128)(2,1)}, bf16[384,2048]{1,0:T(8,128)(2,1)S(1)}, u32[]{:S(2)}, u32[]{:S(2)}) %collective-permute-start.12) | collective-permute-done | bytes 1572896 | tf_op jit(solution)/shard_map/ppermute | solution.py:840
  243.8 32.6 %collective-permute-done.13.refs_1_ = bf16[384,2048]{1,0:T(8,128)(2,1)S(1)} collective-permute-done((bf16[384,2048]{1,0:T(8,128)(2,1)}, bf16[384,2048]{1,0:T(8,128)(2,1)S(1)}, u32[]{:S(2)}, u32[]{:S(2)}) %collective-permute-start.13) | collective-permute-done | bytes 1572896 | tf_op jit(solution)/shard_map/ppermute | solution.py:840
  278.0 7.3 norm_chunk.1
  288.8 19.5 %feed_forward.8 = (f32[384,2048]{1,0:T(8,128)}, bf16[1536,512]{1,0:T(8,128)(2,1)}, bf16[1536,512]{1,0:T(8,128)(2,1)}, bf16[1536,1024]{1,0:T(8,128)(2,1)}, bf16[1...) custom-call(s32[1]{0:T(128)} %bitcast.6.table, bf16[384,2048]{1,0:T(8,128)(2,1)} %get-tuple-element.290.h_ref, ...), custom_call_target="tpu_custom_call" | custom-call | flops 600000000 | bytes 1 | tf_op jit(solution)/shard_map/feed_forward/pallas_call | solution.py:475
  308.3 14.1 %collective-permute-done.16.h_ref = bf16[384,2048]{1,0:T(8,128)(2,1)S(1)} collective-permute-done((bf16[384,2048]{1,0:T(8,128)(2,1)}, bf16[384,2048]{1,0:T(8,128)(2,1)S(1)}, u32[]{:S(2)}, u32[]{:S(2)}) %collective-permute-start.16) | collective-permute-done | bytes 1572896 | tf_op jit(solution)/shard_map/ppermute | solution.py:840
  327.6 18.8 %feed_forward.9 = (f32[384,2048]{1,0:T(8,128)}, bf16[1536,512]{1,0:T(8,128)(2,1)}, bf16[1536,512]{1,0:T(8,128)(2,1)}, bf16[1536,1024]{1,0:T(8,128)(2,1)}, bf16[1...) custom-call(s32[1]{0:T(128)} %bitcast.7.table, ...), custom_call_target="tpu_custom_call", output_to_operand_aliasing={{1}: (5, {}), {2}: (6, {}), {3}: (7, {}), {4}: (8, {}), {6}... | custom-call | flops 600000000 | bytes 1 | tf_op jit(solution)/shard_map/feed_forward/pallas_call | solution.py:475
  346.4 19.0 %feed_forward.10 = (f32[384,2048]{1,0:T(8,128)}, bf16[1536,512]{1,0:T(8,128)(2,1)}, bf16[1536,512]{1,0:T(8,128)(2,1)}, bf16[1536,1024]{1,0:T(8,128)(2,1)}, bf16[...) custom-call(s32[1]{0:T(128)} %bitcast.8.table, ...), custom_call_target="tpu_custom_call", output_to_operand_aliasing={{1}: (5, {}), {2}: (6, {}), {3}: (7, {}), {4}: (8, {}), {6}... | custom-call | flops 600000000 | bytes 1 | tf_op jit(solution)/shard_map/feed_forward/pallas_call | solution.py:475
  367.9 18.6 %feed_forward.11 = (f32[384,2048]{1,0:T(8,128)}, bf16[1536,512]{1,0:T(8,128)(2,1)}, bf16[1536,512]{1,0:T(8,128)(2,1)}, bf16[1536,1024]{1,0:T(8,128)(2,1)}, bf16[...) custom-call(s32[1]{0:T(128)} %bitcast.9.table, ...), custom_call_target="tpu_custom_call", output_to_operand_aliasing={{1}: (5, {}), {2}: (6, {}), {3}: (7, {}), {4}: (8, {}), {6}... | custom-call | flops 600000000 | bytes 1 | tf_op jit(solution)/shard_map/feed_forward/pallas_call | solution.py:475
  386.5 4.5 all-gather.11.cloned.1.call-done.own_ref
  391.1 15.0 %grads.8 = bf16[2048,1536]{1,0:T(8,128)(2,1)} custom-call(bf16[1536,2048]{1,0:T(8,128)(2,1)} %join.1.g_ref.refs_0_, bf16[1536,2048]{1,0:T(8,128)(2,1)} %get-tuple-element.281.refs_1_, bf16[1536,512]{1,0:T(8,128)(2,1)} %get-tuple-element.282.refs_2_, bf16[1536,1024]{1,0:T(8,128)(2,1)} %get-tuple-element.283.refs_3_), custom_call_target="tpu_custom_call" | custom-call | flops 300000000 | bytes 1 | tf_op jit(solution)/shard_map/grads/pallas_call | solution.py:748
  407.2 20.3 %feed_forward.12 = (bf16[384,2048]{1,0:T(8,128)(2,1)}, bf16[1536,512]{1,0:T(8,128)(2,1)}, bf16[1536,512]{1,0:T(8,128)(2,1)}, bf16[1536,1024]{1,0:T(8,128)(2,1)},...) custom-call(s32[5]{0:T(128)} %stack.42.table, ...), custom_call_target="tpu_custom_call" | custom-call | flops 600000000 | bytes 1 | tf_op jit(solution)/shard_map/feed_forward/pallas_call | solution.py:475
  427.5 16.4 %grads.9 = bf16[2048,1536]{1,0:T(8,128)(2,1)} custom-call(bf16[1536,2048]{1,0:T(8,128)(2,1)} %join.1.g_ref.refs_0_, bf16[1536,2048]{1,0:T(8,128)(2,1)} %get-tuple-element.281.refs_1_, bf16[1536,512]{1,0:T(8,128)(2,1)} %get-tuple-element.295.refs_2_, bf16[1536,1024]{1,0:T(8,128)(2,1)} %get-tuple-element.296.refs_3_, ...), custom_call_target="tpu_custom_call" | custom-call | flops 300000000 | bytes 1 | tf_op jit(solution)/shard_map/grads/pallas_call | solution.py:748
  447.4 20.5 %feed_forward.13 = (bf16[384,2048]{1,0:T(8,128)(2,1)}, bf16[1536,512]{1,0:T(8,128)(2,1)}, bf16[1536,512]{1,0:T(8,128)(2,1)}, bf16[1536,1024]{1,0:T(8,128)(2,1)},...) custom-call(s32[5]{0:T(128)} %stack.44.table, ...), custom_call_target="tpu_custom_call", output_to_operand_aliasing={{1}: (7, {}), {2}: (8, {}), {3}: (9, {}), {4}: (10, {}), {5... | custom-call | flops 600000000 | bytes 1 | tf_op jit(solution)/shard_map/feed_forward/pallas_call | solution.py:475
  469.3 20.5 %feed_forward.14 = (bf16[384,2048]{1,0:T(8,128)(2,1)}, bf16[1536,512]{1,0:T(8,128)(2,1)}, bf16[1536,512]{1,0:T(8,128)(2,1)}, bf16[1536,1024]{1,0:T(8,128)(2,1)},...) custom-call(s32[5]{0:T(128)} %stack.43.table, ...), custom_call_target="tpu_custom_call", output_to_operand_aliasing={{1}: (7, {}), {2}: (8, {}), {3}: (9, {}), {4}: (10, {}), {5... | custom-call | flops 600000000 | bytes 1 | tf_op jit(solution)/shard_map/feed_forward/pallas_call | solution.py:475
  491.1 20.7 %feed_forward.15 = (f32[384,2048]{1,0:T(8,128)}, bf16[1536,512]{1,0:T(8,128)(2,1)}, bf16[1536,512]{1,0:T(8,128)(2,1)}, bf16[1536,1024]{1,0:T(8,128)(2,1)}, bf16[...) custom-call(s32[5]{0:T(128)} %stack.41.table, ...), custom_call_target="tpu_custom_call", output_to_operand_aliasing={{1}: (7, {}), {2}: (8, {}), {3}: (9, {}), {4}: (10, {}), {5... | custom-call | flops 600000000 | bytes 1 | tf_op jit(solution)/shard_map/feed_forward/pallas_call | solution.py:475
  511.8 4.5 collective-permute-done.24.refs_1_
  516.3 15.7 %grads.10 = bf16[2048,1536]{1,0:T(8,128)(2,1)} custom-call(bf16[1536,2048]{1,0:T(8,128)(2,1)} %join.1.g_ref.refs_0_, bf16[1536,2048]{1,0:T(8,128)(2,1)} %get-tuple-element.281.refs_1_, bf16[1536,512]{1,0:T(8,128)(2,1)} %get-tuple-element.329.refs_2_, bf16[1536,1024]{1,0:T(8,128)(2,1)} %get-tuple-element.330.refs_3_), custom_call_target="tpu_custom_call" | custom-call | flops 300000000 | bytes 1 | tf_op jit(solution)/shard_map/grads/pallas_call | solution.py:748
  532.1 8.4 back_chunk.1
  542.6 16.5 %grads.11 = bf16[2048,1536]{1,0:T(8,128)(2,1)} custom-call(bf16[1536,2048]{1,0:T(8,128)(2,1)} %join.1.g_ref.refs_0_, bf16[1536,2048]{1,0:T(8,128)(2,1)} %get-tuple-element.281.refs_1_, bf16[1536,512]{1,0:T(8,128)(2,1)} %get-tuple-element.338.refs_2_, bf16[1536,1024]{1,0:T(8,128)(2,1)} %get-tuple-element.339.refs_3_, ...), custom_call_target="tpu_custom_call" | custom-call | flops 300000000 | bytes 1 | tf_op jit(solution)/shard_map/grads/pallas_call | solution.py:748
  559.1 18.3 %collective-permute-done.26.refs_2_ = bf16[384,2048]{1,0:T(8,128)(2,1)S(1)} collective-permute-done((bf16[384,2048]{1,0:T(8,128)(2,1)}, bf16[384,2048]{1,0:T(8,128)(2,1)S(1)}, u32[]{:S(2)}, u32[]{:S(2)}) %collective-permute-start.26) | collective-permute-done | bytes 1572896 | tf_op jit(solution)/shard_map/ppermute | solution.py:840
  581.4 17.3 %collective-permute-done.29 = bf16[192,2048]{1,0:T(8,128)(2,1)S(1)} collective-permute-done((bf16[192,2048]{1,0:T(8,128)(2,1)S(1)}, bf16[192,2048]{1,0:T(8,128)(2,1)S(1)}, u32[]{:S(2)}, u32[]{:S(2)}) %collective-permute-start.29) | collective-permute-done | bytes 786464 | tf_op jit(solution)/shard_map/ppermute | solution.py:840
  600.4 10.2 %dmixed.1 = (bf16[1536,2048]{1,0:T(8,128)(2,1)}, bf16[1536,512]{1,0:T(8,128)(2,1)}) custom-call(s32[4]{0:T(128)} %pad_add_fusion.1.table, bf16[384,2048]{1,0:T(8,128)(2,1)} %get-tuple-element.335.refs_0_, bf16[384,2048]{1,0:T(8,128)(2,1)} %copy-done.10, bf16[384,2048]{1,0:T(8,128)(2,1)} %copy-done.9, bf16[384,2048]{1,0:T(8,128)(2,1)} %pad_maximum_fusion.refs_3_, ...), custom_call_target="tpu_custom_call" | custom-call | flops 210000000 | bytes 1 | tf_op jit(solution)/shard_map/dmixed/pallas_call | solution.py:641
  613.7 31.4 %attend_back.1 = (bf16[1536,512]{1,0:T(8,128)(2,1)}, f32[1536,512]{1,0:T(8,128)}, f32[1536,512]{1,0:T(8,128)}, bf16[2,1024,512]{2,1,0:T(8,128)(2,1)}) custom-call(s32[6]{0:T(128)} %subtract_add_fusion.need, bf16[1536,512]{1,0:T(8,128)(2,1)} %get-tuple-element.212.q_ref, bf16[1536,512]{1,0:T(8,128)(2,1)} %get-tuple-element.213.k_ref, ...), custom_call_target="tpu_custom_call" | custom-call | flops 1290000000 | bytes 1 | tf_op jit(solution)/shard_map/attend_back/pallas_call | solution.py:325
  648.1 31.0 %collective-permute-done.31 = bf16[1536,512]{1,0:T(8,128)(2,1)} collective-permute-done((bf16[1536,512]{1,0:T(8,128)(2,1)}, bf16[1536,512]{1,0:T(8,128)(2,1)}, u32[]{:S(2)}, u32[]{:S(2)}) %collective-permute-start.31) | collective-permute-done | bytes 1572896 | tf_op jit(solution)/shard_map/ppermute | solution.py:819
  688.7 6.1 grads.12
  697.8 6.6 grads.13
  704.4 7.8 finish_attention.1
  712.2 9.1 %grads.14 = bf16[2048,768]{1,0:T(8,128)(2,1)} custom-call(bf16[1536,2048]{1,0:T(8,128)(2,1)} %get-tuple-element.210.refs_0_, bf16[1536,768]{1,0:T(8,128)(2,1)} %get-tuple-element.376.refs_1_.d_oth), custom_call_target="tpu_custom_call" | custom-call | flops 300000000 | bytes 1 | tf_op jit(solution)/shard_map/grads/pallas_call | solution.py:748
  732.4 10.1 %grads.15 = bf16[2048,768]{1,0:T(8,128)(2,1)} custom-call(bf16[1536,2048]{1,0:T(8,128)(2,1)} %get-tuple-element.210.refs_0_, bf16[1536,768]{1,0:T(8,128)(2,1)} %get-tuple-element.375.refs_1_.d_own, bf16[2048,768]{1,0:T(8,128)(2,1)} %copy-done.11), custom_call_target="tpu_custom_call" | custom-call | flops 300000000 | bytes 1 | tf_op jit(solution)/shard_map/grads/pallas_call | solution.py:748
  749.0 23.4 %input_parts.1 = (bf16[1536,512]{1,0:T(8,128)(2,1)}, bf16[1536,512]{1,0:T(8,128)(2,1)}, bf16[1536,512]{1,0:T(8,128)(2,1)}, bf16[1536,512]{1,0:T(8,128)(2,1)}) custom-call(s32[5]{0:T(128)} %stack.41.table, bf16[1536,768]{1,0:T(8,128)(2,1)} %get-tuple-element.375.refs_1_.d_own, bf16[1536,768]{1,0:T(8,128)(2,1)} %get-tuple-element.376.refs_1_.d_oth, ...), custom_call_target="tpu_custom_call" | custom-call | flops 600000000 | bytes 1 | tf_op jit(solution)/shard_map/input_parts/pallas_call | solution.py:557
  772.5 7.2 collective-permute-done.38
  779.7 13.3 %collective-permute-start.39 = (bf16[1536,512]{1,0:T(8,128)(2,1)}, bf16[1536,512]{1,0:T(8,128)(2,1)}, u32[]{:S(2)}, u32[]{:S(2)}) collective-permute-start(bf16[1536,512]{1,0:T(8,128)(2,1)} %get-tuple-element.384), channel_id=1, source_target_pairs={{0,0},{1,4},{2,2},{3,6},{4,1},{5,5},{6,3},{7,7},{8,8},{9,12},{10,1... | collective-permute-start | bytes 4718600 | tf_op jit(solution)/shard_map/ppermute | solution.py:815
  817.4 9.3 %collective-permute-done.40 = bf16[1536,512]{1,0:T(8,128)(2,1)} collective-permute-done((bf16[1536,512]{1,0:T(8,128)(2,1)}, bf16[1536,512]{1,0:T(8,128)(2,1)}, u32[]{:S(2)}, u32[]{:S(2)}) %collective-permute-start.40) | collective-permute-done | bytes 1572896 | tf_op jit(solution)/shard_map/ppermute | solution.py:815
  826.7 36.5 %collective-permute-done.42 = bf16[1536,512]{1,0:T(8,128)(2,1)} collective-permute-done((bf16[1536,512]{1,0:T(8,128)(2,1)}, bf16[1536,512]{1,0:T(8,128)(2,1)}, u32[]{:S(2)}, u32[]{:S(2)}) %collective-permute-start.42) | collective-permute-done | bytes 1572896 | tf_op jit(solution)/shard_map/ppermute | solution.py:815
  863.2 5.6 collective-permute-done.43
  870.1 4.8 add_convert_fusion
  (221 shorter events, 131.3 us)
Async XLA Ops:
  7.2 77.9 %all-gather.5.cloned.1.call-start = ((), (), s32[]{:S(2)}) async-start(), calls=%async_computation.4 | async-start | bytes 3932160 | tf_op jit(solution)/shard_map/all_gather | solution.py:887
  9.3 121.6 %all-gather.7.cloned.1.call-start = ((), (), s32[]{:S(2)}) async-start(), calls=%async_computation.5 | async-start | bytes 1310720 | tf_op jit(solution)/shard_map/all_gather | solution.py:887
  9.4 36.7 %collective-permute-start.1 = (bf16[1536,512]{1,0:T(8,128)(2,1)}, bf16[1536,512]{1,0:T(8,128)(2,1)S(1)}, u32[]{:S(2)}, u32[]{:S(2)}) collective-permute-start(bf16[1536,512]{1,0:T(8,128)(2,1)} %param.11), channel_id=1, source_target_pairs={{0,4},{1,0},{2,6},{3,2},{4,5},{5,1},{6,7},{7,3},{8,12},{9,8},{10,1... | collective-permute-start | bytes 4718600 | tf_op jit(solution)/shard_map/ppermute | solution.py:790
  12.3 33.7 %collective-permute-start = (bf16[1536,512]{1,0:T(8,128)(2,1)}, bf16[1536,512]{1,0:T(8,128)(2,1)S(1)}, u32[]{:S(2)}, u32[]{:S(2)}) collective-permute-start(bf16[1536,512]{1,0:T(8,128)(2,1)} %param.11), channel_id=1, source_target_pairs={{0,0},{1,4},{2,2},{3,6},{4,1},{5,5},{6,3},{7,7},{8,8},{9,12},{10,1... | collective-permute-start | bytes 4718600 | tf_op jit(solution)/shard_map/ppermute | solution.py:790
  14.4 68.6 %collective-permute-start.3 = (bf16[1536,512]{1,0:T(8,128)(2,1)}, bf16[1536,512]{1,0:T(8,128)(2,1)}, u32[]{:S(2)}, u32[]{:S(2)}) collective-permute-start(bf16[1536,512]{1,0:T(8,128)(2,1)} %param.11), channel_id=1, source_target_pairs={{0,6},{1,2},{2,4},{3,0},{4,7},{5,3},{6,5},{7,1},{8,14},{9,10},{10,... | collective-permute-start | bytes 4718600 | tf_op jit(solution)/shard_map/ppermute | solution.py:790
  15.9 69.2 %collective-permute-start.2 = (bf16[1536,512]{1,0:T(8,128)(2,1)}, bf16[1536,512]{1,0:T(8,128)(2,1)}, u32[]{:S(2)}, u32[]{:S(2)}) collective-permute-start(bf16[1536,512]{1,0:T(8,128)(2,1)} %param.11), channel_id=1, source_target_pairs={{0,2},{1,6},{2,0},{3,4},{4,3},{5,7},{6,1},{7,5},{8,10},{9,14},{10,... | collective-permute-start | bytes 4718600 | tf_op jit(solution)/shard_map/ppermute | solution.py:790
  86.9 191.0 %all-gather.9.cloned.1.call-start = ((), (), s32[]{:S(2)}) async-start(), calls=%async_computation.6 | async-start | bytes 7864320 | tf_op jit(solution)/shard_map/all_gather | solution.py:887
  113.9 42.4 %collective-permute-start.5 = (bf16[1024,1024]{1,0:T(8,128)(2,1)}, bf16[1024,1024]{1,0:T(8,128)(2,1)S(1)}, u32[]{:S(2)}, u32[]{:S(2)}) collective-permute-start(bf16[1024,1024]{1,0:T(8,128)(2,1)} %get-tuple-element.215), channel_id=1, source_target_pairs={{0,1},{1,8},{2,3},{3,10},{8,9},{9,16},{10,11},{11,18},{16,17},{17,... | collective-permute-start | bytes 6291464 | tf_op jit(solution)/shard_map/ppermute | solution.py:923
  116.1 32.8 %collective-permute-start.9 = (bf16[1536,512]{1,0:T(8,128)(2,1)}, bf16[1536,512]{1,0:T(8,128)(2,1)}, u32[]{:S(2)}, u32[]{:S(2)}) collective-permute-start(bf16[1536,512]{1,0:T(8,128)(2,1)} %param.12), channel_id=1, source_target_pairs={{0,4},{1,0},{2,6},{3,2},{4,5},{5,1},{6,7},{7,3},{8,12},{9,8},{10,1... | collective-permute-start | bytes 4718600 | tf_op jit(solution)/shard_map/ppermute | solution.py:798
  116.4 32.5 %collective-permute-start.8 = (bf16[1536,512]{1,0:T(8,128)(2,1)}, bf16[1536,512]{1,0:T(8,128)(2,1)}, u32[]{:S(2)}, u32[]{:S(2)}) collective-permute-start(bf16[1536,512]{1,0:T(8,128)(2,1)} %param.12), channel_id=1, source_target_pairs={{0,0},{1,4},{2,2},{3,6},{4,1},{5,5},{6,3},{7,7},{8,8},{9,12},{10,1... | collective-permute-start | bytes 4718600 | tf_op jit(solution)/shard_map/ppermute | solution.py:798
  129.7 26.6 %collective-permute-start.7 = (bf16[1536,512]{1,0:T(8,128)(2,1)}, bf16[1536,512]{1,0:T(8,128)(2,1)}, u32[]{:S(2)}, u32[]{:S(2)}) collective-permute-start(bf16[1536,512]{1,0:T(8,128)(2,1)} %param.12), channel_id=1, source_target_pairs={{0,2},{1,3},{2,0},{3,1},{4,6},{5,7},{6,4},{7,5},{8,10},{9,11},{10,... | collective-permute-start | bytes 4718600 | tf_op jit(solution)/shard_map/ppermute | solution.py:802
  131.0 25.3 %collective-permute-start.6 = (bf16[2048,256]{1,0:T(8,128)(2,1)}, bf16[2048,256]{1,0:T(8,128)(2,1)S(1)}, u32[]{:S(2)}, u32[]{:S(2)}) collective-permute-start(bf16[2048,256]{1,0:T(8,128)(2,1)} %all-gather.7.cloned.1.call-done.w_own.refs_4_), channel_id=1, source_target_pairs={{0,1},{1,0},{2,3},{3,2},{4,5},{5,4},{6,7},{7,6},{8,9},{9,8},{10,11... | collective-permute-start | bytes 3145736 | tf_op jit(solution)/shard_map/ppermute | solution.py:869
  159.8 231.2 %all-gather.11.cloned.1.call-start = ((), (), s32[]{:S(2)}) async-start(), calls=%async_computation.7 | async-start | bytes 7864320 | tf_op jit(solution)/shard_map/all_gather | solution.py:887
  159.8 21.0 %collective-permute-start.10 = (bf16[1536,512]{1,0:T(8,128)(2,1)}, bf16[1536,512]{1,0:T(8,128)(2,1)S(1)}, u32[]{:S(2)}, u32[]{:S(2)}) collective-permute-start(bf16[1536,512]{1,0:T(8,128)(2,1)} %collective-permute-done.7), channel_id=1, source_target_pairs={{0,0},{1,4},{2,2},{3,6},{4,1},{5,5},{6,3},{7,7},{8,8},{9,12},{10,1... | collective-permute-start | bytes 4718600 | tf_op jit(solution)/shard_map/ppermute | solution.py:798
  162.1 32.1 %collective-permute-start.11 = (bf16[1536,512]{1,0:T(8,128)(2,1)}, bf16[1536,512]{1,0:T(8,128)(2,1)S(1)}, u32[]{:S(2)}, u32[]{:S(2)}) collective-permute-start(bf16[1536,512]{1,0:T(8,128)(2,1)} %collective-permute-done.7), channel_id=1, source_target_pairs={{0,4},{1,0},{2,6},{3,2},{4,5},{5,1},{6,7},{7,3},{8,12},{9,8},{10,1... | collective-permute-start | bytes 4718600 | tf_op jit(solution)/shard_map/ppermute | solution.py:798
  197.1 413.4 %reduce-scatter.5.cloned.1.call-start = ((), (), s32[]{:S(2)}) async-start(), calls=%async_computation.8 | async-start | bytes 7864320 | tf_op jit(solution)/shard_map/reduce_scatter | solution.py:966
  197.2 46.7 %collective-permute-start.12 = (bf16[384,2048]{1,0:T(8,128)(2,1)}, bf16[384,2048]{1,0:T(8,128)(2,1)S(1)}, u32[]{:S(2)}, u32[]{:S(2)}) collective-permute-start(bf16[384,2048]{1,0:T(8,128)(2,1)} %get-tuple-element.245), channel_id=1, source_target_pairs={{0,6},{1,7},{2,4},{3,5},{4,2},{5,3},{6,0},{7,1},{8,14},{9,15},{10,... | collective-permute-start | bytes 4718600 | tf_op jit(solution)/shard_map/ppermute | solution.py:840
  208.7 67.8 %collective-permute-start.13 = (bf16[384,2048]{1,0:T(8,128)(2,1)}, bf16[384,2048]{1,0:T(8,128)(2,1)S(1)}, u32[]{:S(2)}, u32[]{:S(2)}) collective-permute-start(bf16[384,2048]{1,0:T(8,128)(2,1)} %get-tuple-element.246), channel_id=1, source_target_pairs={{0,4},{1,5},{2,6},{3,7},{4,0},{5,1},{6,2},{7,3},{8,12},{9,13},{10,... | collective-permute-start | bytes 4718600 | tf_op jit(solution)/shard_map/ppermute | solution.py:840
  208.7 69.2 %collective-permute-start.14 = (bf16[384,2048]{1,0:T(8,128)(2,1)}, bf16[384,2048]{1,0:T(8,128)(2,1)}, u32[]{:S(2)}, u32[]{:S(2)}) collective-permute-start(bf16[384,2048]{1,0:T(8,128)(2,1)} %get-tuple-element.247), channel_id=1, source_target_pairs={{0,2},{1,3},{2,0},{3,1},{4,6},{5,7},{6,4},{7,5},{8,10},{9,11},{10,... | collective-permute-start | bytes 4718600 | tf_op jit(solution)/shard_map/ppermute | solution.py:840
  277.9 11.0 %collective-permute-start.17 = (bf16[2048,1536]{1,0:T(8,128)(2,1)}, bf16[2048,1536]{1,0:T(8,128)(2,1)}, u32[]{:S(2)}, u32[]{:S(2)}) collective-permute-start(bf16[2048,1536]{1,0:T(8,128)(2,1)} %all-gather.9.cloned.1.call-done.own_ref), channel_id=1, source_target_pairs={{0,1},{1,0},{2,3},{3,2},{4,5},{5,4},{6,7},{7,6},{8,9},{9,8},{10,11... | collective-permute-start | bytes 18874376 | tf_op jit(solution)/shard_map/ppermute | solution.py:869
  285.3 37.2 %collective-permute-start.16 = (bf16[384,2048]{1,0:T(8,128)(2,1)}, bf16[384,2048]{1,0:T(8,128)(2,1)S(1)}, u32[]{:S(2)}, u32[]{:S(2)}) collective-permute-start(bf16[384,2048]{1,0:T(8,128)(2,1)} %get-tuple-element.290.h_ref), channel_id=1, source_target_pairs={{0,4},{1,5},{2,6},{3,7},{4,0},{5,1},{6,2},{7,3},{8,12},{9,13},{10,... | collective-permute-start | bytes 4718600 | tf_op jit(solution)/shard_map/ppermute | solution.py:840
  287.3 36.6 %collective-permute-start.15 = (bf16[384,2048]{1,0:T(8,128)(2,1)}, bf16[384,2048]{1,0:T(8,128)(2,1)S(1)}, u32[]{:S(2)}, u32[]{:S(2)}) collective-permute-start(bf16[384,2048]{1,0:T(8,128)(2,1)} %get-tuple-element.290.h_ref), channel_id=1, source_target_pairs={{0,2},{1,3},{2,0},{3,1},{4,6},{5,7},{6,4},{7,5},{8,10},{9,11},{10,... | collective-permute-start | bytes 4718600 | tf_op jit(solution)/shard_map/ppermute | solution.py:840
  325.9 39.5 %collective-permute-start.19 = (bf16[192,2048]{1,0:T(8,128)(2,1)}, bf16[192,2048]{1,0:T(8,128)(2,1)S(1)}, u32[]{:S(2)}, u32[]{:S(2)}) collective-permute-start(bf16[192,2048]{1,0:T(8,128)(2,1)} %slice.101), channel_id=1, source_target_pairs={{0,2},{1,3},{2,0},{3,1},{4,6},{5,7},{6,4},{7,5},{8,10},{9,11},{10,... | collective-permute-start | bytes 2359304 | tf_op jit(solution)/shard_map/ppermute | solution.py:840
  327.2 38.3 %collective-permute-start.18 = (bf16[192,2048]{1,0:T(8,128)(2,1)}, bf16[192,2048]{1,0:T(8,128)(2,1)}, u32[]{:S(2)}, u32[]{:S(2)}) collective-permute-start(bf16[192,2048]{1,0:T(8,128)(2,1)} %slice.100), channel_id=1, source_target_pairs={{0,4},{1,5},{2,6},{3,7},{4,0},{5,1},{6,2},{7,3},{8,12},{9,13},{10,... | collective-permute-start | bytes 2359304 | tf_op jit(solution)/shard_map/ppermute | solution.py:840
  391.0 15.1 %collective-permute-start.20 = (bf16[2048,1536]{1,0:T(8,128)(2,1)}, bf16[2048,1536]{1,0:T(8,128)(2,1)}, u32[]{:S(2)}, u32[]{:S(2)}) collective-permute-start(bf16[2048,1536]{1,0:T(8,128)(2,1)} %all-gather.11.cloned.1.call-done.own_ref), channel_id=1, source_target_pairs={{0,1},{1,0},{2,3},{3,2},{4,5},{5,4},{6,7},{7,6},{8,9},{9,8},{10,11... | collective-permute-start | bytes 18874376 | tf_op jit(solution)/shard_map/ppermute | solution.py:869
  406.1 21.3 %collective-permute-start.22 = (bf16[2048,1536]{1,0:T(8,128)(2,1)}, bf16[2048,1536]{1,0:T(8,128)(2,1)}, u32[]{:S(2)}, u32[]{:S(2)}) collective-permute-start(bf16[2048,1536]{1,0:T(8,128)(2,1)} %grads.8), channel_id=1, source_target_pairs={{0,1},{1,0},{2,3},{3,2},{4,5},{5,4},{6,7},{7,6},{8,9},{9,8},{10,11... | collective-permute-start | bytes 18874376 | tf_op jit(solution)/shard_map/ppermute | solution.py:869
  443.8 298.8 %reduce-scatter.7.cloned.1.call-start = ((), (), s32[]{:S(2)}) async-start(), calls=%async_computation.9 | async-start | bytes 7864320 | tf_op jit(solution)/shard_map/reduce_scatter | solution.py:966
  445.1 46.0 %collective-permute-start.21 = (bf16[384,2048]{1,0:T(8,128)(2,1)}, bf16[384,2048]{1,0:T(8,128)(2,1)S(1)}, u32[]{:S(2)}, u32[]{:S(2)}) collective-permute-start(bf16[384,2048]{1,0:T(8,128)(2,1)} %get-tuple-element.289), channel_id=1, source_target_pairs={{0,6},{1,7},{2,4},{3,5},{4,2},{5,3},{6,0},{7,1},{8,14},{9,15},{10,... | collective-permute-start | bytes 4718600 | tf_op jit(solution)/shard_map/ppermute | solution.py:840
  467.9 48.4 %collective-permute-start.24 = (bf16[384,2048]{1,0:T(8,128)(2,1)}, bf16[384,2048]{1,0:T(8,128)(2,1)S(1)}, u32[]{:S(2)}, u32[]{:S(2)}) collective-permute-start(bf16[384,2048]{1,0:T(8,128)(2,1)} %get-tuple-element.328), channel_id=1, source_target_pairs={{0,4},{1,5},{2,6},{3,7},{4,0},{5,1},{6,2},{7,3},{8,12},{9,13},{10,... | collective-permute-start | bytes 4718600 | tf_op jit(solution)/shard_map/ppermute | solution.py:840
  489.8 42.2 %collective-permute-start.23 = (bf16[384,2048]{1,0:T(8,128)(2,1)}, bf16[384,2048]{1,0:T(8,128)(2,1)}, u32[]{:S(2)}, u32[]{:S(2)}) collective-permute-start(bf16[384,2048]{1,0:T(8,128)(2,1)} %get-tuple-element.325), channel_id=1, source_target_pairs={{0,2},{1,3},{2,0},{3,1},{4,6},{5,7},{6,4},{7,5},{8,10},{9,11},{10,... | collective-permute-start | bytes 4718600 | tf_op jit(solution)/shard_map/ppermute | solution.py:840
  540.5 36.9 %collective-permute-start.26 = (bf16[384,2048]{1,0:T(8,128)(2,1)}, bf16[384,2048]{1,0:T(8,128)(2,1)S(1)}, u32[]{:S(2)}, u32[]{:S(2)}) collective-permute-start(bf16[384,2048]{1,0:T(8,128)(2,1)} %get-tuple-element.335.refs_0_), channel_id=1, source_target_pairs={{0,4},{1,5},{2,6},{3,7},{4,0},{5,1},{6,2},{7,3},{8,12},{9,13},{10,... | collective-permute-start | bytes 4718600 | tf_op jit(solution)/shard_map/ppermute | solution.py:840
  541.9 36.7 %collective-permute-start.25 = (bf16[384,2048]{1,0:T(8,128)(2,1)}, bf16[384,2048]{1,0:T(8,128)(2,1)S(1)}, u32[]{:S(2)}, u32[]{:S(2)}) collective-permute-start(bf16[384,2048]{1,0:T(8,128)(2,1)} %get-tuple-element.335.refs_0_), channel_id=1, source_target_pairs={{0,2},{1,3},{2,0},{3,1},{4,6},{5,7},{6,4},{7,5},{8,10},{9,11},{10,... | collective-permute-start | bytes 4718600 | tf_op jit(solution)/shard_map/ppermute | solution.py:840
  578.6 225.1 %reduce-scatter.9.cloned.1.call-start = ((), (), s32[]{:S(2)}) async-start(), calls=%async_computation.10 | async-start | bytes 3932160 | tf_op jit(solution)/shard_map/reduce_scatter | solution.py:966
  579.9 18.8 %collective-permute-start.29 = (bf16[192,2048]{1,0:T(8,128)(2,1)S(1)}, bf16[192,2048]{1,0:T(8,128)(2,1)S(1)}, u32[]{:S(2)}, u32[]{:S(2)}) collective-permute-start(bf16[192,2048]{1,0:T(8,128)(2,1)S(1)} %slice.103), channel_id=1, source_target_pairs={{0,2},{1,3},{2,0},{3,1},{4,6},{5,7},{6,4},{7,5},{8,10},{9,11},{10,... | collective-permute-start | bytes 2359304 | tf_op jit(solution)/shard_map/ppermute | solution.py:840
  580.6 18.5 %collective-permute-start.28 = (bf16[192,2048]{1,0:T(8,128)(2,1)S(1)}, bf16[192,2048]{1,0:T(8,128)(2,1)S(1)}, u32[]{:S(2)}, u32[]{:S(2)}) collective-permute-start(bf16[192,2048]{1,0:T(8,128)(2,1)S(1)} %slice.102), channel_id=1, source_target_pairs={{0,4},{1,5},{2,6},{3,7},{4,0},{5,1},{6,2},{7,3},{8,12},{9,13},{10,... | collective-permute-start | bytes 2359304 | tf_op jit(solution)/shard_map/ppermute | solution.py:840
  610.6 37.5 %collective-permute-start.30 = (bf16[1536,512]{1,0:T(8,128)(2,1)S(1)}, bf16[1536,512]{1,0:T(8,128)(2,1)}, u32[]{:S(2)}, u32[]{:S(2)}) collective-permute-start(bf16[1536,512]{1,0:T(8,128)(2,1)S(1)} %copy-done.3), channel_id=1, source_target_pairs={{0,2},{1,3},{2,0},{3,1},{4,6},{5,7},{6,4},{7,5},{8,10},{9,11},{10,... | collective-permute-start | bytes 4718600 | tf_op jit(solution)/shard_map/ppermute | solution.py:819
  611.9 67.2 %collective-permute-start.31 = (bf16[1536,512]{1,0:T(8,128)(2,1)}, bf16[1536,512]{1,0:T(8,128)(2,1)}, u32[]{:S(2)}, u32[]{:S(2)}) collective-permute-start(bf16[1536,512]{1,0:T(8,128)(2,1)} %get-tuple-element.353), channel_id=1, source_target_pairs={{0,2},{1,3},{2,0},{3,1},{4,6},{5,7},{6,4},{7,5},{8,10},{9,11},{10,... | collective-permute-start | bytes 4718600 | tf_op jit(solution)/shard_map/ppermute | solution.py:819
  612.7 66.4 %collective-permute-start.32 = (bf16[512,1536]{1,0:T(8,128)(2,1)}, bf16[512,1536]{1,0:T(8,128)(2,1)}, u32[]{:S(2)}, u32[]{:S(2)}) collective-permute-start(bf16[512,1536]{1,0:T(8,128)(2,1)} %reduce-scatter.5.cloned.1.call-done), channel_id=1, source_target_pairs={{0,4},{4,0},{1,5},{5,1},{2,6},{6,2},{3,7},{7,3},{8,12},{12,8},{9,1... | collective-permute-start | bytes 4718600 | tf_op jit(solution)/shard_map/ppermute | solution.py:969
  645.1 59.3 %collective-permute-start.33 = (bf16[2,1024,512]{2,1,0:T(8,128)(2,1)}, bf16[2,1024,512]{2,1,0:T(8,128)(2,1)}, u32[]{:S(2)}, u32[]{:S(2)}) collective-permute-start(bf16[2,1024,512]{2,1,0:T(8,128)(2,1)} %get-tuple-element.358), channel_id=1, source_target_pairs={{1,0},{8,1},{3,2},{10,3},{9,8},{16,9},{11,10},{18,11},{17,16},{24,... | collective-permute-start | bytes 6291464 | tf_op jit(solution)/shard_map/ppermute | solution.py:1021
  682.2 39.1 %collective-permute-start.35 = (bf16[1536,512]{1,0:T(8,128)(2,1)}, bf16[1536,512]{1,0:T(8,128)(2,1)S(1)}, u32[]{:S(2)}, u32[]{:S(2)}) collective-permute-start(bf16[1536,512]{1,0:T(8,128)(2,1)} %add_convert_fusion.3), channel_id=1, source_target_pairs={{0,0},{1,4},{2,2},{3,6},{4,1},{5,5},{6,3},{7,7},{8,8},{9,12},{10,1... | collective-permute-start | bytes 4718600 | tf_op jit(solution)/shard_map/ppermute | solution.py:831
  686.2 36.2 %collective-permute-start.36 = (bf16[1536,512]{1,0:T(8,128)(2,1)S(1)}, bf16[1536,512]{1,0:T(8,128)(2,1)}, u32[]{:S(2)}, u32[]{:S(2)}) collective-permute-start(bf16[1536,512]{1,0:T(8,128)(2,1)S(1)} %add_convert_fusion.2), channel_id=1, source_target_pairs={{0,1},{1,5},{2,3},{3,7},{4,0},{5,4},{6,2},{7,6},{8,9},{9,13},{10,1... | collective-permute-start | bytes 4718600 | tf_op jit(solution)/shard_map/ppermute | solution.py:831
  742.5 126.3 %reduce-scatter.11.cloned.1.call-start = ((), (), s32[]{:S(2)}) async-start(), calls=%async_computation.11 | async-start | bytes 1310720 | tf_op jit(solution)/shard_map/reduce_scatter | solution.py:966
  742.6 37.1 %collective-permute-start.38 = (bf16[512,1536]{1,0:T(8,128)(2,1)}, bf16[512,1536]{1,0:T(8,128)(2,1)}, u32[]{:S(2)}, u32[]{:S(2)}) collective-permute-start(bf16[512,1536]{1,0:T(8,128)(2,1)} %reduce-scatter.7.cloned.1.call-done), channel_id=1, source_target_pairs={{0,4},{4,0},{1,5},{5,1},{2,6},{6,2},{3,7},{7,3},{8,12},{12,8},{9,1... | collective-permute-start | bytes 4718600 | tf_op jit(solution)/shard_map/ppermute | solution.py:969
  779.7 37.7 %collective-permute-start.39 = (bf16[1536,512]{1,0:T(8,128)(2,1)}, bf16[1536,512]{1,0:T(8,128)(2,1)}, u32[]{:S(2)}, u32[]{:S(2)}) collective-permute-start(bf16[1536,512]{1,0:T(8,128)(2,1)} %get-tuple-element.384), channel_id=1, source_target_pairs={{0,0},{1,4},{2,2},{3,6},{4,1},{5,5},{6,3},{7,7},{8,8},{9,12},{10,1... | collective-permute-start | bytes 4718600 | tf_op jit(solution)/shard_map/ppermute | solution.py:815
  792.9 33.8 %collective-permute-start.40 = (bf16[1536,512]{1,0:T(8,128)(2,1)}, bf16[1536,512]{1,0:T(8,128)(2,1)}, u32[]{:S(2)}, u32[]{:S(2)}) collective-permute-start(bf16[1536,512]{1,0:T(8,128)(2,1)} %get-tuple-element.385), channel_id=1, source_target_pairs={{0,1},{1,5},{2,3},{3,7},{4,0},{5,4},{6,2},{7,6},{8,9},{9,13},{10,1... | collective-permute-start | bytes 4718600 | tf_op jit(solution)/shard_map/ppermute | solution.py:815
  792.9 33.8 %collective-permute-start.41 = (bf16[1536,512]{1,0:T(8,128)(2,1)}, bf16[1536,512]{1,0:T(8,128)(2,1)}, u32[]{:S(2)}, u32[]{:S(2)}) collective-permute-start(bf16[1536,512]{1,0:T(8,128)(2,1)} %get-tuple-element.386), channel_id=1, source_target_pairs={{0,2},{1,6},{2,0},{3,4},{4,3},{5,7},{6,1},{7,5},{8,10},{9,14},{10,... | collective-permute-start | bytes 4718600 | tf_op jit(solution)/shard_map/ppermute | solution.py:815
  794.4 68.8 %collective-permute-start.42 = (bf16[1536,512]{1,0:T(8,128)(2,1)}, bf16[1536,512]{1,0:T(8,128)(2,1)}, u32[]{:S(2)}, u32[]{:S(2)}) collective-permute-start(bf16[1536,512]{1,0:T(8,128)(2,1)} %get-tuple-element.387), channel_id=1, source_target_pairs={{0,3},{1,7},{2,1},{3,5},{4,2},{5,6},{6,0},{7,4},{8,11},{9,15},{10,... | collective-permute-start | bytes 4718600 | tf_op jit(solution)/shard_map/ppermute | solution.py:815
  803.7 65.1 %collective-permute-start.43 = (bf16[512,768]{1,0:T(8,128)(2,1)}, bf16[512,768]{1,0:T(8,128)(2,1)S(1)}, u32[]{:S(2)}, u32[]{:S(2)}) collective-permute-start(bf16[512,768]{1,0:T(8,128)(2,1)} %reduce-scatter.9.cloned.1.call-done), channel_id=1, source_target_pairs={{0,4},{4,0},{1,5},{5,1},{2,6},{6,2},{3,7},{7,3},{8,12},{12,8},{9,1... | collective-permute-start | bytes 2359304 | tf_op jit(solution)/shard_map/ppermute | solution.py:969
  (36 other events, 428.2 us)
Sparse Core Ops, SparseCore 0:
  10.2 66.1 all-gather.4
  87.0 28.3 all-gather.6
  159.9 116.0 all-gather.8
  277.4 113.5 all-gather.10
  444.0 108.9 reduce-scatter.4
  578.8 120.2 reduce-scatter.6
  742.6 60.3 reduce-scatter.8
  805.9 27.1 reduce-scatter.10
